TPU v7x, 32 devices: a whole 2x2x4 slice. The times are simulated.
32 devices in a mesh: wide: 8 (over y, x, core), narrow: 4 (over z).
Axes of the slice: x: 2, y: 2, z: 4, core: 2. Of those that a mesh axis runs over, the one named last changes fastest.
Arguments:
- tokens: bfloat16 [10240, 2048], P(('wide', 'narrow')), may hold values from -6 to 6
- cotangent: bfloat16 [10240, 2048], P(('wide', 'narrow')), may hold values from -6 to 6
- lengths: int32 [32], P(('wide', 'narrow')), may hold values from 40 to 320, as said below
- positions: int32 [10240], P(('wide', 'narrow')), may hold values from 0 to 319, as said below
- norm_attn: bfloat16 [2048], P(('wide', 'narrow')), may hold values from 0.25 to 1.75
- w_query: bfloat16 [2048, 2048], P(('wide', 'narrow')), may hold values from -0.1875 to 0.1875
- w_key: bfloat16 [2048, 256], P(('wide', 'narrow')), may hold values from -0.1875 to 0.1875
- w_value: bfloat16 [2048, 256], P(('wide', 'narrow')), may hold values from -0.125 to 0.125
- w_output: bfloat16 [2048, 2048], P(('wide', 'narrow')), may hold values from -0.5 to 0.5
- norm_mlp: bfloat16 [2048], P(('wide', 'narrow')), may hold values from 0.25 to 1.75
- w_gate: bfloat16 [2048, 5632], P(('wide', 'narrow')), may hold values from -0.125 to 0.125
- w_up: bfloat16 [2048, 5632], P(('wide', 'narrow')), may hold values from -0.125 to 0.125
- w_down: bfloat16 [2048, 5632], P(('wide', 'narrow')), may hold values from -0.109375 to 0.109375
Outputs:
- output: bfloat16 [10240, 2048], P(('wide', 'narrow'))
- grad_tokens: float32 [10240, 2048], P(('wide', 'narrow'))
- grad_norm_attn: float32 [2048], P(('wide', 'narrow'))
- grad_w_query: float32 [2048, 2048], P(('wide', 'narrow'))
- grad_w_key: float32 [2048, 256], P(('wide', 'narrow'))
- grad_w_value: float32 [2048, 256], P(('wide', 'narrow'))
- grad_w_output: float32 [2048, 2048], P(('wide', 'narrow'))
- grad_norm_mlp: float32 [2048], P(('wide', 'narrow'))
- grad_w_gate: float32 [2048, 5632], P(('wide', 'narrow'))
- grad_w_up: float32 [2048, 5632], P(('wide', 'narrow'))
- grad_w_down: float32 [2048, 5632], P(('wide', 'narrow'))
Inputs may be any that keep to these rules, and one draw needn't show every extreme that they name: `lengths`: one sequence of every draw uses all 320 slots. Within a sequence positions rise by one from slot to slot and restart at 0 where a packed document starts; every sequence starts at position 0, and the first sequence holds a single document.
All inputs are finite; a program needn't handle non-finite values.
Results may differ from a plain program's by a relative error of at most 0.014.
The roundings to bfloat16 on the way count: a program that leaves them out, or rounds other values in their place, can miss the bound.
Values may be sent and summed in bfloat16 or wider, within the bound.
A program may use at most 384 MiB of HBM per device.

v0:
```python
import math

import jax
import jax.numpy as jnp
from jax import lax
from jax.sharding import PartitionSpec as P

QUERY_HEADS = 32
KEY_VALUE_HEADS = 4
HEAD_SIZE = 64


norm_eps = 1e-05
rope_base = 10000.0
masked_score = -1e30
contract_last = (((1,), (1,)), ((), ()))
contract_first = (((0,), (0,)), ((), ()))


def rope_tables(positions):
    half_dim = HEAD_SIZE // 2
    inv_freq = jnp.exp(
        -math.log(rope_base) * jnp.arange(half_dim, dtype=jnp.float32) * 2.0 / HEAD_SIZE
    )
    angles = positions.astype(jnp.float32)[..., None] * inv_freq
    cosine = jnp.cos(angles)
    sine_part = jnp.sin(angles)
    return (jnp.concatenate([cosine, cosine], -1), jnp.concatenate([sine_part, sine_part], -1))


def apply_rotary(values, cosine_table, sine_table):
    half_dim = values.shape[-1] // 2
    turned = jnp.concatenate([-values[..., half_dim:], values[..., :half_dim]], -1)
    return values * cosine_table[..., None, :] + turned * sine_table[..., None, :]


def invert_rotary(grad_rows, cosine_table, sine_table):
    half_dim = grad_rows.shape[-1] // 2
    with_cos = grad_rows * cosine_table[..., None, :]
    with_sin = grad_rows * sine_table[..., None, :]
    return with_cos + jnp.concatenate([with_sin[..., half_dim:], -with_sin[..., :half_dim]], -1)


def normalize(values):
    return values * lax.rsqrt(jnp.mean(values * values, axis=-1, keepdims=True) + norm_eps)


def norm_back(grad_hat, normed, values):
    row_scale = lax.rsqrt(jnp.mean(values * values, axis=-1, keepdims=True) + norm_eps)
    return row_scale * (grad_hat - normed * jnp.mean(grad_hat * normed, axis=-1, keepdims=True))


def attention_inputs(normed, norm_attn, w_query, w_key, w_value):
    gain_piece = lax.all_gather(norm_attn, ("wide", "narrow"), axis=0, tiled=True)
    query_rows = lax.all_gather(w_query, ("wide", "narrow"), axis=0, tiled=True)
    key_rows = lax.all_gather(w_key, ("wide", "narrow"), axis=0, tiled=True)
    value_rows = lax.all_gather(w_value, ("wide", "narrow"), axis=0, tiled=True)
    gain_float = gain_piece.astype(jnp.float32)
    columns = (normed * gain_float).astype(jnp.bfloat16)
    query_sum = jnp.dot(columns, query_rows, preferred_element_type=jnp.float32)
    key_sum = jnp.dot(columns, key_rows, preferred_element_type=jnp.float32)
    value_sum = jnp.dot(columns, value_rows, preferred_element_type=jnp.float32)
    return (gain_float, columns, query_sum, key_sum, value_sum)


def mlp_inputs(normed, norm_mlp, w_gate, w_up):
    gain_piece = lax.all_gather(norm_mlp, ("wide", "narrow"), axis=0, tiled=True)
    gate_rows = lax.all_gather(w_gate, ("wide", "narrow"), axis=0, tiled=True)
    up_rows = lax.all_gather(w_up, ("wide", "narrow"), axis=0, tiled=True)
    gain_float = gain_piece.astype(jnp.float32)
    columns = (normed * gain_float).astype(jnp.bfloat16)
    gate_sum = jnp.dot(columns, gate_rows, preferred_element_type=jnp.float32)
    up_sum = jnp.dot(columns, up_rows, preferred_element_type=jnp.float32)
    return (gain_float, columns, gate_sum, up_sum)


def head_slices(query_rotated, key_rotated, value_reduced, shared_key_head):
    row_total_count = query_rotated.shape[0]
    heads_per_group = QUERY_HEADS // KEY_VALUE_HEADS
    query_head = query_rotated[
        :,
        shared_key_head
        * heads_per_group
        * HEAD_SIZE : (shared_key_head + 1)
        * heads_per_group
        * HEAD_SIZE,
    ].reshape(row_total_count, heads_per_group, HEAD_SIZE)
    key_head = key_rotated[:, shared_key_head * HEAD_SIZE : (shared_key_head + 1) * HEAD_SIZE]
    value_head = value_reduced[:, shared_key_head * HEAD_SIZE : (shared_key_head + 1) * HEAD_SIZE]
    return (query_head, key_head, value_head)


def head_scores(query_head, key_head):
    row_total_count = query_head.shape[0]
    causal = jnp.arange(row_total_count)[:, None] >= jnp.arange(row_total_count)[None, :]
    raw_scores = jnp.einsum("qrd,kd->rqk", query_head, key_head, preferred_element_type=jnp.float32)
    return jnp.where(causal, raw_scores * HEAD_SIZE ** (-0.5), masked_score)


def attend(query_rotated, key_rotated, value_reduced):
    row_total_count = query_rotated.shape[0]
    heads_per_group = QUERY_HEADS // KEY_VALUE_HEADS
    contexts = []
    log_totals = []
    for shared_key_head in range(KEY_VALUE_HEADS):
        query_head, key_head, value_head = head_slices(
            query_rotated, key_rotated, value_reduced, shared_key_head
        )
        scores = head_scores(query_head, key_head)
        row_peak = jnp.max(scores, axis=-1, keepdims=True)
        exp_scores = jnp.exp(scores - row_peak)
        row_total = jnp.sum(exp_scores, axis=-1, keepdims=True)
        probs = exp_scores / row_total
        context_head = jnp.einsum(
            "rqk,kd->qrd",
            probs.astype(jnp.bfloat16),
            value_head,
            preferred_element_type=jnp.float32,
        )
        contexts.append(context_head.reshape(row_total_count, heads_per_group * HEAD_SIZE))
        log_totals.append(row_peak + jnp.log(row_total))
    return (jnp.concatenate(contexts, 1).astype(jnp.bfloat16), log_totals)


def attend_back(query_rotated, key_rotated, value_reduced, log_totals, grad_context):
    row_total_count = query_rotated.shape[0]
    heads_per_group = QUERY_HEADS // KEY_VALUE_HEADS
    score_scale = HEAD_SIZE ** (-0.5)
    query_grads = []
    key_grads = []
    value_grads = []
    for shared_key_head in range(KEY_VALUE_HEADS):
        query_head, key_head, value_head = head_slices(
            query_rotated, key_rotated, value_reduced, shared_key_head
        )
        scores = head_scores(query_head, key_head)
        probs = jnp.exp(scores - log_totals[shared_key_head])
        probs_low = probs.astype(jnp.bfloat16)
        grad_head = grad_context[
            :,
            shared_key_head
            * heads_per_group
            * HEAD_SIZE : (shared_key_head + 1)
            * heads_per_group
            * HEAD_SIZE,
        ].reshape(row_total_count, heads_per_group, HEAD_SIZE)
        grad_probs = jnp.einsum(
            "qrd,kd->rqk", grad_head, value_head, preferred_element_type=jnp.float32
        )
        value_grads.append(
            jnp.einsum("rqk,qrd->kd", probs_low, grad_head, preferred_element_type=jnp.float32)
        )
        inner_sum = jnp.sum(grad_probs * probs, axis=-1, keepdims=True)
        grad_scores = (probs * (grad_probs - inner_sum) * score_scale).astype(jnp.bfloat16)
        query_grad = jnp.einsum(
            "rqk,kd->qrd", grad_scores, key_head, preferred_element_type=jnp.float32
        )
        query_grads.append(query_grad.reshape(row_total_count, heads_per_group * HEAD_SIZE))
        key_grads.append(
            jnp.einsum("rqk,qrd->kd", grad_scores, query_head, preferred_element_type=jnp.float32)
        )
    return (
        jnp.concatenate(query_grads, 1),
        jnp.concatenate(key_grads, 1),
        jnp.concatenate(value_grads, 1),
    )


def make_term(width_sides, other_sides):
    down_side, mlp_side, attn_side, qkv_side = width_sides
    mixed_rows, gate_rows, up_rows, context_rows, query_rows, key_rows, value_rows = other_sides

    def grad_term(first_row, row_span):
        pieces = [
            lax.dot_general(
                down_side, mixed_rows, contract_first, preferred_element_type=jnp.float32
            ),
            lax.dot_general(
                mlp_side, gate_rows, contract_first, preferred_element_type=jnp.float32
            ),
            lax.dot_general(mlp_side, up_rows, contract_first, preferred_element_type=jnp.float32),
            lax.dot_general(
                attn_side, context_rows, contract_first, preferred_element_type=jnp.float32
            ),
            lax.dot_general(
                qkv_side, query_rows, contract_first, preferred_element_type=jnp.float32
            ),
            lax.dot_general(qkv_side, key_rows, contract_first, preferred_element_type=jnp.float32),
            lax.dot_general(
                qkv_side, value_rows, contract_first, preferred_element_type=jnp.float32
            ),
        ]
        return jnp.concatenate(pieces, 1)

    return grad_term


def per_device(
    tokens,
    cotangent,
    lengths,
    positions,
    norm_attn,
    w_query,
    w_key,
    w_value,
    w_output,
    norm_mlp,
    w_gate,
    w_up,
    w_down,
):
    row_total_count = tokens.shape[0]
    shard_rows = w_query.shape[0]
    query_width = w_query.shape[1]
    key_width = w_key.shape[1]
    hidden_width = w_gate.shape[1]
    inputs = tokens.astype(jnp.float32)
    valid_rows = (jnp.arange(row_total_count) < lengths[0]).astype(jnp.float32)[:, None]
    cosine_table, sine_table = rope_tables(positions)
    normed_attn = normalize(inputs)
    gain_attn_full, scaled_attn, query_pre, key_unrotated, value_pre = attention_inputs(
        normed_attn, norm_attn, w_query, w_key, w_value
    )
    query_rotated = (
        apply_rotary(
            query_pre.reshape(row_total_count, QUERY_HEADS, HEAD_SIZE), cosine_table, sine_table
        )
        .reshape(row_total_count, query_width)
        .astype(jnp.bfloat16)
    )
    key_rotated = (
        apply_rotary(
            key_unrotated.reshape(row_total_count, KEY_VALUE_HEADS, HEAD_SIZE),
            cosine_table,
            sine_table,
        )
        .reshape(row_total_count, key_width)
        .astype(jnp.bfloat16)
    )
    value_reduced = value_pre.astype(jnp.bfloat16)
    context, log_totals = attend(query_rotated, key_rotated, value_reduced)
    attn_out = lax.dot_general(
        context,
        lax.all_gather(w_output, ("wide", "narrow"), axis=0, tiled=True),
        contract_last,
        preferred_element_type=jnp.float32,
    )
    hidden = inputs + attn_out
    normed_mlp = normalize(hidden)
    gain_mlp_full, scaled_mlp, gate_proj, up_proj = mlp_inputs(normed_mlp, norm_mlp, w_gate, w_up)
    mixed_low = (gate_proj * jax.nn.sigmoid(gate_proj) * up_proj).astype(jnp.bfloat16)
    mlp_out = lax.dot_general(
        mixed_low,
        lax.all_gather(w_down, ("wide", "narrow"), axis=0, tiled=True),
        contract_last,
        preferred_element_type=jnp.float32,
    )
    output = (valid_rows * (hidden + mlp_out)).astype(jnp.bfloat16)
    grad_y = cotangent.astype(jnp.float32) * valid_rows
    grad_y_low = grad_y.astype(jnp.bfloat16)
    grad_cols = grad_y_low
    grad_mixed = jnp.dot(
        grad_cols,
        lax.all_gather(w_down, ("wide", "narrow"), axis=0, tiled=True),
        preferred_element_type=jnp.float32,
    )
    again_values = mlp_inputs(normed_mlp, norm_mlp, w_gate, w_up)
    gate_proj = again_values[2]
    up_proj = again_values[3]
    sigmoid_gate = jax.nn.sigmoid(gate_proj)
    grad_gate = (
        grad_mixed * up_proj * (sigmoid_gate * (1.0 + gate_proj * (1.0 - sigmoid_gate)))
    ).astype(jnp.bfloat16)
    grad_up = (grad_mixed * (gate_proj * sigmoid_gate)).astype(jnp.bfloat16)
    gate_rows = lax.all_gather(w_gate, ("wide", "narrow"), axis=0, tiled=True)
    up_rows = lax.all_gather(w_up, ("wide", "narrow"), axis=0, tiled=True)
    columns = lax.dot_general(
        grad_gate, gate_rows, contract_last, preferred_element_type=jnp.float32
    )
    columns = columns + lax.dot_general(
        grad_up, up_rows, contract_last, preferred_element_type=jnp.float32
    )
    grad_xn2 = columns
    grad_gain_mlp = jnp.sum(grad_xn2 * normed_mlp, axis=0)
    grad_hidden = grad_y + norm_back(grad_xn2 * gain_mlp_full, normed_mlp, hidden)
    grad_attn_low = grad_hidden.astype(jnp.bfloat16)
    grad_cols = grad_attn_low
    grad_context = jnp.dot(
        grad_cols,
        lax.all_gather(w_output, ("wide", "narrow"), axis=0, tiled=True),
        preferred_element_type=jnp.float32,
    )
    grad_context = grad_context.astype(jnp.bfloat16)
    grad_query_rot, gradient_key_rotated, grad_value_sum = attend_back(
        query_rotated, key_rotated, value_reduced, log_totals, grad_context
    )
    grad_query = (
        invert_rotary(
            grad_query_rot.reshape(row_total_count, QUERY_HEADS, HEAD_SIZE),
            cosine_table,
            sine_table,
        )
        .reshape(row_total_count, query_width)
        .astype(jnp.bfloat16)
    )
    grad_key = (
        invert_rotary(
            gradient_key_rotated.reshape(row_total_count, KEY_VALUE_HEADS, HEAD_SIZE),
            cosine_table,
            sine_table,
        )
        .reshape(row_total_count, key_width)
        .astype(jnp.bfloat16)
    )
    grad_value = grad_value_sum.astype(jnp.bfloat16)
    query_rows = lax.all_gather(w_query, ("wide", "narrow"), axis=0, tiled=True)
    key_rows = lax.all_gather(w_key, ("wide", "narrow"), axis=0, tiled=True)
    value_rows = lax.all_gather(w_value, ("wide", "narrow"), axis=0, tiled=True)
    columns = lax.dot_general(
        grad_query, query_rows, contract_last, preferred_element_type=jnp.float32
    )
    columns = columns + lax.dot_general(
        grad_key, key_rows, contract_last, preferred_element_type=jnp.float32
    )
    columns = columns + lax.dot_general(
        grad_value, value_rows, contract_last, preferred_element_type=jnp.float32
    )
    local_term = make_term(
        (grad_y_low, scaled_mlp, grad_attn_low, scaled_attn),
        (mixed_low, grad_gate, grad_up, context, grad_query, grad_key, grad_value),
    )
    all_sums = lax.psum_scatter(
        local_term(jnp.int32(0), lax.axis_size(("wide", "narrow")) * shard_rows),
        ("wide", "narrow"),
        scatter_dimension=0,
        tiled=True,
    )
    edges = [0]
    for width in (
        hidden_width,
        hidden_width,
        hidden_width,
        query_width,
        query_width,
        key_width,
        key_width,
    ):
        edges.append(edges[-1] + width)
    grad_w_down = all_sums[:, edges[0] : edges[1]]
    grad_w_gate = all_sums[:, edges[1] : edges[2]]
    grad_w_up = all_sums[:, edges[2] : edges[3]]
    grad_w_output = all_sums[:, edges[3] : edges[4]]
    grad_w_query = all_sums[:, edges[4] : edges[5]]
    grad_w_key = all_sums[:, edges[5] : edges[6]]
    grad_w_value = all_sums[:, edges[6] : edges[7]]
    grad_gain_attn = jnp.sum(columns * normed_attn, axis=0)
    grad_tokens = grad_hidden + norm_back(columns * gain_attn_full, normed_attn, inputs)
    grad_norm_attn, grad_norm_mlp = (
        lax.psum_scatter(grad_gain_attn, ("wide", "narrow"), scatter_dimension=0, tiled=True),
        lax.psum_scatter(grad_gain_mlp, ("wide", "narrow"), scatter_dimension=0, tiled=True),
    )
    return (
        output,
        grad_tokens,
        grad_norm_attn,
        grad_w_query,
        grad_w_key,
        grad_w_value,
        grad_w_output,
        grad_norm_mlp,
        grad_w_gate,
        grad_w_up,
        grad_w_down,
    )


def solution(mesh):
    in_specs = (
        P(("wide", "narrow"), None),
        P(("wide", "narrow"), None),
        P(("wide", "narrow")),
        P(("wide", "narrow")),
        P(("wide", "narrow")),
        P(("wide", "narrow"), None),
        P(("wide", "narrow"), None),
        P(("wide", "narrow"), None),
        P(("wide", "narrow"), None),
        P(("wide", "narrow")),
        P(("wide", "narrow"), None),
        P(("wide", "narrow"), None),
        P(("wide", "narrow"), None),
    )
    out_specs = (
        P(("wide", "narrow"), None),
        P(("wide", "narrow"), None),
        P(("wide", "narrow")),
        P(("wide", "narrow"), None),
        P(("wide", "narrow"), None),
        P(("wide", "narrow"), None),
        P(("wide", "narrow"), None),
        P(("wide", "narrow")),
        P(("wide", "narrow"), None),
        P(("wide", "narrow"), None),
        P(("wide", "narrow"), None),
    )
    return jax.shard_map(
        per_device, mesh=mesh, in_specs=in_specs, out_specs=out_specs, check_vma=False
    )
```

profile of v0, /device:TPU:0, one launch (start us, length us, event | category | flops | bytes accessed | tf_op | source)
XLA Modules:
  0.0 2423.2 jit_solution(7380186025434072481)
XLA Ops:
  15.0 42.1 %all-reduce.5 = (bf16[2048]{0:T(1024)(128)(2,1)S(1)}, bf16[2048]{0:T(1024)(128)(2,1)S(1)}) all-reduce(bf16[2048]{0:T(1024)(128)(2,1)S(1)} %dynamic-update-slice, bf16[2048]{0:T(1024)(128)(2,1)S(1)} %dynamic-update-slice.1), channel_id=1, replica_groups=mesh['wide'=8,'narrow'=4] {'wide','narrow'}, use_global_device_ids=true, to_apply=%add | all-reduce | flops 4096 | bytes 16384
  59.6 3.4 copy.141
  63.4 4.1 all-gather.10.cloned.1.call-done
  69.8 53.6 %all-gather.8.cloned.1.call-done = bf16[2048,256]{1,0:T(8,128)(2,1)} async-done(((bf16[64,256]{1,0:T(8,128)(2,1)}), bf16[2048,256]{1,0:T(8,128)(2,1)}) %all-gather.8.cloned.1.call-update) | async-done | bytes 1048592 | tf_op jit(solution)/shard_map/all_gather | solution.py:57
  123.4 2.5 convolution_convert_fusion.1
  125.8 76.9 %all-gather.12.cloned.1.call-done = bf16[2048,2048]{1,0:T(8,128)(2,1)} async-done(((bf16[64,2048]{1,0:T(8,128)(2,1)}), bf16[2048,2048]{1,0:T(8,128)(2,1)}) %all-gather.12.cloned.1.call-update) | async-done | bytes 8388624 | tf_op jit(solution)/shard_map/all_gather | solution.py:55
  202.7 7.8 fusion.144
  210.5 3.5 copy.142
  218.1 3.6 copy.143
  221.6 3.9 add_convert_fusion
  238.2 43.3 %all-gather.14.cloned.1.call-done = bf16[2048,2048]{1,0:T(8,128)(2,1)} async-done(((bf16[64,2048]{1,0:T(8,128)(2,1)}), bf16[2048,2048]{1,0:T(8,128)(2,1)}) %all-gather.14.cloned.1.call-update) | async-done | bytes 8388624 | tf_op jit(solution)/shard_map/all_gather | solution.py:245
  281.5 7.5 multiply_reduce_fusion.2
  291.4 136.0 %all-gather.18.cloned.1.call-done = bf16[2048,5632]{1,0:T(8,128)(2,1)} async-done(((bf16[64,5632]{1,0:T(8,128)(2,1)}), bf16[2048,5632]{1,0:T(8,128)(2,1)}) %all-gather.18.cloned.1.call-update) | async-done | bytes 23068688 | tf_op jit(solution)/shard_map/all_gather | solution.py:69
  427.4 14.9 fusion.161
  442.3 130.6 %all-gather.16.cloned.1.call-done = bf16[2048,5632]{1,0:T(8,128)(2,1)} async-done(((bf16[64,5632]{1,0:T(8,128)(2,1)}), bf16[2048,5632]{1,0:T(8,128)(2,1)}) %all-gather.16.cloned.1.call-update) | async-done | bytes 23068688 | tf_op jit(solution)/shard_map/all_gather | solution.py:68
  572.9 14.9 fusion.160
  587.8 130.7 %all-gather.20.cloned.1.call-done = bf16[2048,5632]{1,0:T(8,128)(2,1)} async-done(((bf16[64,5632]{1,0:T(8,128)(2,1)}), bf16[2048,5632]{1,0:T(8,128)(2,1)}) %all-gather.20.cloned.1.call-update) | async-done | bytes 23068688 | tf_op jit(solution)/shard_map/all_gather | solution.py:255
  718.6 20.5 multiply_convert_fusion
  739.0 14.3 fusion.162
  753.4 15.6 multiply_reduce_fusion
  769.0 3.7 multiply_add_fusion
  772.8 6.2 convolution_convert_fusion
  781.3 3.6 fusion.117
  785.7 7.3 fusion.83
  793.0 8.2 fusion.75
  801.5 3.5 fusion.118
  807.1 8.2 fusion.84
  815.3 8.7 fusion.76
  824.3 3.6 fusion.119
  830.0 8.0 fusion.85
  838.0 8.3 fusion.77
  846.6 3.6 fusion.116
  852.3 8.0 fusion.82
  860.3 8.2 fusion.74
  870.4 2.5 pad_maximum_fusion
  874.9 23.4 convolution_dynamic-update-slice_fusion.2
  898.3 23.2 convolution_dynamic-update-slice_fusion.1
  921.4 20.5 convolution_dynamic-update-slice_fusion
  942.0 9.8 convolution_dynamic-update-slice_fusion.4
  955.1 8.6 convolution_dynamic-update-slice_fusion.3
  963.7 2.3 convolution_dynamic-update-slice_fusion.6
  968.3 7.0 fusion.163
  977.4 2.7 fusion.37
  980.2 38.6 %all-reduce.4 = (f32[2048]{0:T(1024)S(1)}, f32[2048]{0:T(1024)S(1)}) all-reduce(f32[2048]{0:T(1024)S(1)} %get-tuple-element.13, f32[2048]{0:T(1024)S(1)} %copy-done.66), channel_id=2, replica_groups=mesh['wide'=8,'narrow'=4] {'wide','narrow'}, use_global_device_ids=true, to_apply=%region_17.18.clone | all-reduce | flops 4096 | bytes 32768
  1020.0 5.0 fusion.36
  1025.0 19.3 fusion.31
  1044.3 1363.6 %reduce-scatter.2.cloned.1.call-done = f32[64,21504]{1,0:T(8,128)} async-done(((f32[2048,21504]{1,0:T(8,128)}), f32[64,21504]{1,0:T(8,128)}) %reduce-scatter.2.cloned.1.call-update) | async-done | bytes 5505040 | tf_op jit(solution)/shard_map/reduce_scatter | solution.py:333
  2411.7 4.4 fusion.149
  (224 shorter events, 57.3 us)
Async XLA Ops:
  7.2 60.4 %all-gather.10.cloned.1.call-start = ((), (), s32[]{:S(2)}) async-start(), calls=%async_computation.2 | async-start | bytes 1081344 | tf_op jit(solution)/shard_map/all_gather | solution.py:56
  7.9 115.4 %all-gather.8.cloned.1.call-start = ((), (), s32[]{:S(2)}) async-start(), calls=%async_computation.1 | async-start | bytes 1081344 | tf_op jit(solution)/shard_map/all_gather | solution.py:57
  8.7 194.0 %all-gather.12.cloned.1.call-start = ((), (), s32[]{:S(2)}) async-start(), calls=%async_computation.3 | async-start | bytes 8650752 | tf_op jit(solution)/shard_map/all_gather | solution.py:55
  9.4 272.1 %all-gather.14.cloned.1.call-start = ((), (), s32[]{:S(2)}) async-start(), calls=%async_computation.4 | async-start | bytes 8650752 | tf_op jit(solution)/shard_map/all_gather | solution.py:245
  10.0 417.4 %all-gather.18.cloned.1.call-start = ((), (), s32[]{:S(2)}) async-start(), calls=%async_computation.6 | async-start | bytes 23789568 | tf_op jit(solution)/shard_map/all_gather | solution.py:69
  10.6 562.3 %all-gather.16.cloned.1.call-start = ((), (), s32[]{:S(2)}) async-start(), calls=%async_computation.5 | async-start | bytes 23789568 | tf_op jit(solution)/shard_map/all_gather | solution.py:68
  11.1 707.4 %all-gather.20.cloned.1.call-start = ((), (), s32[]{:S(2)}) async-start(), calls=%async_computation.7 | async-start | bytes 23789568 | tf_op jit(solution)/shard_map/all_gather | solution.py:255
  11.9 2396.0 %reduce-scatter.2.cloned.1.call-start = ((), (), s32[]{:S(2)}) async-start(), calls=%async_computation.8 | async-start | bytes 181665792 | tf_op jit(solution)/shard_map/reduce_scatter | solution.py:333
  57.1 145.6 %copy-start.55 = (f32[2048]{0:T(1024)}, f32[2048]{0:T(1024)S(1)}, u32[]{:S(2)}) copy-start(f32[2048]{0:T(1024)S(1)} %convert_element_type.106) | copy-start | bytes 24580
  62.9 706.1 %copy-start.57 = (f32[320]{0:T(512)}, f32[320]{0:T(512)S(1)}, u32[]{:S(2)}) copy-start(f32[320]{0:T(512)S(1)} %fusion.120) | copy-start | bytes 3844
  63.0 153.2 %copy-start.22 = (f32[320,64]{0,1:T(8,128)}, f32[320,64]{0,1:T(8,128)S(1)}, u32[]{:S(2)}) copy-start(f32[320,64]{0,1:T(8,128)S(1)} %pad_maximum_fusion.9) | copy-start | bytes 245764
  63.4 139.3 %copy-start.59 = (f32[320]{0:T(512)}, f32[320]{0:T(512)S(1)}, u32[]{:S(2)}) copy-start(f32[320]{0:T(512)S(1)} %add_rsqrt_fusion.1) | copy-start | bytes 3844
  69.8 162.9 %copy-start.30 = (bf16[320,256]{1,0:T(8,128)(2,1)}, bf16[320,256]{1,0:T(8,128)(2,1)S(1)}, u32[]{:S(2)}) copy-start(bf16[320,256]{1,0:T(8,128)(2,1)S(1)} %add_convert_fusion.1) | copy-start | bytes 491524
  226.6 6.1 copy-start.24
  235.0 46.5 %copy-start.48 = (bf16[64,8,320]{2,0,1:T(8,128)(2,1)}, bf16[64,8,320]{2,0,1:T(8,128)(2,1)S(1)}, u32[]{:S(2)}) copy-start(bf16[64,8,320]{2,0,1:T(8,128)(2,1)S(1)} %fusion.80) | copy-start | bytes 983044
  235.8 45.7 %copy-start.50 = (bf16[64,8,320]{2,0,1:T(8,128)(2,1)}, bf16[64,8,320]{2,0,1:T(8,128)(2,1)S(1)}, u32[]{:S(2)}) copy-start(bf16[64,8,320]{2,0,1:T(8,128)(2,1)S(1)} %fusion.79) | copy-start | bytes 983044
  236.7 44.8 %copy-start.51 = (bf16[64,8,320]{2,0,1:T(8,128)(2,1)}, bf16[64,8,320]{2,0,1:T(8,128)(2,1)S(1)}, u32[]{:S(2)}) copy-start(bf16[64,8,320]{2,0,1:T(8,128)(2,1)S(1)} %fusion.78) | copy-start | bytes 983044
  289.1 495.8 %copy-start.64 = (f32[8,320]{1,0:T(8,128)}, f32[8,320]{1,0:T(8,128)S(1)}, u32[]{:S(2)}) copy-start(f32[8,320]{1,0:T(8,128)S(1)} %log_add_fusion.2) | copy-start | bytes 30724
  291.4 281.5 %copy-start.11 = (bf16[320,2048]{1,0:T(8,128)(2,1)}, bf16[320,2048]{1,0:T(8,128)(2,1)S(1)}, u32[]{:S(2)}) copy-start(bf16[320,2048]{1,0:T(8,128)(2,1)S(1)} %multiply_convert_fusion.3) | copy-start | bytes 3932164
  442.3 276.2 %copy-start.16 = (bf16[320,2048]{1,0:T(8,128)(2,1)S(1)}, bf16[320,2048]{1,0:T(8,128)(2,1)}, u32[]{:S(2)}) copy-start(bf16[320,2048]{1,0:T(8,128)(2,1)} %param.14) | copy-start | bytes 3932164
  739.0 14.3 copy-start.15
  785.7 7.3 copy-start.31
  785.7 7.3 copy-start.65
  793.0 8.2 copy-start.37
  801.5 5.7 copy-start.29
  807.1 8.2 copy-start.32
  807.1 8.2 copy-start.63
  815.3 8.7 copy-start.36
  824.2 5.7 copy-start.27
  830.0 8.0 copy-start.33
  830.0 8.1 copy-start.62
  838.0 8.4 copy-start.35
  852.3 8.0 copy-start.34
  852.3 8.0 copy-start.61
  860.2 8.3 copy-start.45
  860.2 8.3 copy-start.46
  860.2 8.3 copy-start.47
  860.2 8.4 copy-start.23
  860.3 8.5 copy-start.21
  898.3 23.2 copy-start.12
  921.4 20.5 copy-start.49
  942.0 9.8 copy-start.18
  942.0 9.8 copy-start.19
  955.0 8.6 copy-start.17
  955.0 10.9 copy-start.52
  955.0 10.9 copy-start.53
  955.0 10.9 copy-start.54
  968.3 7.0 copy-start.38
  (27 other events, 77.9 us)
Sparse Core Ops, SparseCore 0:
  11.0 56.4 all-gather.9
  70.5 52.8 all-gather.7
  126.3 76.3 all-gather.11
  205.5 75.9 all-gather.13
  284.2 143.1 all-gather.17
  430.1 142.7 all-gather.15
  575.7 142.7 all-gather.19
  968.4 1439.4 reduce-scatter.1
where the time goes:
time: 2430 us; the launch traced here: 2420 us
  waiting for transfers between devices  1940 us (80%)
  matrix products  319 us (13%)
  blocking collectives  80.7 us (3%)
  local copies, waits for them, and re-layouts  35.2 us (1%)
  other arithmetic  28.4 us (1%)
    reduce_scatter x1, waiting for transfers between devices, per_device(): lax.psum_scatter(local_term(jnp.int32(0), lax.axis_size(('wide', 'narrow'...  1360 us
    all_gather x1, waiting for transfers between devices, mlp_inputs(): up_rows = lax.all_gather(w_up, ('wide', 'narrow'), axis=0, tiled=True)  136 us
    all_gather x1, waiting for transfers between devices, per_device(): lax.all_gather(w_down, ('wide', 'narrow'), axis=0, tiled=True)  131 us
    all_gather x1, waiting for transfers between devices, mlp_inputs(): gate_rows = lax.all_gather(w_gate, ('wide', 'narrow'), axis=0, tiled=True)  131 us
    unnamed x2, blocking collectives  80.7 us
    all_gather x1, waiting for transfers between devices, attention_inputs(): query_rows = lax.all_gather(w_query, ('wide', 'narrow'), axis=0, tiled=True)  76.9 us
    all_gather x1, waiting for transfers between devices, attention_inputs(): value_rows = lax.all_gather(w_value, ('wide', 'narrow'), axis=0, tiled=True)  53.6 us
  transfers between devices with their start and end apart: 8, of which 8 were waited for; matrix products, arithmetic and copies ran while one was open for 5% of the time, Pallas kernels for 0%

commit v1 on v0

--- a/solution.py
+++ b/solution.py
@@ -1,8 +1,11 @@
+import functools
 import math
 
 import jax
 import jax.numpy as jnp
 from jax import lax
+from jax.experimental import pallas as pl
+from jax.experimental.pallas import tpu as pltpu
 from jax.sharding import PartitionSpec as P
 
 QUERY_HEADS = 32
@@ -375,6 +378,337 @@
     )
 
 
+MESH = pl.DeviceIdType.MESH
+ANY = pl.BlockSpec(memory_space=pl.ANY)
+
+CHIPS, CORES = 4, 2
+
+def place():
+    w = lax.axis_index("wide"); n = lax.axis_index("narrow")
+    return w // CORES, w % CORES, n
+
+def remote(src, dst, send, recv, chip, core, z):
+    return pltpu.make_async_remote_copy(src_ref=src, dst_ref=dst, send_sem=send, recv_sem=recv,
+        device_id={"wide": chip * CORES + core, "narrow": z}, device_id_type=MESH)
+
+def hello(partners):
+    barrier = pltpu.get_barrier_semaphore()
+    count = 0
+    for cond, chip, core, z in partners:
+        def sig(chip=chip, core=core, z=z):
+            pl.semaphore_signal(barrier, inc=1, device_id={"wide": chip * CORES + core, "narrow": z}, device_id_type=MESH)
+        if cond is None:
+            sig(); count = count + 1
+        else:
+            pl.when(cond)(sig); count = count + jnp.where(cond, 1, 0)
+    pl.semaphore_wait(barrier, count)
+
+def gather_kernel(nz, wq, wk, wv, wo, gains, wg, wu, wd, gy, QKV, WO, GAIN, G0, G1, G2, GY,
+                  loc, a2a_s, a2a_r, gy_s, gy_r, z_s, z_r, d_s, d_r, p_s, p_r, e_s, e_r):
+    c, k, n = place()
+    G = (G0, G1, G2); W = (wg, wu, wd)
+    cols = G0.shape[-1]
+    rows = wq.shape[0]
+    other = 1 - k
+    left, right = n > 0, n < nz - 1
+    others = [(c + i) % CHIPS for i in range(1, CHIPS)]
+    hello([(None, cc, k, n) for cc in others] + [(None, c, other, n), (left, c, k, n - 1), (right, c, k, n + 1)])
+    kn = k * nz + n
+    b = (c * CORES + k) * nz + n
+    started = []
+    def start(cond, desc):
+        if cond is None: desc.start()
+        else: pl.when(cond)(lambda: desc.start())
+        started.append((cond, desc))
+    def recv(cond, desc):
+        if cond is None: desc.wait_recv()
+        else: pl.when(cond)(lambda: desc.wait_recv())
+    def blk(z): return pl.ds(pl.multiple_of(((c * CORES + k) * nz + z) * rows, rows), rows)
+    mine = blk(n)
+    q, kv = wq.shape[1], wk.shape[1]
+    for i, cc in enumerate(others):
+        for m in range(3):
+            start(None, remote(W[m].at[:, pl.ds(pl.multiple_of(cc * cols, 128), cols)], G[m].at[c, kn], a2a_s.at[m, i], a2a_r.at[m, i], cc, k, n))
+    own = [pltpu.make_async_copy(wq, QKV.at[mine, pl.ds(0, q)], loc.at[0]),
+           pltpu.make_async_copy(wk, QKV.at[mine, pl.ds(q, kv)], loc.at[1]),
+           pltpu.make_async_copy(wv, QKV.at[mine, pl.ds(q + kv, kv)], loc.at[2]),
+           pltpu.make_async_copy(wo, WO.at[mine], loc.at[3]),
+           pltpu.make_async_copy(gains, GAIN.at[mine], loc.at[4])]
+    ownff = [pltpu.make_async_copy(W[m].at[:, pl.ds(pl.multiple_of(c * cols, 128), cols)], G[m].at[c, kn], loc.at[5 + m]) for m in range(3)]
+    owngy = pltpu.make_async_copy(gy, GY.at[c], loc.at[8])
+    for cp in own + ownff + [owngy]: cp.start()
+    for cp in own: cp.wait()
+    A = (QKV, WO, GAIN)
+    def zsend(item, ref, dirn, s):
+        cond = (right & (n - s >= 0)) if dirn == 0 else (left & (n + s <= nz - 1))
+        z = n + 1 if dirn == 0 else n - 1
+        return cond, remote(ref, ref, z_s.at[item, dirn, s], z_r.at[item, dirn, s], c, k, z)
+    def zrecv(item, ref, dirn, s):
+        cond = (n - s >= 0) if dirn == 0 else (n + s <= nz - 1)
+        return cond, remote(ref, ref, z_s.at[item, dirn, s - 1], z_r.at[item, dirn, s - 1], c, k, n)
+    def origin(dirn, s):
+        o = n - s if dirn == 0 else n + s
+        return jnp.clip(o, 0, nz - 1)
+    for a in range(3):
+        for dirn in range(2):
+            start(*zsend(a, A[a].at[mine], dirn, 0))
+    for i, cc in enumerate(others):
+        start(None, remote(gy, GY.at[c], gy_s.at[i], gy_r.at[i], cc, k, n))
+    for s in range(1, nz):
+        for dirn in range(2):
+            for a in range(3):
+                ref = A[a].at[blk(origin(dirn, s))]
+                recv(*zrecv(a, ref, dirn, s))
+                if s < nz - 1: start(*zsend(a, ref, dirn, s))
+    def part(cc, kk): return pl.ds(pl.multiple_of((cc * CORES + kk) * nz * rows, rows), nz * rows)
+    for a in range(3):
+        for i, cc in enumerate(others):
+            start(None, remote(A[a].at[part(c, k)], A[a].at[part(c, k)], p_s.at[a, i], p_r.at[a, i], cc, k, n))
+        start(None, remote(A[a].at[part(c, k)], A[a].at[part(c, k)], d_s.at[a, 0], d_r.at[a, 0], c, other, n))
+    for m in range(3):
+        ownff[m].wait()
+        for i in range(CHIPS - 1):
+            remote(G[m].at[c, kn], G[m].at[c, kn], a2a_s.at[m, i], a2a_r.at[m, i], c, k, n).wait_recv()
+        ref = G[m].at[:, kn]
+        for dirn in range(2): start(*zsend(3 + m, ref, dirn, 0))
+        start(None, remote(ref, ref, e_s.at[m, 0, 0], e_r.at[m, 0, 0], c, other, n))
+    for s in range(1, nz):
+        for dirn in range(2):
+            for m in range(3):
+                ref = G[m].at[:, k * nz + origin(dirn, s)]
+                cond, d = zrecv(3 + m, ref, dirn, s)
+                recv(cond, d)
+                if s < nz - 1: start(*zsend(3 + m, ref, dirn, s))
+                start(cond, remote(ref, ref, e_s.at[m, dirn, s], e_r.at[m, dirn, s], c, other, n))
+    for i in range(CHIPS - 1):
+        cc = (c + CHIPS - 1 - i) % CHIPS
+        for a in range(3):
+            ref = A[a].at[part(cc, k)]
+            remote(ref, ref, p_s.at[a, i], p_r.at[a, i], c, k, n).wait_recv()
+            start(None, remote(ref, ref, d_s.at[a, 1 + i], d_r.at[a, 1 + i], c, other, n))
+    owngy.wait()
+    for i in range(CHIPS - 1):
+        remote(gy, GY.at[c], gy_s.at[i], gy_r.at[i], c, k, n).wait_recv()
+    for a in range(3):
+        for i in range(CHIPS):
+            remote(A[a].at[part(c, k)], A[a].at[part(c, k)], d_s.at[a, i], d_r.at[a, i], c, k, n).wait_recv()
+    for m in range(3):
+        ref = G[m].at[:, kn]
+        remote(ref, ref, e_s.at[m, 0, 0], e_r.at[m, 0, 0], c, k, n).wait_recv()
+        for s in range(1, nz):
+            for dirn in range(2):
+                cond = (n - s >= 0) if dirn == 0 else (n + s <= nz - 1)
+                recv(cond, remote(ref, ref, e_s.at[m, dirn, s], e_r.at[m, dirn, s], c, k, n))
+    for cond, desc in started:
+        if cond is None: desc.wait_send()
+        else: pl.when(cond)(lambda desc=desc: desc.wait_send())
+
+def gather_all(nz, wq, wk, wv, wo, gains, wg, wu, wd, gy):
+    D = wq.shape[0] * CHIPS * CORES * nz
+    cols = wg.shape[1] // CHIPS
+    bf = jnp.bfloat16
+    ff = jax.ShapeDtypeStruct((CHIPS, CORES * nz, wg.shape[0], cols), bf)
+    dma = pltpu.SemaphoreType.DMA
+    return pl.pallas_call(
+        functools.partial(gather_kernel, nz),
+        out_shape=(jax.ShapeDtypeStruct((D, wq.shape[1] + 2 * wk.shape[1]), bf), jax.ShapeDtypeStruct((D, wo.shape[1]), bf),
+                   jax.ShapeDtypeStruct((D, 128), bf), ff, ff, ff, jax.ShapeDtypeStruct((CHIPS,) + gy.shape, bf)),
+        in_specs=[ANY] * 9, out_specs=(ANY,) * 7,
+        scratch_shapes=[dma((9,)), dma((3, 3)), dma((3, 3)), dma((3,)), dma((3,)), dma((6, 2, nz)), dma((6, 2, nz)),
+                        dma((3, 4)), dma((3, 4)), dma((3, 3)), dma((3, 3)), dma((3, 2, nz)), dma((3, 2, nz))],
+        compiler_params=pltpu.CompilerParams(collective_id=0, has_side_effects=True),
+        name="gather_all",
+    )(wq, wk, wv, wo, gains, wg, wu, wd, gy)
+
+def exchange_kernel(scatter, src, dst, loc, s_s, s_r):
+    c, k, n = place()
+    others = [(c + i) % CHIPS for i in range(1, CHIPS)]
+    hello([(None, cc, k, n) for cc in others])
+    cps = []
+    for i, cc in enumerate(others):
+        cp = remote(src.at[cc] if scatter else src, dst.at[c], s_s.at[i], s_r.at[i], cc, k, n)
+        cp.start(); cps.append(cp)
+    own = pltpu.make_async_copy(src.at[c] if scatter else src, dst.at[c], loc)
+    own.start(); own.wait()
+    for cp in cps: cp.wait()
+
+def exchange(x, scatter, cid):
+    dma = pltpu.SemaphoreType.DMA
+    shape = x.shape if scatter else (CHIPS,) + x.shape
+    return pl.pallas_call(
+        functools.partial(exchange_kernel, scatter),
+        out_shape=jax.ShapeDtypeStruct(shape, x.dtype), in_specs=[ANY], out_specs=ANY,
+        scratch_shapes=[dma, dma((3,)), dma((3,))],
+        compiler_params=pltpu.CompilerParams(collective_id=cid, has_side_effects=True),
+        name="exchange%d" % cid,
+    )(x)
+
+
+def core_kernel(srcs, *refs):
+    src, dst = refs[:srcs], refs[srcs : 2 * srcs]
+    s_s, s_r = refs[2 * srcs :]
+    c, k, n = place()
+    hello([(None, c, 1 - k, n)])
+    cps = []
+    for m in range(srcs):
+        cp = remote(src[m].at[:, 1 - k], dst[m], s_s.at[m], s_r.at[m], c, 1 - k, n)
+        cp.start(); cps.append(cp)
+    for cp in cps: cp.wait()
+
+def core_exchange(xs, cid):
+    dma = pltpu.SemaphoreType.DMA
+    m = len(xs)
+    return pl.pallas_call(
+        functools.partial(core_kernel, m),
+        out_shape=tuple(jax.ShapeDtypeStruct((x.shape[0],) + x.shape[2:], x.dtype) for x in xs),
+        in_specs=[ANY] * m, out_specs=(ANY,) * m,
+        scratch_shapes=[dma((m,)), dma((m,))],
+        compiler_params=pltpu.CompilerParams(collective_id=cid, has_side_effects=True),
+        name="core_exchange",
+    )(*xs)
+
+
+def fits(mesh):
+    return mesh.shape["wide"] == CHIPS * CORES
+
+
+def fast_device(
+    nz,
+    tokens,
+    cotangent,
+    lengths,
+    positions,
+    norm_attn,
+    w_query,
+    w_key,
+    w_value,
+    w_output,
+    norm_mlp,
+    w_gate,
+    w_up,
+    w_down,
+):
+    f32, bf16 = jnp.float32, jnp.bfloat16
+    c, k, n = place()
+    slots, width = tokens.shape
+    rows = w_query.shape[0]
+    query_width, key_width = w_query.shape[1], w_key.shape[1]
+    cols = w_gate.shape[1] // CHIPS
+    inputs = tokens.astype(f32)
+    valid_rows = (jnp.arange(slots) < lengths[0]).astype(f32)[:, None]
+    cosine_table, sine_table = rope_tables(positions)
+    grad_y = cotangent.astype(f32) * valid_rows
+    grad_y_low = grad_y.astype(bf16)
+    gains = jnp.zeros((rows, 128), bf16).at[:, 0].set(norm_attn).at[:, 1].set(norm_mlp)
+    w_qkv, w_out, gain_cols, ff_gate, ff_up, ff_down, gy_all = gather_all(
+        nz, w_query, w_key, w_value, w_output, gains, w_gate, w_up, w_down, grad_y_low
+    )
+    ff_gate, ff_up, ff_down = (w.reshape(width, cols) for w in (ff_gate, ff_up, ff_down))
+    gy_all = gy_all.reshape(CHIPS * slots, width)
+    gain_attn = gain_cols[:, 0].astype(f32)
+    gain_mlp = gain_cols[:, 1].astype(f32)
+
+    normed_attn = normalize(inputs)
+    scaled_attn = (normed_attn * gain_attn).astype(bf16)
+    qkv = jnp.dot(scaled_attn, w_qkv, preferred_element_type=f32)
+    query_rotated = (
+        apply_rotary(qkv[:, :query_width].reshape(slots, QUERY_HEADS, HEAD_SIZE), cosine_table, sine_table)
+        .reshape(slots, query_width)
+        .astype(bf16)
+    )
+    key_rotated = (
+        apply_rotary(
+            qkv[:, query_width : query_width + key_width].reshape(slots, KEY_VALUE_HEADS, HEAD_SIZE),
+            cosine_table,
+            sine_table,
+        )
+        .reshape(slots, key_width)
+        .astype(bf16)
+    )
+    value_reduced = qkv[:, query_width + key_width :].astype(bf16)
+    context, log_totals = attend(query_rotated, key_rotated, value_reduced)
+    hidden = inputs + lax.dot_general(context, w_out, contract_last, preferred_element_type=f32)
+    normed_mlp = normalize(hidden)
+    scaled_mlp = (normed_mlp * gain_mlp).astype(bf16)
+
+    x_all = exchange(scaled_mlp, False, 1).reshape(CHIPS * slots, width)
+    gate = jnp.dot(x_all, ff_gate, preferred_element_type=f32)
+    up = jnp.dot(x_all, ff_up, preferred_element_type=f32)
+    sigmoid_gate = jax.nn.sigmoid(gate)
+    mixed = (gate * sigmoid_gate * up).astype(bf16)
+    grad_mixed = jnp.dot(gy_all, ff_down, preferred_element_type=f32)
+    grad_gate = (grad_mixed * up * (sigmoid_gate * (1.0 + gate * (1.0 - sigmoid_gate)))).astype(bf16)
+    grad_up = (grad_mixed * (gate * sigmoid_gate)).astype(bf16)
+    grad_x = lax.dot_general(grad_gate, ff_gate, contract_last, preferred_element_type=f32)
+    grad_x = grad_x + lax.dot_general(grad_up, ff_up, contract_last, preferred_element_type=f32)
+    grad_x_parts = exchange(grad_x.astype(bf16).reshape(CHIPS, slots, width), True, 2)
+    mlp_part = lax.dot_general(mixed, ff_down, contract_last, preferred_element_type=f32)
+    mlp_parts = exchange(mlp_part.astype(bf16).reshape(CHIPS, slots, width), True, 3)
+    output = (valid_rows * (hidden + jnp.sum(mlp_parts.astype(f32), axis=0))).astype(bf16)
+
+    grad_xn2 = jnp.sum(grad_x_parts.astype(f32), axis=0)
+    grad_gain_mlp = jnp.sum(grad_xn2 * normed_mlp, axis=0)
+    grad_hidden = grad_y + norm_back(grad_xn2 * gain_mlp, normed_mlp, hidden)
+    grad_attn_low = grad_hidden.astype(bf16)
+    grad_context = jnp.dot(grad_attn_low, w_out, preferred_element_type=f32).astype(bf16)
+    grad_query_rot, grad_key_rot, grad_value_sum = attend_back(
+        query_rotated, key_rotated, value_reduced, log_totals, grad_context
+    )
+    grad_query = (
+        invert_rotary(grad_query_rot.reshape(slots, QUERY_HEADS, HEAD_SIZE), cosine_table, sine_table)
+        .reshape(slots, query_width)
+        .astype(bf16)
+    )
+    grad_key = (
+        invert_rotary(grad_key_rot.reshape(slots, KEY_VALUE_HEADS, HEAD_SIZE), cosine_table, sine_table)
+        .reshape(slots, key_width)
+        .astype(bf16)
+    )
+    grad_qkv = jnp.concatenate([grad_query, grad_key, grad_value_sum.astype(bf16)], 1)
+    grad_xn1 = lax.dot_general(grad_qkv, w_qkv, contract_last, preferred_element_type=f32)
+    grad_gain_attn = jnp.sum(grad_xn1 * normed_attn, axis=0)
+    grad_tokens = grad_hidden + norm_back(grad_xn1 * gain_attn, normed_attn, inputs)
+
+    def over_rows(left, right):
+        return lax.dot_general(left, right, contract_first, preferred_element_type=f32)
+
+    ff_terms = [
+        over_rows(a, b).astype(bf16).reshape(CHIPS, CORES, nz, rows, cols)
+        for a, b in ((gy_all, mixed), (x_all, grad_gate), (x_all, grad_up))
+    ]
+    from_core = core_exchange(ff_terms, 4)
+    ff_sums = jnp.stack(
+        [lax.dynamic_index_in_dim(t, k, 1, False).astype(f32) + r.astype(f32) for t, r in zip(ff_terms, from_core)], 2
+    ).astype(bf16)
+    ff_sums = lax.psum_scatter(ff_sums, "narrow", scatter_dimension=1, tiled=True)
+    ff_sums = exchange(ff_sums.reshape(CHIPS, 3 * rows, cols), True, 5).reshape(CHIPS, 3, rows, cols)
+    grad_w_down, grad_w_gate, grad_w_up = (
+        jnp.transpose(ff_sums[:, m], (1, 0, 2)).reshape(rows, CHIPS * cols).astype(f32) for m in range(3)
+    )
+    attn_terms = jnp.concatenate([over_rows(grad_attn_low, context), over_rows(scaled_attn, grad_qkv)], 1)
+    attn_sums = lax.psum_scatter(attn_terms.astype(bf16), ("wide", "narrow"), scatter_dimension=0, tiled=True).astype(f32)
+    grad_w_output = attn_sums[:, :query_width]
+    grad_w_query = attn_sums[:, query_width : 2 * query_width]
+    grad_w_key = attn_sums[:, 2 * query_width : 2 * query_width + key_width]
+    grad_w_value = attn_sums[:, 2 * query_width + key_width :]
+    grad_norm_attn, grad_norm_mlp = (
+        lax.psum_scatter(g, ("wide", "narrow"), scatter_dimension=0, tiled=True) for g in (grad_gain_attn, grad_gain_mlp)
+    )
+    return (
+        output,
+        grad_tokens,
+        grad_norm_attn,
+        grad_w_query,
+        grad_w_key,
+        grad_w_value,
+        grad_w_output,
+        grad_norm_mlp,
+        grad_w_gate,
+        grad_w_up,
+        grad_w_down,
+    )
+
+
 def solution(mesh):
     in_specs = (
         P(("wide", "narrow"), None),
@@ -404,6 +738,7 @@
         P(("wide", "narrow"), None),
         P(("wide", "narrow"), None),
     )
+    body = functools.partial(fast_device, mesh.shape["narrow"]) if fits(mesh) else per_device
     return jax.shard_map(
-        per_device, mesh=mesh, in_specs=in_specs, out_specs=out_specs, check_vma=False
-    )
+        body, mesh=mesh, in_specs=in_specs, out_specs=out_specs, check_vma=False
+    )

time: 2430 us -> 1020 us (0.42)
  waiting for transfers between devices: 1940 us -> 114 us
  Pallas kernels: 0 us -> 454 us
  matrix products: 319 us -> 262 us
  other arithmetic: 28.4 us -> 72 us
  blocking collectives: 80.7 us -> 37.2 us
    reduce_scatter x1, waiting for transfers between devices: 1360 us -> 114 us  [fast_device(): lax.psum_scatter(attn_terms.astype(bf16), ('wide', 'narrow'), scatter_dim...]
    all_gather x7 -> x0, waiting for transfers between devices: 575 us -> none  [the longest x1 136 us: mlp_inputs(): up_rows = lax.all_gather(w_up, ('wide', 'narrow'), axis=0, tiled=True)]
    pallas_call x0 -> x6, Pallas kernels: none -> 454 us  [the longest x4 221 us: exchange(): pl.pallas_call(functools.partial(exchange_kernel, scatter), out_shape=jax...]
    dot_general x21 -> x15, matrix products: 226 us -> 164 us  [the longest x5 50.3 us: over_rows(): lax.dot_general(left, right, contract_first, preferred_element_type=f32)]
    unnamed x2 -> x1, blocking collectives: 80.7 us -> 37.2 us
  transfers between devices with their start and end apart: 8 -> 2, of which waited for: 8 -> 1; matrix products, arithmetic and copies ran while one was open for 5% -> 23% of each run, Pallas kernels for 0% -> 16%
where the time goes in v1:
time: 1020 us; the launch traced here: 1010 us
  Pallas kernels  454 us (45%)
  matrix products  262 us (26%)
  waiting for transfers between devices  114 us (11%)
  other arithmetic  72 us (7%)
  local copies, waits for them, and re-layouts  52.7 us (5%)
  blocking collectives  37.2 us (4%)
  between operations  17.8 us (2%)
    pallas_call x4, Pallas kernels, exchange(): pl.pallas_call(functools.partial(exchange_kernel, scatter), out_shape=jax...  221 us
    pallas_call x1, Pallas kernels, gather_all(): pl.pallas_call(functools.partial(gather_kernel, nz), out_shape=(jax.Shape...  219 us
    reduce_scatter x1, waiting for transfers between devices, fast_device(): lax.psum_scatter(attn_terms.astype(bf16), ('wide', 'narrow'), scatter_dim...  114 us
    dot_general x5, matrix products, over_rows(): lax.dot_general(left, right, contract_first, preferred_element_type=f32)  50.3 us
    unnamed x1, blocking collectives  37.2 us
    dot_general x4, matrix products, attend_back(): jnp.einsum('rqk,kd->qrd', grad_scores, key_head, preferred_element_type=j...  33.9 us
    dot_general x4, matrix products, attend_back(): jnp.einsum('rqk,qrd->kd', grad_scores, query_head, preferred_element_type...  32.6 us
  transfers between devices with their start and end apart: 2, of which 1 were waited for; matrix products, arithmetic and copies ran while one was open for 23% of the time, Pallas kernels for 16%

profile of v1, /device:TPU:0, one launch (start us, length us, event | category | flops | bytes accessed | tf_op | source)
XLA Modules:
  0.0 1009.3 jit_solution(16650215528813567886)
XLA Ops:
  14.9 2.7 fusion.43.gy
  17.5 218.8 %gather_all.1 = (bf16[2048,2560]{1,0:T(8,128)(2,1)}, bf16[2048,2048]{1,0:T(8,128)(2,1)}, bf16[2048,128]{1,0:T(8,128)(2,1)}, bf16[4,8,64,1408]{3,2,1,0:T(8,128)(2...) custom-call(bf16[64,2048]{1,0:T(8,128)(2,1)} %wq.1, ...), custom_call_target="tpu_custom_call" | custom-call | tf_op jit(solution)/shard_map/gather_all/pallas_call | solution.py:512
  238.2 8.7 fusion.164
  261.7 3.9 add_convert_fusion.1
  279.5 3.4 fusion.85
  284.4 4.2 multiply_reduce_fusion.2
  291.4 59.8 %exchange1.1 = bf16[4,320,2048]{2,1,0:T(8,128)(2,1)} custom-call(bf16[320,2048]{1,0:T(8,128)(2,1)} %multiply_convert_fusion.4.src), custom_call_target="tpu_custom_call" | custom-call | tf_op jit(solution)/shard_map/exchange1/pallas_call | solution.py:538
  351.3 13.8 %fusion.169 = f32[1280,1408]{1,0:T(8,128)} fusion(bf16[1280,2048]{1,0:T(8,128)(2,1)} %bitcast.377, bf16[2048,1408]{1,0:T(8,128)(2,1)} %bitcast.408), kind=kOutput, calls=%fused_computation.249 | convolution fusion | flops 7381975040 | bytes 18219008 | tf_op jit(solution)/shard_map/dot_general | solution.py:636
  365.1 10.3 %fusion.168 = f32[1280,1408]{1,0:T(8,128)} fusion(bf16[1280,2048]{1,0:T(8,128)(2,1)S(1)} %bitcast.378, bf16[2048,1408]{1,0:T(8,128)(2,1)S(1)} %bitcast.412), kind=kOutput, calls=%fused_computation.248 | convolution fusion | flops 7381975040 | bytes 18219008 | tf_op jit(solution)/shard_map/dot_general | solution.py:635
  375.4 19.7 %multiply_convert_fusion = (bf16[1280,1408]{1,0:T(8,128)(2,1)}, bf16[1280,1408]{1,0:T(8,128)(2,1)}, bf16[1280,1408]{1,0:T(8,128)(2,1)}) fusion(f32[1280,1408]{1,0:T(8,128)} %fusion.168, f32[1280,1408]{1,0:T(8,128)} %fusion.169, bf16[1280,2048]{1,0:T(8,128)(2,1)} %bitcast.418, bf16[2048,1408]{1,0:T(8,128)(2,1)} %bitcast.416), kind=kOutput, calls=%fused_computation.15 | convolution fusion | flops 7409008640 | bytes 36241408 | tf_op jit(solution)/shard_map/dot_general | solution.py:639
  395.1 12.5 %convolution_convert_fusion.4 = bf16[2048,1408]{1,0:T(8,128)(2,1)} fusion(bf16[1280,2048]{1,0:T(8,128)(2,1)S(1)} %bitcast.421, bf16[1280,1408]{1,0:T(8,128)(2,1)} %get-tuple-element.65), kind=kOutput, calls=%fused_computation.13 | convolution fusion | flops 7384858624 | bytes 14614528 | tf_op jit(solution)/shard_map/dot_general | solution.py:673
  407.6 10.1 convolution_convert_fusion.2
  417.7 10.1 convolution_convert_fusion.3
  427.8 13.9 %core_exchange.1 = (bf16[4,4,64,1408]{3,2,1,0:T(8,128)(2,1)}, bf16[4,4,64,1408]{3,2,1,0:T(8,128)(2,1)}, bf16[4,4,64,1408]{3,2,1,0:T(8,128)(2,1)}) custom-call(bf16[4,2,4,64,1408]{4,3,2,1,0:T(8,128)(2,1)} %bitcast.364, bf16[4,2,4,64,1408]{4,3,2,1,0:T(8,128)(2,1)} %bitcast.366, bf16[4,2,4,64,1408]{4,3,2,1,0:T(8,128)(2,1)} %bitcast.370), custom_call_target="tpu_custom_call" | custom-call | tf_op jit(solution)/shard_map/core_exchange/pallas_call | solution.py:561
  441.8 3.7 fusion.35
  446.1 2.9 fusion.33
  450.6 4.1 pad_maximum_fusion.1
  454.8 13.6 %convolution_convert_fusion.5 = bf16[1280,2048]{1,0:T(8,128)(2,1)} fusion(bf16[1280,1408]{1,0:T(8,128)(2,1)} %get-tuple-element.65, bf16[2048,1408]{1,0:T(8,128)(2,1)} %bitcast.417), kind=kOutput, calls=%fused_computation.14 | convolution fusion | flops 7384596480 | bytes 14614528 | tf_op jit(solution)/shard_map/dot_general | solution.py:645
  468.4 11.1 %fusion.170 = f32[1280,2048]{1,0:T(8,128)} fusion(bf16[1280,1408]{1,0:T(8,128)(2,1)S(1)} %copy-done.57, bf16[2048,1408]{1,0:T(8,128)(2,1)S(1)} %bitcast.415), kind=kOutput, calls=%fused_computation.250 | convolution fusion | flops 7381975040 | bytes 19857408 | tf_op jit(solution)/shard_map/dot_general | solution.py:642
  479.4 60.2 %exchange3.1 = bf16[4,320,2048]{2,1,0:T(8,128)(2,1)} custom-call(bf16[4,320,2048]{2,1,0:T(8,128)(2,1)} %bitcast.381), custom_call_target="tpu_custom_call" | custom-call | tf_op jit(solution)/shard_map/exchange3/pallas_call | solution.py:538
  539.7 5.5 convert_reduce_fusion.1
  545.2 14.3 %add_convert_fusion = bf16[1280,2048]{1,0:T(8,128)(2,1)} fusion(f32[1280,2048]{1,0:T(8,128)} %fusion.170, bf16[1280,1408]{1,0:T(8,128)(2,1)S(1)} %copy-done.55, bf16[2048,1408]{1,0:T(8,128)(2,1)} %bitcast.409), kind=kOutput, calls=%fused_computation.7 | convolution fusion | flops 7387217920 | bytes 25100288 | tf_op jit(solution)/shard_map/dot_general | solution.py:643
  559.5 60.1 %exchange2.1 = bf16[4,320,2048]{2,1,0:T(8,128)(2,1)} custom-call(bf16[4,320,2048]{2,1,0:T(8,128)(2,1)} %bitcast.382), custom_call_target="tpu_custom_call" | custom-call | tf_op jit(solution)/shard_map/exchange2/pallas_call | solution.py:538
  619.6 4.0 convert_reduce_fusion
  628.0 6.4 convolution_convert_fusion.6
  634.5 9.5 convolution_convert_fusion.1
  649.1 12.5 %copy.200 = bf16[2048,2048]{1,0:T(8,128)(2,1)} copy(bf16[2048,2048]{0,1:T(8,128)(2,1)} %convolution_convert_fusion.1) | data formatting | bytes 16777216 | tf_op jit(solution)/shard_map/convert.20
  661.6 3.8 fusion.133
  665.4 8.6 fusion.79
  674.0 3.4 fusion.134
  677.4 8.5 fusion.80
  685.8 3.6 fusion.135
  689.4 8.6 fusion.81
  698.0 3.6 fusion.132
  701.6 8.3 fusion.78
  709.9 2.6 pad_maximum_fusion.2
  715.4 7.9 fusion.87
  723.3 8.2 fusion.88
  731.5 8.4 fusion.89
  739.8 8.1 fusion.86
  758.0 8.0 convolution_convert_fusion
  766.1 11.9 %pad_maximum_fusion = bf16[2048,4608]{1,0:T(8,128)(2,1)} fusion(bf16[2048,2560]{1,0:T(8,128)(2,1)S(1)} %convolution_convert_fusion, bf16[2048,2048]{1,0:T(8,128)(2,1)S(1)} %bitcast.363), kind=kLoop, calls=%fused_computation.4 | loop fusion | flops 37748736 | bytes 37748736 | tf_op jit(solution)/shard_map/concatenate | solution.py:688
  779.2 11.2 %fusion.41 = (f32[2048]{0:T(1024)S(1)}, f32[320]{0:T(512)S(1)}, f32[320,2048]{1,0:T(8,128)}) fusion(bf16[320,2048]{1,0:T(8,128)(2,1)} %param.17, f32[320]{0:T(512)S(1)} %copy-done.43, f32[2048]{0:T(1024)S(1)} %copy-done.38, bf16[320,2560]{0,1:T(8,128)(2,1)} %fusion.105, bf16[2048,2560]{1,0:T(8,128)(2,1)} %get-tuple-element.46), kind=kOutput, calls=%fused_computation.92 | convolution fusion | flops 3360028416 | bytes 16075264 | tf_op jit(solution)/shard_map/dot_general | solution.py:668
  790.4 37.2 %all-reduce.4 = (f32[2048]{0:T(1024)S(1)}, f32[2048]{0:T(1024)S(1)}) all-reduce(f32[2048]{0:T(1024)S(1)} %get-tuple-element.57, f32[2048]{0:T(1024)S(1)} %copy-done.39), channel_id=2, replica_groups=mesh['wide'=8,'narrow'=4] {'wide','narrow'}, use_global_device_ids=true, to_apply=%region_21.22.clone | all-reduce | flops 4096 | bytes 32768
  828.8 4.3 fusion.40
  833.1 2.4 constant_dynamic-slice_fusion
  837.1 40.8 %exchange5.1 = bf16[4,192,1408]{2,1,0:T(8,128)(2,1)} custom-call(bf16[4,192,1408]{2,1,0:T(8,128)(2,1)} %bitcast.376), custom_call_target="tpu_custom_call" | custom-call | tf_op jit(solution)/shard_map/exchange5/pallas_call | solution.py:538
  883.7 114.2 %reduce-scatter.5.cloned.1.call-done = bf16[64,4608]{1,0:T(8,128)(2,1)} async-done(((bf16[2048,4608]{1,0:T(8,128)(2,1)}), bf16[64,4608]{1,0:T(8,128)(2,1)}) %reduce-scatter.5.cloned.1.call-update) | async-done | bytes 589840 | tf_op jit(solution)/shard_map/reduce_scatter | solution.py:689
  (237 shorter events, 78.2 us)
Async XLA Ops:
  8.0 825.1 %all-reduce.7.cloned.1.call-start = ((), (), s32[]{:S(2)}) async-start(), calls=%async_computation.2 | async-start | bytes 17301504
  10.0 226.3 %copy-start.40 = (f32[320]{0:T(512)}, f32[320]{0:T(512)S(1)}, u32[]{:S(2)}) copy-start(f32[320]{0:T(512)S(1)} %fusion.136) | copy-start | bytes 3844
  11.7 226.4 %copy-start.42 = (f32[320]{0:T(512)}, f32[320]{0:T(512)S(1)}, u32[]{:S(2)}) copy-start(f32[320]{0:T(512)S(1)} %add_rsqrt_fusion.1) | copy-start | bytes 3844
  13.2 225.0 %copy-start.13 = (bf16[320,2048]{1,0:T(8,128)(2,1)S(1)}, bf16[320,2048]{1,0:T(8,128)(2,1)}, u32[]{:S(2)}) copy-start(bf16[320,2048]{1,0:T(8,128)(2,1)} %param.17) | copy-start | bytes 3932164
  238.1 8.8 copy-start.37
  238.1 50.5 %copy-start.32 = (f32[2048]{0:T(1024)}, f32[2048]{0:T(1024)S(1)}, u32[]{:S(2)}) copy-start(f32[2048]{0:T(1024)S(1)} %get-tuple-element.59) | copy-start | bytes 24580
  250.8 8.2 copy-start.23
  266.0 12.1 %copy-start.25 = (bf16[320,512]{0,1:T(8,128)(2,1)}, bf16[320,512]{0,1:T(8,128)(2,1)S(1)}, u32[]{:S(2)}) copy-start(bf16[320,512]{0,1:T(8,128)(2,1)S(1)} %copy.160) | copy-start | bytes 983044
  266.2 8.6 copy-start.26
  267.9 10.2 %copy-start.29 = (bf16[320,256]{1,0:T(8,128)(2,1)}, bf16[320,256]{1,0:T(8,128)(2,1)S(1)}, u32[]{:S(2)}) copy-start(bf16[320,256]{1,0:T(8,128)(2,1)S(1)} %add_convert_fusion.2) | copy-start | bytes 491524
  272.5 10.5 %copy-start.45 = (bf16[64,8,320]{2,0,1:T(8,128)(2,1)}, bf16[64,8,320]{2,0,1:T(8,128)(2,1)S(1)}, u32[]{:S(2)}) copy-start(bf16[64,8,320]{2,0,1:T(8,128)(2,1)S(1)} %fusion.84) | copy-start | bytes 983044
  274.8 8.2 copy-start.47
  278.1 4.9 copy-start.49
  278.9 4.1 copy-start.6
  278.9 4.1 slice-start.4
  279.5 4.8 slice-start.5
  283.0 5.6 copy-start.51
  288.6 62.6 %copy-start.35 = (f32[320]{0:T(512)}, f32[320]{0:T(512)S(1)}, u32[]{:S(2)}) copy-start(f32[320]{0:T(512)S(1)} %add_rsqrt_fusion) | copy-start | bytes 3844
  291.4 73.6 %slice-start.6 = ((s8[5767168]{0:T(1024)(128)(4,1)}), s8[1572864]{0:T(1024)(128)(4,1)S(1)}, s32[]{:S(2)}) async-start(s8[5767168]{0:T(1024)(128)(4,1)} %bitcast.410), calls=%async_computation.9 | async-start | bytes 3145728
  351.2 13.8 %copy-start.16 = (bf16[4,320,2048]{2,1,0:T(8,128)(2,1)S(1)}, bf16[4,320,2048]{2,1,0:T(8,128)(2,1)}, u32[]{:S(2)}) copy-start(bf16[4,320,2048]{2,1,0:T(8,128)(2,1)} %exchange1.1) | copy-start | bytes 15728644
  351.3 13.8 %slice-start.7 = ((s8[5767168]{0:T(1024)(128)(4,1)}), s8[4194304]{0:T(1024)(128)(4,1)S(1)}, s32[]{:S(2)}) async-start(s8[5767168]{0:T(1024)(128)(4,1)} %bitcast.410), calls=%async_computation.10 | async-start | bytes 8388608
  365.1 30.0 %slice-start.10 = ((s8[5242880]{0:T(1024)(128)(4,1)}), s8[1048576]{0:T(1024)(128)(4,1)S(1)}, s32[]{:S(2)}) async-start(s8[5242880]{0:T(1024)(128)(4,1)} %bitcast.419), calls=%async_computation.13 | async-start | bytes 2097152
  375.4 19.7 %slice-start.11 = ((s8[5242880]{0:T(1024)(128)(4,1)}), s8[4194304]{0:T(1024)(128)(4,1)S(1)}, s32[]{:S(2)}) async-start(s8[5242880]{0:T(1024)(128)(4,1)} %bitcast.419), calls=%async_computation.14 | async-start | bytes 8388608
  395.1 12.6 %copy-start.54 = (bf16[1280,1408]{1,0:T(8,128)(2,1)S(1)}, bf16[1280,1408]{1,0:T(8,128)(2,1)}, u32[]{:S(2)}) copy-start(bf16[1280,1408]{1,0:T(8,128)(2,1)} %get-tuple-element.63) | copy-start | bytes 10813444
  407.6 10.1 copy-start.56
  441.7 4.3 copy-start.10
  441.8 7.2 slice-start.2
  446.1 3.6 copy-start.20
  454.6 13.8 %slice-start.8 = ((s8[5767168]{0:T(1024)(128)(4,1)}), s8[1572864]{0:T(1024)(128)(4,1)S(1)}, s32[]{:S(2)}) async-start(s8[5767168]{0:T(1024)(128)(4,1)} %bitcast.413), calls=%async_computation.11 | async-start | bytes 3145728
  454.6 543.3 %reduce-scatter.5.cloned.1.call-start = ((), (), s32[]{:S(2)}) async-start(), calls=%async_computation.1 | async-start | bytes 19464192 | tf_op jit(solution)/shard_map/reduce_scatter | solution.py:689
  454.7 13.6 %slice-start.9 = ((s8[5767168]{0:T(1024)(128)(4,1)}), s8[4194304]{0:T(1024)(128)(4,1)S(1)}, s32[]{:S(2)}) async-start(s8[5767168]{0:T(1024)(128)(4,1)} %bitcast.413), calls=%async_computation.12 | async-start | bytes 8388608
  454.8 13.6 %copy-start.57 = (bf16[1280,1408]{1,0:T(8,128)(2,1)S(1)}, bf16[1280,1408]{1,0:T(8,128)(2,1)}, u32[]{:S(2)}) copy-start(bf16[1280,1408]{1,0:T(8,128)(2,1)} %get-tuple-element.64) | copy-start | bytes 10813444
  539.7 5.5 copy-start.55
  619.6 4.1 copy-start.9
  619.6 4.1 copy-start.33
  619.6 4.1 copy-start.36
  628.0 6.4 copy-start.46
  628.0 6.4 copy-start.48
  628.0 6.4 copy-start.50
  628.0 6.5 copy-start.52
  701.6 8.3 copy-start.24
  748.0 4.5 copy-start.7
  748.0 4.5 copy-start.18
  749.2 4.7 copy-start.3
  749.2 4.7 copy-start.19
  756.6 9.4 slice-start
  758.0 8.1 slice-start.1
  779.2 11.2 %copy-start.39 = (f32[2048]{0:T(1024)S(1)}, f32[2048]{0:T(1024)}, u32[]{:S(2)}) copy-start(f32[2048]{0:T(1024)} %get-tuple-element.55) | copy-start | bytes 24580
  (24 other events, 56.9 us)
Sparse Core Ops, SparseCore 0:
  454.8 298.6 all-reduce.6
Sparse Core Ops, SparseCore 1:
  778.1 219.8 reduce-scatter.4

commit v2 on v1

--- a/solution.py
+++ b/solution.py
@@ -387,6 +387,11 @@
     w = lax.axis_index("wide"); n = lax.axis_index("narrow")
     return w // CORES, w % CORES, n
 
+def chip_at(c, r):
+    xb, yb, rx, ry = c % 2, c // 2, r % 2, r // 2
+    return (yb + ry - 2 * yb * ry) * 2 + (xb + rx - 2 * xb * rx)
+
+
 def remote(src, dst, send, recv, chip, core, z):
     return pltpu.make_async_remote_copy(src_ref=src, dst_ref=dst, send_sem=send, recv_sem=recv,
         device_id={"wide": chip * CORES + core, "narrow": z}, device_id_type=MESH)
@@ -403,15 +408,15 @@
             pl.when(cond)(sig); count = count + jnp.where(cond, 1, 0)
     pl.semaphore_wait(barrier, count)
 
-def gather_kernel(nz, wq, wk, wv, wo, gains, wg, wu, wd, gy, QKV, WO, GAIN, G0, G1, G2, GY,
+def gather_kernel(nz, wq, wk, wv, wo, gains, wgu, wd, gy, QKV, WO, GAIN, G0, G1, GY,
                   loc, a2a_s, a2a_r, gy_s, gy_r, z_s, z_r, d_s, d_r, p_s, p_r, e_s, e_r):
     c, k, n = place()
-    G = (G0, G1, G2); W = (wg, wu, wd)
-    cols = G0.shape[-1]
+    G = (G0, G1); W = (wgu, wd)
+    FF = len(G)
     rows = wq.shape[0]
     other = 1 - k
     left, right = n > 0, n < nz - 1
-    others = [(c + i) % CHIPS for i in range(1, CHIPS)]
+    others = [chip_at(c, r) for r in range(1, CHIPS)]
     hello([(None, cc, k, n) for cc in others] + [(None, c, other, n), (left, c, k, n - 1), (right, c, k, n + 1)])
     kn = k * nz + n
     b = (c * CORES + k) * nz + n
@@ -425,17 +430,20 @@
         else: pl.when(cond)(lambda: desc.wait_recv())
     def blk(z): return pl.ds(pl.multiple_of(((c * CORES + k) * nz + z) * rows, rows), rows)
     mine = blk(n)
+    def mycols(m, cc):
+        cols = G[m].shape[-1]
+        return W[m].at[:, pl.ds(pl.multiple_of(cc * cols, 128), cols)]
     q, kv = wq.shape[1], wk.shape[1]
     for i, cc in enumerate(others):
-        for m in range(3):
-            start(None, remote(W[m].at[:, pl.ds(pl.multiple_of(cc * cols, 128), cols)], G[m].at[c, kn], a2a_s.at[m, i], a2a_r.at[m, i], cc, k, n))
+        for m in range(FF):
+            start(None, remote(mycols(m, cc), G[m].at[c, kn], a2a_s.at[m, i], a2a_r.at[m, i], cc, k, n))
     own = [pltpu.make_async_copy(wq, QKV.at[mine, pl.ds(0, q)], loc.at[0]),
            pltpu.make_async_copy(wk, QKV.at[mine, pl.ds(q, kv)], loc.at[1]),
            pltpu.make_async_copy(wv, QKV.at[mine, pl.ds(q + kv, kv)], loc.at[2]),
            pltpu.make_async_copy(wo, WO.at[mine], loc.at[3]),
            pltpu.make_async_copy(gains, GAIN.at[mine], loc.at[4])]
-    ownff = [pltpu.make_async_copy(W[m].at[:, pl.ds(pl.multiple_of(c * cols, 128), cols)], G[m].at[c, kn], loc.at[5 + m]) for m in range(3)]
-    owngy = pltpu.make_async_copy(gy, GY.at[c], loc.at[8])
+    ownff = [pltpu.make_async_copy(mycols(m, c), G[m].at[c, kn], loc.at[5 + m]) for m in range(FF)]
+    owngy = pltpu.make_async_copy(gy, GY.at[0], loc.at[8])
     for cp in own + ownff + [owngy]: cp.start()
     for cp in own: cp.wait()
     A = (QKV, WO, GAIN)
@@ -453,7 +461,7 @@
         for dirn in range(2):
             start(*zsend(a, A[a].at[mine], dirn, 0))
     for i, cc in enumerate(others):
-        start(None, remote(gy, GY.at[c], gy_s.at[i], gy_r.at[i], cc, k, n))
+        start(None, remote(gy, GY.at[1 + i], gy_s.at[i], gy_r.at[i], cc, k, n))
     for s in range(1, nz):
         for dirn in range(2):
             for a in range(3):
@@ -465,7 +473,7 @@
         for i, cc in enumerate(others):
             start(None, remote(A[a].at[part(c, k)], A[a].at[part(c, k)], p_s.at[a, i], p_r.at[a, i], cc, k, n))
         start(None, remote(A[a].at[part(c, k)], A[a].at[part(c, k)], d_s.at[a, 0], d_r.at[a, 0], c, other, n))
-    for m in range(3):
+    for m in range(FF):
         ownff[m].wait()
         for i in range(CHIPS - 1):
             remote(G[m].at[c, kn], G[m].at[c, kn], a2a_s.at[m, i], a2a_r.at[m, i], c, k, n).wait_recv()
@@ -474,25 +482,25 @@
         start(None, remote(ref, ref, e_s.at[m, 0, 0], e_r.at[m, 0, 0], c, other, n))
     for s in range(1, nz):
         for dirn in range(2):
-            for m in range(3):
+            for m in range(FF):
                 ref = G[m].at[:, k * nz + origin(dirn, s)]
                 cond, d = zrecv(3 + m, ref, dirn, s)
                 recv(cond, d)
                 if s < nz - 1: start(*zsend(3 + m, ref, dirn, s))
                 start(cond, remote(ref, ref, e_s.at[m, dirn, s], e_r.at[m, dirn, s], c, other, n))
     for i in range(CHIPS - 1):
-        cc = (c + CHIPS - 1 - i) % CHIPS
+        cc = others[i]
         for a in range(3):
             ref = A[a].at[part(cc, k)]
             remote(ref, ref, p_s.at[a, i], p_r.at[a, i], c, k, n).wait_recv()
             start(None, remote(ref, ref, d_s.at[a, 1 + i], d_r.at[a, 1 + i], c, other, n))
     owngy.wait()
     for i in range(CHIPS - 1):
-        remote(gy, GY.at[c], gy_s.at[i], gy_r.at[i], c, k, n).wait_recv()
+        remote(gy, GY.at[1 + i], gy_s.at[i], gy_r.at[i], c, k, n).wait_recv()
     for a in range(3):
         for i in range(CHIPS):
             remote(A[a].at[part(c, k)], A[a].at[part(c, k)], d_s.at[a, i], d_r.at[a, i], c, k, n).wait_recv()
-    for m in range(3):
+    for m in range(FF):
         ref = G[m].at[:, kn]
         remote(ref, ref, e_s.at[m, 0, 0], e_r.at[m, 0, 0], c, k, n).wait_recv()
         for s in range(1, nz):
@@ -503,45 +511,47 @@
         if cond is None: desc.wait_send()
         else: pl.when(cond)(lambda desc=desc: desc.wait_send())
 
-def gather_all(nz, wq, wk, wv, wo, gains, wg, wu, wd, gy):
+def gather_all(nz, wq, wk, wv, wo, gains, wgu, wd, gy):
     D = wq.shape[0] * CHIPS * CORES * nz
-    cols = wg.shape[1] // CHIPS
     bf = jnp.bfloat16
-    ff = jax.ShapeDtypeStruct((CHIPS, CORES * nz, wg.shape[0], cols), bf)
+    def ff(w):
+        return jax.ShapeDtypeStruct((CHIPS, CORES * nz, w.shape[0], w.shape[1] // CHIPS), bf)
     dma = pltpu.SemaphoreType.DMA
     return pl.pallas_call(
         functools.partial(gather_kernel, nz),
         out_shape=(jax.ShapeDtypeStruct((D, wq.shape[1] + 2 * wk.shape[1]), bf), jax.ShapeDtypeStruct((D, wo.shape[1]), bf),
-                   jax.ShapeDtypeStruct((D, 128), bf), ff, ff, ff, jax.ShapeDtypeStruct((CHIPS,) + gy.shape, bf)),
-        in_specs=[ANY] * 9, out_specs=(ANY,) * 7,
+                   jax.ShapeDtypeStruct((D, 128), bf), ff(wgu), ff(wd), jax.ShapeDtypeStruct((CHIPS,) + gy.shape, bf)),
+        in_specs=[ANY] * 8, out_specs=(ANY,) * 6,
         scratch_shapes=[dma((9,)), dma((3, 3)), dma((3, 3)), dma((3,)), dma((3,)), dma((6, 2, nz)), dma((6, 2, nz)),
                         dma((3, 4)), dma((3, 4)), dma((3, 3)), dma((3, 3)), dma((3, 2, nz)), dma((3, 2, nz))],
         compiler_params=pltpu.CompilerParams(collective_id=0, has_side_effects=True),
         name="gather_all",
-    )(wq, wk, wv, wo, gains, wg, wu, wd, gy)
-
-def exchange_kernel(scatter, src, dst, loc, s_s, s_r):
+    )(wq, wk, wv, wo, gains, wgu, wd, gy)
+
+def exchange_kernel(by_chip, src, dst, loc, s_s, s_r):
     c, k, n = place()
-    others = [(c + i) % CHIPS for i in range(1, CHIPS)]
-    hello([(None, cc, k, n) for cc in others])
-    cps = []
-    for i, cc in enumerate(others):
-        cp = remote(src.at[cc] if scatter else src, dst.at[c], s_s.at[i], s_r.at[i], cc, k, n)
-        cp.start(); cps.append(cp)
-    own = pltpu.make_async_copy(src.at[c] if scatter else src, dst.at[c], loc)
-    own.start(); own.wait()
+    hello([(None, chip_at(c, r), k, n) for r in (1, 2, 3)])
+    cps = [pltpu.make_async_copy(src.at[c if by_chip else 0], dst.at[c if by_chip else 0], loc)]
+    for r in (1, 2, 3):
+        cc = chip_at(c, r)
+        cps.append(remote(src.at[cc if by_chip else r], dst.at[c if by_chip else r], s_s.at[r - 1], s_r.at[r - 1], cc, k, n))
+    for cp in cps: cp.start()
     for cp in cps: cp.wait()
 
-def exchange(x, scatter, cid):
+
+def exchange(x, cid, by_chip=False):
     dma = pltpu.SemaphoreType.DMA
-    shape = x.shape if scatter else (CHIPS,) + x.shape
     return pl.pallas_call(
-        functools.partial(exchange_kernel, scatter),
-        out_shape=jax.ShapeDtypeStruct(shape, x.dtype), in_specs=[ANY], out_specs=ANY,
+        functools.partial(exchange_kernel, by_chip),
+        out_shape=jax.ShapeDtypeStruct(x.shape, x.dtype), in_specs=[ANY], out_specs=ANY,
         scratch_shapes=[dma, dma((3,)), dma((3,))],
         compiler_params=pltpu.CompilerParams(collective_id=cid, has_side_effects=True),
-        name="exchange%d" % cid,
+        name="exchange",
     )(x)
+
+
+def plane_swap(x, cid):
+    return exchange(x, cid, True)
 
 
 def core_kernel(srcs, *refs):
@@ -566,6 +576,260 @@
         compiler_params=pltpu.CompilerParams(collective_id=cid, has_side_effects=True),
         name="core_exchange",
     )(*xs)
+
+
+def mlp_kernel(x, gy, gu_hbm, gd_hbm, x_all, mix_all, ggu_all, gx_parts, mlp_parts,
+               xs, gys, gu, gd, mix, ggu, gx, mo, load, ag_s, ag_r, rs_s, rs_r, own, out):
+    c, k, n = place()
+    slots, width = x.shape
+    half = slots // 2
+    cols = gd.shape[-1]
+    hello([(None, chip_at(c, r), k, n) for r in (1, 2, 3)])
+    loads = [pltpu.make_async_copy(x, xs.at[0], load.at[0])]
+    sends = [remote(x, xs.at[r], ag_s.at[r], ag_r.at[r], chip_at(c, r), k, n) for r in (1, 2)]
+    for cp in sends: cp.start()
+    loads += [pltpu.make_async_copy(gu_hbm, gu, load.at[1]), pltpu.make_async_copy(gd_hbm, gd, load.at[2]),
+              pltpu.make_async_copy(gy, gys, load.at[3])]
+    for cp in loads: cp.start()
+    relays = [remote(xs.at[1, pl.ds(0, half)], xs.at[3, pl.ds(0, half)], ag_s.at[0], ag_r.at[0], chip_at(c, 2), k, n),
+              remote(xs.at[2, pl.ds(half, half)], xs.at[3, pl.ds(half, half)], ag_s.at[3], ag_r.at[3], chip_at(c, 1), k, n)]
+    for cp in loads: cp.wait()
+
+    def block(r, carry):
+        @pl.when(r == 1)
+        def _():
+            for cp in sends: cp.wait_recv()
+            for cp in relays: cp.start()
+        @pl.when(r == 3)
+        def _():
+            for cp in relays: cp.wait_recv()
+        def chunk(col, w):
+            h = jnp.dot(xs[r], gu[:, pl.ds(2 * col, 2 * w)], preferred_element_type=jnp.float32)
+            gm = jnp.dot(gys[r], gd[:, pl.ds(col, w)], preferred_element_type=jnp.float32)
+            for q in range(w // 128):
+                gate, up, g = h[:, 256 * q : 256 * q + 128], h[:, 256 * q + 128 : 256 * q + 256], gm[:, 128 * q : 128 * q + 128]
+                sg = 1.0 / (1.0 + jnp.exp(-gate))
+                act = gate * sg
+                mix[r, :, pl.ds(col + 128 * q, 128)] = (act * up).astype(jnp.bfloat16)
+                ggu[r, :, pl.ds(2 * col + 256 * q, 128)] = (g * up * (sg * (1.0 + gate * (1.0 - sg)))).astype(jnp.bfloat16)
+                ggu[r, :, pl.ds(2 * col + 256 * q + 128, 128)] = (g * act).astype(jnp.bfloat16)
+        def pair(j, carry):
+            chunk(pl.multiple_of(j * 256, 256), 256)
+            return carry
+        lax.fori_loop(0, cols // 256, pair, 0)
+        if cols % 256: chunk(cols - 128, 128)
+        def back(i, carry):
+            at = pl.ds(pl.multiple_of(i * 256, 256), 256)
+            gx[r, :, at] = lax.dot_general(ggu[r], gu[at, :], contract_last, preferred_element_type=jnp.float32).astype(jnp.bfloat16)
+            return carry
+        lax.fori_loop(0, width // 256, back, 0)
+        @pl.when(r == 0)
+        def _(): pltpu.make_async_copy(gx.at[0], gx_parts.at[0], own).start()
+        @pl.when(r > 0)
+        def _(): remote(gx.at[r], gx_parts.at[r], rs_s.at[r], rs_r.at[r], chip_at(c, r), k, n).start()
+        def down(i, carry):
+            at = pl.ds(pl.multiple_of(i * 256, 256), 256)
+            mo[r, :, at] = lax.dot_general(mix[r], gd[at, :], contract_last, preferred_element_type=jnp.float32).astype(jnp.bfloat16)
+            return carry
+        lax.fori_loop(0, width // 256, down, 0)
+        for i, (a, b) in enumerate(((xs, x_all), (mix, mix_all), (ggu, ggu_all), (mo, mlp_parts))):
+            pltpu.make_async_copy(a.at[r], b.at[r], out.at[i, r]).start()
+        return carry
+    lax.fori_loop(0, CHIPS, block, 0)
+    for cp in sends + relays: cp.wait_send()
+    pltpu.make_async_copy(gx.at[0], gx_parts.at[0], own).wait()
+    for r in range(CHIPS):
+        for i, (a, b) in enumerate(((xs, x_all), (mix, mix_all), (ggu, ggu_all), (mo, mlp_parts))):
+            pltpu.make_async_copy(a.at[r], b.at[r], out.at[i, r]).wait()
+    for r in (1, 2, 3):
+        remote(gx.at[r], gx_parts.at[r], rs_s.at[r], rs_r.at[r], chip_at(c, r), k, n).wait()
+
+
+def mlp_all(x, gy, gu, gd):
+    slots, width = x.shape
+    cols = gd.shape[1]
+    bf, dma, vm = jnp.bfloat16, pltpu.SemaphoreType.DMA, pltpu.VMEM
+    def blocks(w): return jax.ShapeDtypeStruct((CHIPS, slots, w), bf)
+    flops = 2 * 6 * CHIPS * slots * width * cols
+    return pl.pallas_call(
+        mlp_kernel,
+        out_shape=(blocks(width), blocks(cols), blocks(2 * cols), blocks(width), blocks(width)),
+        in_specs=[ANY] * 4, out_specs=(ANY,) * 5,
+        scratch_shapes=[vm((CHIPS, slots, width), bf), vm((CHIPS, slots, width), bf), vm((width, 2 * cols), bf), vm((width, cols), bf),
+                        vm((CHIPS, slots, cols), bf), vm((CHIPS, slots, 2 * cols), bf), vm((CHIPS, slots, width), bf),
+                        vm((CHIPS, slots, width), bf), dma((4,)), dma((4,)), dma((4,)), dma((4,)), dma((4,)), dma, dma((4, 4))],
+        compiler_params=pltpu.CompilerParams(collective_id=1, has_side_effects=True, vmem_limit_bytes=62 << 20),
+        cost_estimate=pl.CostEstimate(flops=flops, bytes_accessed=60 << 20, transcendentals=CHIPS * slots * cols),
+        name="mlp_all",
+    )(x, gy, gu, gd)
+
+
+PAIR = 2 * HEAD_SIZE
+REPEAT = QUERY_HEADS // KEY_VALUE_HEADS
+PAIRS = REPEAT // 2
+
+
+def lane_tables(positions):
+    cosine, sine = rope_tables(positions)
+    first = jnp.arange(HEAD_SIZE) < HEAD_SIZE // 2
+    low, high = jnp.where(first, -sine, 0.0), jnp.where(first, 0.0, sine)
+    return jnp.stack([jnp.concatenate([t, t], 1) for t in (cosine, low, high)])
+
+
+def rotate(u, tables):
+    half = HEAD_SIZE // 2
+    return u * tables[0] + pltpu.roll(u, PAIR - half, 1) * tables[1] + pltpu.roll(u, half, 1) * tables[2]
+
+
+def unrotate(g, tables):
+    half = HEAD_SIZE // 2
+    return g * tables[0] + pltpu.roll(g * tables[2], PAIR - half, 1) + pltpu.roll(g * tables[1], half, 1)
+
+
+def row_blocks(slots):
+    return [(at, min(128, slots - at), at + 128) for at in range(0, slots, 128)]
+
+
+def causal(s, below, fill):
+    clear = s.shape[1] - 128
+    last = jnp.where(below, s[:, clear:], fill)
+    return jnp.concatenate([s[:, :clear], last], 1) if clear else last
+
+
+def attend_kernel(q_ref, k_ref, v_ref, tab_ref, qr_ref, k_out, v_out, lse_ref, ctx_ref, ks, vs):
+    g = pl.program_id(0)
+    f32, bf16 = jnp.float32, jnp.bfloat16
+    slots = q_ref.shape[0]
+    @pl.when(g == 0)
+    def _():
+        ks[...] = jnp.zeros_like(ks)
+        vs[...] = jnp.zeros_like(vs)
+    lane = lax.broadcasted_iota(jnp.int32, (slots, PAIR), 1)
+    tables = (tab_ref[0], tab_ref[1], tab_ref[2])
+    key, val = rotate(k_ref[...], tables), v_ref[...]
+    odd = g % 2 == 1
+    for x, own, stack, scale in ((key, k_out, ks, HEAD_SIZE ** -0.5), (val, v_out, vs, 1.0)):
+        x = jnp.where(lane < HEAD_SIZE, jnp.where(odd, pltpu.roll(x, HEAD_SIZE, 1), x), 0.0).astype(bf16)
+        own[0] = x
+        x = x.astype(f32) * scale
+        stack[0, 0:slots, :] = x.astype(bf16)
+        stack[1, 0:slots, :] = pltpu.roll(x, HEAD_SIZE, 1).astype(bf16)
+    for at, size, keys in row_blocks(slots):
+        below = lax.broadcasted_iota(jnp.int32, (size, 128), 0) >= lax.broadcasted_iota(jnp.int32, (size, 128), 1)
+        lse = jnp.zeros((size, PAIR), f32)
+        here = lane[0:size]
+        for p in range(PAIRS):
+            span = slice(p * PAIR, (p + 1) * PAIR)
+            rows = slice(at, at + size)
+            q = rotate(q_ref[rows, span], tuple(t[rows] for t in tables)).astype(bf16)
+            qr_ref[rows, span] = q
+            ctx = jnp.zeros((size, PAIR), f32)
+            for h in range(2):
+                s = lax.dot_general(q, ks[h, 0:keys, :], contract_last, preferred_element_type=f32)
+                s = causal(s, below, masked_score)
+                peak = jnp.max(s, axis=-1, keepdims=True)
+                e = jnp.exp(s - peak)
+                total = jnp.sum(e, axis=-1, keepdims=True)
+                lse = jnp.where(here == 2 * p + h, peak + jnp.log(total), lse)
+                probs = (e * (1.0 / total)).astype(bf16)
+                ctx = ctx + jnp.dot(probs, vs[h, 0:keys, :], preferred_element_type=f32)
+            ctx_ref[rows, span] = ctx.astype(bf16)
+        lse_ref[0, at : at + size, :] = lse
+
+
+def attend_all(qkv, tables):
+    slots = qkv.shape[0]
+    wide = REPEAT * HEAD_SIZE
+    first = QUERY_HEADS * HEAD_SIZE // PAIR
+    bf16 = jnp.bfloat16
+    keys = -(-slots // 128) * 128
+    shape = jax.ShapeDtypeStruct
+    per_head = pl.BlockSpec((1, slots, PAIR), lambda g: (g, 0, 0))
+    wide_spec = pl.BlockSpec((slots, wide), lambda g: (0, g))
+    return pl.pallas_call(
+        attend_kernel,
+        grid=(KEY_VALUE_HEADS,),
+        out_shape=(shape((slots, QUERY_HEADS * HEAD_SIZE), bf16), shape((KEY_VALUE_HEADS, slots, PAIR), bf16),
+                   shape((KEY_VALUE_HEADS, slots, PAIR), bf16), shape((KEY_VALUE_HEADS, slots, PAIR), jnp.float32),
+                   shape((slots, QUERY_HEADS * HEAD_SIZE), bf16)),
+        in_specs=[wide_spec, pl.BlockSpec((slots, PAIR), lambda g: (0, first + g // 2)),
+                  pl.BlockSpec((slots, PAIR), lambda g: (0, first + KEY_VALUE_HEADS // 2 + g // 2)),
+                  pl.BlockSpec((3, slots, PAIR), lambda g: (0, 0, 0))],
+        out_specs=(wide_spec, per_head, per_head, per_head, wide_spec),
+        scratch_shapes=[pltpu.VMEM((2, keys, PAIR), bf16), pltpu.VMEM((2, keys, PAIR), bf16)],
+        compiler_params=pltpu.CompilerParams(vmem_limit_bytes=32 << 20),
+        name="attend",
+    )(qkv, qkv, qkv, tables)
+
+
+def attend_back_kernel(q_ref, k_ref, v_ref, lse_ref, gc_ref, tab_ref, gq_ref, gk_ref, gv_ref, ks, kt, vt, ds, pr, qs, gs):
+    g = pl.program_id(0)
+    f32, bf16 = jnp.float32, jnp.bfloat16
+    slots = q_ref.shape[0]
+    scale = HEAD_SIZE ** -0.5
+    @pl.when(g == 0)
+    def _():
+        for ref in (ks, kt, vt, ds, pr): ref[...] = jnp.zeros_like(ref)
+    lane = lax.broadcasted_iota(jnp.int32, (slots, PAIR), 1)
+    tables = (tab_ref[0], tab_ref[1], tab_ref[2])
+    key, val = k_ref[0].astype(f32), v_ref[0].astype(f32)
+    for stack, x in ((ks, key * scale), (kt, key), (vt, val)):
+        stack[0, 0:slots, :] = x.astype(bf16)
+        stack[1, 0:slots, :] = pltpu.roll(x, HEAD_SIZE, 1).astype(bf16)
+    for at, size, keys in row_blocks(slots):
+        rows = slice(at, at + size)
+        below = lax.broadcasted_iota(jnp.int32, (size, 128), 0) >= lax.broadcasted_iota(jnp.int32, (size, 128), 1)
+        lse = lse_ref[0, rows, :]
+        for p in range(PAIRS):
+            span = slice(p * PAIR, (p + 1) * PAIR)
+            deep = slice(p * slots + at, p * slots + at + size)
+            q, gc = q_ref[rows, span], gc_ref[rows, span]
+            qs[deep, :] = q
+            gs[deep, :] = gc
+            gq = jnp.zeros((size, PAIR), f32)
+            for h in range(2):
+                s = lax.dot_general(q, ks[h, 0:keys, :], contract_last, preferred_element_type=f32)
+                e = jnp.exp(s - lse[:, 2 * p + h : 2 * p + h + 1])
+                probs = causal(e, below, 0.0)
+                pr[h, deep, 0:keys] = probs.astype(bf16)
+                gp = lax.dot_general(gc, vt[h, 0:keys, :], contract_last, preferred_element_type=f32)
+                inner = jnp.sum(gp * probs, axis=-1, keepdims=True)
+                grad = (probs * (gp - inner) * scale).astype(bf16)
+                ds[h, deep, 0:keys] = grad
+                gq = gq + jnp.dot(grad, kt[h, 0:keys, :], preferred_element_type=f32)
+            gq_ref[rows, span] = unrotate(gq, tuple(t[rows] for t in tables)).astype(bf16)
+    for src, right, out, turn in ((ds, qs, gk_ref, True), (pr, gs, gv_ref, False)):
+        lo, hi = (
+            lax.dot_general(src[h], right[...], contract_first, preferred_element_type=f32)[0:slots] for h in range(2)
+        )
+        x = jnp.where(lane < HEAD_SIZE, lo + pltpu.roll(hi, HEAD_SIZE, 1), 0.0)
+        if turn: x = unrotate(x, tables)
+        @pl.when(g % 2 == 0)
+        def _(): out[...] = x
+        @pl.when(g % 2 == 1)
+        def _(): out[...] = jnp.where(lane < HEAD_SIZE, out[...], pltpu.roll(x, HEAD_SIZE, 1))
+
+
+def attend_back_all(q, k, v, lse, grad_context, tables):
+    slots = q.shape[0]
+    wide = REPEAT * HEAD_SIZE
+    bf16, f32, vm = jnp.bfloat16, jnp.float32, pltpu.VMEM
+    keys = -(-slots // 128) * 128
+    shape = jax.ShapeDtypeStruct
+    per_head = pl.BlockSpec((1, slots, PAIR), lambda g: (g, 0, 0))
+    wide_spec = pl.BlockSpec((slots, wide), lambda g: (0, g))
+    two = pl.BlockSpec((slots, PAIR), lambda g: (0, g // 2))
+    return pl.pallas_call(
+        attend_back_kernel,
+        grid=(KEY_VALUE_HEADS,),
+        out_shape=(shape((slots, QUERY_HEADS * HEAD_SIZE), bf16), shape((slots, KEY_VALUE_HEADS * HEAD_SIZE), f32),
+                   shape((slots, KEY_VALUE_HEADS * HEAD_SIZE), f32)),
+        in_specs=[wide_spec, per_head, per_head, per_head, wide_spec, pl.BlockSpec((3, slots, PAIR), lambda g: (0, 0, 0))],
+        out_specs=(wide_spec, two, two),
+        scratch_shapes=[vm((2, keys, PAIR), bf16)] * 3 + [vm((2, PAIRS * slots, keys), bf16)] * 2 + [vm((PAIRS * slots, PAIR), bf16)] * 2,
+        compiler_params=pltpu.CompilerParams(vmem_limit_bytes=40 << 20),
+        name="attend_back",
+    )(q, k, v, lse, grad_context, tables)
 
 
 def fits(mesh):
@@ -596,54 +860,30 @@
     cols = w_gate.shape[1] // CHIPS
     inputs = tokens.astype(f32)
     valid_rows = (jnp.arange(slots) < lengths[0]).astype(f32)[:, None]
-    cosine_table, sine_table = rope_tables(positions)
+    tables = lane_tables(positions)
     grad_y = cotangent.astype(f32) * valid_rows
     grad_y_low = grad_y.astype(bf16)
     gains = jnp.zeros((rows, 128), bf16).at[:, 0].set(norm_attn).at[:, 1].set(norm_mlp)
-    w_qkv, w_out, gain_cols, ff_gate, ff_up, ff_down, gy_all = gather_all(
-        nz, w_query, w_key, w_value, w_output, gains, w_gate, w_up, w_down, grad_y_low
-    )
-    ff_gate, ff_up, ff_down = (w.reshape(width, cols) for w in (ff_gate, ff_up, ff_down))
-    gy_all = gy_all.reshape(CHIPS * slots, width)
+    chunks = (rows, w_gate.shape[1] // 128, 128)
+    w_gate_up = jnp.stack([w_gate.reshape(chunks), w_up.reshape(chunks)], 2).reshape(rows, 2 * w_gate.shape[1])
+    w_qkv, w_out, gain_cols, ff_gate_up, ff_down, gy_all = gather_all(
+        nz, w_query, w_key, w_value, w_output, gains, w_gate_up, w_down, grad_y_low
+    )
+    ff_gate_up, ff_down = ff_gate_up.reshape(width, 2 * cols), ff_down.reshape(width, cols)
     gain_attn = gain_cols[:, 0].astype(f32)
     gain_mlp = gain_cols[:, 1].astype(f32)
 
     normed_attn = normalize(inputs)
     scaled_attn = (normed_attn * gain_attn).astype(bf16)
     qkv = jnp.dot(scaled_attn, w_qkv, preferred_element_type=f32)
-    query_rotated = (
-        apply_rotary(qkv[:, :query_width].reshape(slots, QUERY_HEADS, HEAD_SIZE), cosine_table, sine_table)
-        .reshape(slots, query_width)
-        .astype(bf16)
-    )
-    key_rotated = (
-        apply_rotary(
-            qkv[:, query_width : query_width + key_width].reshape(slots, KEY_VALUE_HEADS, HEAD_SIZE),
-            cosine_table,
-            sine_table,
-        )
-        .reshape(slots, key_width)
-        .astype(bf16)
-    )
-    value_reduced = qkv[:, query_width + key_width :].astype(bf16)
-    context, log_totals = attend(query_rotated, key_rotated, value_reduced)
+    query_rotated, key_rotated, value_reduced, log_totals, context = attend_all(qkv, tables)
     hidden = inputs + lax.dot_general(context, w_out, contract_last, preferred_element_type=f32)
     normed_mlp = normalize(hidden)
     scaled_mlp = (normed_mlp * gain_mlp).astype(bf16)
 
-    x_all = exchange(scaled_mlp, False, 1).reshape(CHIPS * slots, width)
-    gate = jnp.dot(x_all, ff_gate, preferred_element_type=f32)
-    up = jnp.dot(x_all, ff_up, preferred_element_type=f32)
-    sigmoid_gate = jax.nn.sigmoid(gate)
-    mixed = (gate * sigmoid_gate * up).astype(bf16)
-    grad_mixed = jnp.dot(gy_all, ff_down, preferred_element_type=f32)
-    grad_gate = (grad_mixed * up * (sigmoid_gate * (1.0 + gate * (1.0 - sigmoid_gate)))).astype(bf16)
-    grad_up = (grad_mixed * (gate * sigmoid_gate)).astype(bf16)
-    grad_x = lax.dot_general(grad_gate, ff_gate, contract_last, preferred_element_type=f32)
-    grad_x = grad_x + lax.dot_general(grad_up, ff_up, contract_last, preferred_element_type=f32)
-    grad_x_parts = exchange(grad_x.astype(bf16).reshape(CHIPS, slots, width), True, 2)
-    mlp_part = lax.dot_general(mixed, ff_down, contract_last, preferred_element_type=f32)
-    mlp_parts = exchange(mlp_part.astype(bf16).reshape(CHIPS, slots, width), True, 3)
+    x_all, mixed, grad_gate_up, grad_x_parts, mlp_part = mlp_all(scaled_mlp, gy_all, ff_gate_up, ff_down)
+    x_all, mixed, grad_gate_up, gy_all = (t.reshape(CHIPS * slots, -1) for t in (x_all, mixed, grad_gate_up, gy_all))
+    mlp_parts = exchange(mlp_part, 3)
     output = (valid_rows * (hidden + jnp.sum(mlp_parts.astype(f32), axis=0))).astype(bf16)
 
     grad_xn2 = jnp.sum(grad_x_parts.astype(f32), axis=0)
@@ -651,20 +891,10 @@
     grad_hidden = grad_y + norm_back(grad_xn2 * gain_mlp, normed_mlp, hidden)
     grad_attn_low = grad_hidden.astype(bf16)
     grad_context = jnp.dot(grad_attn_low, w_out, preferred_element_type=f32).astype(bf16)
-    grad_query_rot, grad_key_rot, grad_value_sum = attend_back(
-        query_rotated, key_rotated, value_reduced, log_totals, grad_context
-    )
-    grad_query = (
-        invert_rotary(grad_query_rot.reshape(slots, QUERY_HEADS, HEAD_SIZE), cosine_table, sine_table)
-        .reshape(slots, query_width)
-        .astype(bf16)
-    )
-    grad_key = (
-        invert_rotary(grad_key_rot.reshape(slots, KEY_VALUE_HEADS, HEAD_SIZE), cosine_table, sine_table)
-        .reshape(slots, key_width)
-        .astype(bf16)
-    )
-    grad_qkv = jnp.concatenate([grad_query, grad_key, grad_value_sum.astype(bf16)], 1)
+    grad_query, grad_key, grad_value = attend_back_all(
+        query_rotated, key_rotated, value_reduced, log_totals, grad_context, tables
+    )
+    grad_qkv = jnp.concatenate([grad_query, grad_key.astype(bf16), grad_value.astype(bf16)], 1)
     grad_xn1 = lax.dot_general(grad_qkv, w_qkv, contract_last, preferred_element_type=f32)
     grad_gain_attn = jnp.sum(grad_xn1 * normed_attn, axis=0)
     grad_tokens = grad_hidden + norm_back(grad_xn1 * gain_attn, normed_attn, inputs)
@@ -673,18 +903,18 @@
         return lax.dot_general(left, right, contract_first, preferred_element_type=f32)
 
     ff_terms = [
-        over_rows(a, b).astype(bf16).reshape(CHIPS, CORES, nz, rows, cols)
-        for a, b in ((gy_all, mixed), (x_all, grad_gate), (x_all, grad_up))
+        over_rows(a, b).astype(bf16).reshape(CHIPS, CORES, nz, rows, -1) for a, b in ((gy_all, mixed), (x_all, grad_gate_up))
     ]
     from_core = core_exchange(ff_terms, 4)
-    ff_sums = jnp.stack(
-        [lax.dynamic_index_in_dim(t, k, 1, False).astype(f32) + r.astype(f32) for t, r in zip(ff_terms, from_core)], 2
+    ff_sums = jnp.concatenate(
+        [lax.dynamic_index_in_dim(t, k, 1, False).astype(f32) + r.astype(f32) for t, r in zip(ff_terms, from_core)], 3
     ).astype(bf16)
-    ff_sums = lax.psum_scatter(ff_sums, "narrow", scatter_dimension=1, tiled=True)
-    ff_sums = exchange(ff_sums.reshape(CHIPS, 3 * rows, cols), True, 5).reshape(CHIPS, 3, rows, cols)
-    grad_w_down, grad_w_gate, grad_w_up = (
-        jnp.transpose(ff_sums[:, m], (1, 0, 2)).reshape(rows, CHIPS * cols).astype(f32) for m in range(3)
-    )
+    ff_sums = lax.psum_scatter(jnp.swapaxes(ff_sums, 0, 1), "narrow", scatter_dimension=0, tiled=True)
+    ff_sums = plane_swap(ff_sums.reshape(CHIPS, rows, 3 * cols), 5)
+    grad_w_down = jnp.swapaxes(ff_sums[:, :, :cols], 0, 1).reshape(rows, CHIPS * cols).astype(f32)
+    grad_gate_up = jnp.swapaxes(ff_sums[:, :, cols:], 0, 1).reshape(rows, CHIPS * cols // 128, 2, 128).astype(f32)
+    grad_w_gate = grad_gate_up[:, :, 0].reshape(rows, CHIPS * cols)
+    grad_w_up = grad_gate_up[:, :, 1].reshape(rows, CHIPS * cols)
     attn_terms = jnp.concatenate([over_rows(grad_attn_low, context), over_rows(scaled_attn, grad_qkv)], 1)
     attn_sums = lax.psum_scatter(attn_terms.astype(bf16), ("wide", "narrow"), scatter_dimension=0, tiled=True).astype(f32)
     grad_w_output = attn_sums[:, :query_width]

time: 1020 us -> 846 us (0.83)
  matrix products: 262 us -> 71.7 us
  Pallas kernels: 454 us -> 493 us
  other arithmetic: 72 us -> 56.4 us
    dot_general x30 -> x0, matrix products: 181 us -> none  [the longest x4 33.9 us: attend_back(): jnp.einsum('rqk,kd->qrd', grad_scores, key_head, preferred_element_type=j...]
    pallas_call x4 -> x5, Pallas kernels: 221 us -> 261 us  [the longest x1 119 us: mlp_all(): pl.pallas_call(mlp_kernel, out_shape=(blocks(width), blocks(cols), blocks...]
    dot_general x5 -> x4, matrix products: 50.3 us -> 45.6 us  [over_rows(): lax.dot_general(left, right, contract_first, preferred_element_type=f32)]
  transfers between devices with their start and end apart: 2 -> 2, of which waited for: 1 -> 1; matrix products, arithmetic and copies ran while one was open for 23% -> 11% of each run, Pallas kernels for 16% -> 14%
where the time goes in v2:
time: 846 us; the launch traced here: 839 us
  Pallas kernels  493 us (58%)
  waiting for transfers between devices  112 us (13%)
  matrix products  71.7 us (8%)
  other arithmetic  56.4 us (7%)
  local copies, waits for them, and re-layouts  52.8 us (6%)
  blocking collectives  37.6 us (4%)
  between operations  15.6 us (2%)
    pallas_call x1, Pallas kernels, gather_all(): pl.pallas_call(functools.partial(gather_kernel, nz), out_shape=(jax.Shape...  219 us
    pallas_call x1, Pallas kernels, mlp_all(): pl.pallas_call(mlp_kernel, out_shape=(blocks(width), blocks(cols), blocks...  119 us
    reduce_scatter x1, waiting for transfers between devices, fast_device(): lax.psum_scatter(attn_terms.astype(bf16), ('wide', 'narrow'), scatter_dim...  112 us
    pallas_call x2, Pallas kernels, exchange(): pl.pallas_call(functools.partial(exchange_kernel, by_chip), out_shape=jax...  93.7 us
    dot_general x4, matrix products, over_rows(): lax.dot_general(left, right, contract_first, preferred_element_type=f32)  45.6 us
    unnamed x1, blocking collectives  37.6 us
    pallas_call x1, Pallas kernels, attend_back_all(): pl.pallas_call(attend_back_kernel, grid=(KEY_VALUE_HEADS,), out_shape=(sh...  25 us
    pallas_call x1, Pallas kernels, attend_all(): pl.pallas_call(attend_kernel, grid=(KEY_VALUE_HEADS,), out_shape=(shape((...  22.8 us
  transfers between devices with their start and end apart: 2, of which 1 were waited for; matrix products, arithmetic and copies ran while one was open for 11% of the time, Pallas kernels for 14%

profile of v2, /device:TPU:0, one launch (start us, length us, event | category | flops | bytes accessed | tf_op | source)
XLA Modules:
  0.0 839.1 jit_solution(9968449762550435280)
XLA Ops:
  9.2 1.5 stack_reshape.6
  10.7 1.5 stack_reshape.7
  12.4 1.5 copy.45
  13.9 2.0 reshape.158.wgu
  17.4 1.3 fusion.13.gy
  19.6 218.8 %gather_all.1 = (bf16[2048,2560]{1,0:T(8,128)(2,1)}, bf16[2048,2048]{1,0:T(8,128)(2,1)}, bf16[2048,128]{1,0:T(8,128)(2,1)}, bf16[4,8,64,2816]{3,2,1,0:T(8,128)(2...) custom-call(bf16[64,2048]{1,0:T(8,128)(2,1)} %wq.1, bf16[64,256]{1,0:T(8,128)(2,1)} %wk.1, ...), custom_call_target="tpu_custom_call" | custom-call | tf_op jit(solution)/shard_map/gather_all/pallas_call | solution.py:520
  238.3 1.7 convert_reduce_fusion.2
  241.6 6.8 fusion.18.q_ref.k_ref.v_ref
  248.4 22.8 %attend.1 = (bf16[320,2048]{1,0:T(8,128)(2,1)S(1)}, bf16[4,320,128]{2,1,0:T(8,128)(2,1)S(1)}, bf16[4,320,128]{2,1,0:T(8,128)(2,1)S(1)}, f32[4,320,128]{2,1,0:T(8,128)S(1)}, bf16[320,2048]{1,0:T(8,128)(2,1)S(1)}) custom-call(f32[320,2560]{1,0:T(8,128)S(1)} %fusion.18.q_ref.k_ref.v_ref, f32[320,2560]{1,0:T(8,128)S(1)} %fusion.18.q_ref.k_ref.v_ref, ...), custom_call_target="tpu_custom_call" | custom-call | tf_op jit(solution)/shard_map/attend/pallas_call | solution.py:749
  271.2 0.8 copy-done
  273.5 3.1 multiply_reduce_fusion.2
  276.6 1.5 copy-done.8
  278.1 1.3 multiply_convert_fusion.1.x
  279.4 119.1 %mlp_all.1 = (bf16[4,320,2048]{2,1,0:T(8,128)(2,1)}, bf16[4,320,1408]{2,1,0:T(8,128)(2,1)}, bf16[4,320,2816]{2,1,0:T(8,128)(2,1)}, bf16[4,320,2048]{2,1,0:T(8,128)(2,1)}, bf16[4,320,2048]{2,1,0:T(8,128)(2,1)}) custom-call(bf16[320,2048]{1,0:T(8,128)(2,1)} %multiply_convert_fusion.1.x, bf16[4,320,2048]{2,1,0:T(8,128)(2,1)} %get-tuple-element.60.gy, ...), custom_call_target="tpu_custom_call" | custom-call | flops 44291850240 | bytes 62914560 | tf_op jit(solution)/shard_map/mlp_all/pallas_call | solution.py:654
  398.5 13.6 %bitcast_convert_fusion.1 = bf16[2048,1408]{1,0:T(8,128)(2,1)} fusion(bf16[4,320,2048]{2,1,0:T(8,128)(2,1)} %get-tuple-element.60.gy, bf16[4,320,1408]{2,1,0:T(8,128)(2,1)} %get-tuple-element.72), kind=kOutput, calls=%fused_computation.4 | convolution fusion | flops 7384858624 | bytes 14614528 | tf_op jit(solution)/shard_map/dot_general | solution.py:903
  412.1 18.7 %bitcast_convert_fusion = bf16[2048,2816]{1,0:T(8,128)(2,1)} fusion(bf16[4,320,2048]{2,1,0:T(8,128)(2,1)S(1)} %copy-done.23, bf16[4,320,2816]{2,1,0:T(8,128)(2,1)S(1)} %copy-done.22), kind=kOutput, calls=%fused_computation | convolution fusion | flops 14769717248 | bytes 23986176 | tf_op jit(solution)/shard_map/dot_general | solution.py:903
  430.7 13.9 %core_exchange.1 = (bf16[4,4,64,1408]{3,2,1,0:T(8,128)(2,1)}, bf16[4,4,64,2816]{3,2,1,0:T(8,128)(2,1)}) custom-call(bf16[4,2,4,64,1408]{4,3,2,1,0:T(8,128)(2,1)} %bitcast.61, bf16[4,2,4,64,2816]{4,3,2,1,0:T(8,128)(2,1)} %bitcast.59), custom_call_target="tpu_custom_call" | custom-call | tf_op jit(solution)/shard_map/core_exchange/pallas_call | solution.py:571
  444.7 5.3 fusion.1
  450.0 6.8 fusion
  456.8 7.9 maximum_bitcast_fusion
  465.0 60.3 %exchange.2 = bf16[4,320,2048]{2,1,0:T(8,128)(2,1)} custom-call(bf16[4,320,2048]{2,1,0:T(8,128)(2,1)} %get-tuple-element.63.src), custom_call_target="tpu_custom_call" | custom-call | tf_op jit(solution)/shard_map/exchange/pallas_call | solution.py:544
  525.2 4.0 convert_reduce_fusion
  530.1 1.9 copy-done.10
  532.0 1.0 convert_reduce_fusion.1
  533.3 2.2 multiply_add_fusion
  535.5 1.5 copy-done.11
  537.0 6.9 convolution_convert_fusion.1
  543.9 12.3 %copy.46 = bf16[2048,2048]{1,0:T(8,128)(2,1)} copy(bf16[2048,2048]{0,1:T(8,128)(2,1)} %convolution_convert_fusion.1) | data formatting | bytes 16777216 | tf_op jit(solution)/shard_map/convert.10
  556.2 7.2 convolution_convert_fusion.2.gc_ref
  563.4 25.0 %attend_back.1 = (bf16[320,2048]{1,0:T(8,128)(2,1)S(1)}, f32[320,256]{1,0:T(8,128)S(1)}, f32[320,256]{1,0:T(8,128)S(1)}) custom-call(bf16[320,2048]{1,0:T(8,128)(2,1)S(1)} %get-tuple-element.65.q_ref, bf16[4,320,128]{2,1,0:T(8,128)(2,1)S(1)} %copy-done.3, bf16[4,320,128]{2,1,0:T(8,128)(2,1)S(1)} %copy-done.5, f32[4,320,128]{2,1,0:T(8,128)S(1)} %copy-done.1, ...), custom_call_target="tpu_custom_call" | custom-call | tf_op jit(solution)/shard_map/attend_back/pallas_call | solution.py:822
  588.5 6.5 convolution_convert_fusion
  595.1 11.6 %pad_maximum_fusion = bf16[2048,4608]{1,0:T(8,128)(2,1)} fusion(bf16[2048,2560]{1,0:T(8,128)(2,1)S(1)} %convolution_convert_fusion, bf16[2048,2048]{1,0:T(8,128)(2,1)S(1)} %bitcast.58), kind=kLoop, calls=%fused_computation.1 | loop fusion | flops 37748736 | bytes 37748736 | tf_op jit(solution)/shard_map/concatenate | solution.py:918
  606.7 1.3 copy-done.15
  608.0 9.2 %fusion.11 = (f32[2048]{0:T(1024)S(1)}, f32[320]{0:T(512)S(1)}, f32[320,2048]{1,0:T(8,128)}) fusion(bf16[320,2048]{1,0:T(8,128)(2,1)S(1)} %copy-done.15, f32[320]{0:T(512)S(1)} %add_rsqrt_fusion.1, f32[2048]{0:T(1024)S(1)} %get-tuple-element.84, bf16[2048,2560]{1,0:T(8,128)(2,1)} %get-tuple-element.57, bf16[320,256]{1,0:T(8,128)(2,1)S(1)} %convert_element_type.130, ...), kind=kOutput, calls=%fused_computation.28 | convolution fusion | flops 3364943616 | bytes 16075264 | tf_op jit(solution)/shard_map/dot_general | solution.py:898
  617.1 37.6 %all-reduce.3 = (f32[2048]{0:T(1024)S(1)}, f32[2048]{0:T(1024)S(1)}) all-reduce(f32[2048]{0:T(1024)S(1)} %get-tuple-element.79, f32[2048]{0:T(1024)S(1)} %get-tuple-element.77), channel_id=2, replica_groups=mesh['wide'=8,'narrow'=4] {'wide','narrow'}, use_global_device_ids=true, to_apply=%region_9.10.clone | all-reduce | flops 4096 | bytes 32768
  655.9 5.2 fusion.10
  661.1 33.4 %exchange.3 = bf16[4,64,4224]{2,1,0:T(8,128)(2,1)} custom-call(bf16[4,64,4224]{2,1,0:T(8,128)(2,1)} %bitcast.65), custom_call_target="tpu_custom_call" | custom-call | tf_op jit(solution)/shard_map/exchange/pallas_call | solution.py:544
  694.5 1.6 convert_bitcast_fusion
  696.1 3.4 copy.51
  699.5 4.1 reshape.168
  703.6 7.7 slice_reduce_fusion
  711.3 1.5 copy.68
  712.8 1.5 copy.69
  714.4 1.2 convert_bitcast_fusion.1
  715.6 1.2 copy.55
  716.8 111.5 %reduce-scatter.3.cloned.1.call-done = bf16[64,4608]{1,0:T(8,128)(2,1)} async-done(((bf16[2048,4608]{1,0:T(8,128)(2,1)}), bf16[64,4608]{1,0:T(8,128)(2,1)}) %reduce-scatter.3.cloned.1.call-update) | async-done | bytes 589840 | tf_op jit(solution)/shard_map/reduce_scatter | solution.py:919
  828.3 2.1 fusion.26
  830.4 1.4 fusion.27
  (86 shorter events, 9.3 us)
Async XLA Ops:
  7.2 653.9 %reduce-scatter.5.cloned.1.call-start = ((), (), s32[]{:S(2)}) async-start(), calls=%async_computation.3 | async-start | bytes 10813440 | tf_op jit(solution)/shard_map/reduce_scatter | solution.py:912
  12.4 3.5 copy-start.20
  12.4 4.3 copy-start.21
  12.4 5.0 copy-start.16
  18.8 221.3 %copy-start.13 = (bf16[320,2048]{1,0:T(8,128)(2,1)S(1)}, bf16[320,2048]{1,0:T(8,128)(2,1)}, u32[]{:S(2)}) copy-start(bf16[320,2048]{1,0:T(8,128)(2,1)} %param.17) | copy-start | bytes 3932164
  18.9 0.6 copy-start.18
  19.5 220.9 %copy-start.19 = (s32[320]{0:T(512)S(1)}, s32[320]{0:T(512)}, u32[]{:S(2)}) copy-start(s32[320]{0:T(512)} %param.20) | copy-start | bytes 3844
  241.4 32.1 %slice-start.2 = ((s8[8388608]{0:T(1024)(128)(4,1)}), s8[4194304]{0:T(1024)(128)(4,1)S(1)}, s32[]{:S(2)}) async-start(s8[8388608]{0:T(1024)(128)(4,1)} %bitcast.70), calls=%async_computation.6 | async-start | bytes 8388608
  241.6 31.9 %slice-start.3 = ((s8[8388608]{0:T(1024)(128)(4,1)}), s8[4194304]{0:T(1024)(128)(4,1)S(1)}, s32[]{:S(2)}) async-start(s8[8388608]{0:T(1024)(128)(4,1)} %bitcast.70), calls=%async_computation.7 | async-start | bytes 8388608
  271.2 0.8 copy-start
  272.1 0.7 copy-start.2
  272.8 0.7 copy-start.4
  273.5 3.1 copy-start.6
  276.6 1.5 copy-start.8
  398.5 13.6 %copy-start.22 = (bf16[4,320,2816]{2,1,0:T(8,128)(2,1)S(1)}, bf16[4,320,2816]{2,1,0:T(8,128)(2,1)}, u32[]{:S(2)}) copy-start(bf16[4,320,2816]{2,1,0:T(8,128)(2,1)} %get-tuple-element.74) | copy-start | bytes 21626884
  398.5 13.6 %copy-start.23 = (bf16[4,320,2048]{2,1,0:T(8,128)(2,1)S(1)}, bf16[4,320,2048]{2,1,0:T(8,128)(2,1)}, u32[]{:S(2)}) copy-start(bf16[4,320,2048]{2,1,0:T(8,128)(2,1)} %get-tuple-element.73) | copy-start | bytes 15728644
  444.7 5.3 copy-start.12
  464.8 363.5 %reduce-scatter.3.cloned.1.call-start = ((), (), s32[]{:S(2)}) async-start(), calls=%async_computation.2 | async-start | bytes 19464192 | tf_op jit(solution)/shard_map/reduce_scatter | solution.py:919
  525.2 4.0 copy-start.9
  529.3 2.7 copy-start.10
  532.0 1.3 copy-start.17
  533.3 3.7 copy-start.7
  535.5 1.5 copy-start.11
  556.2 7.2 copy-start.1
  556.2 7.2 copy-start.3
  556.2 7.2 copy-start.5
  563.4 25.1 %copy-start.14 = (bf16[320,2048]{1,0:T(8,128)(2,1)S(1)}, bf16[320,2048]{1,0:T(8,128)(2,1)}, u32[]{:S(2)}) copy-start(bf16[320,2048]{1,0:T(8,128)(2,1)} %param.17) | copy-start | bytes 3932164
  588.5 6.6 slice-start
  588.5 6.5 slice-start.1
  606.7 1.3 copy-start.15
Sparse Core Ops, SparseCore 0:
  464.9 147.1 reduce-scatter.4
  618.5 209.7 reduce-scatter.2

commit v3 on v2

--- a/solution.py
+++ b/solution.py
@@ -528,63 +528,16 @@
         name="gather_all",
     )(wq, wk, wv, wo, gains, wgu, wd, gy)
 
-def exchange_kernel(by_chip, src, dst, loc, s_s, s_r):
+def mlp_kernel(nz, x, gy, gu_hbm, gd_hbm, gx_parts, mlp_parts, sums,
+               xs, gys, gu, gd, mix, ggu, gx, mo, xt, load, ag_s, ag_r, rs_s, rs_r, own, out, core_s, core_r, ready, done):
     c, k, n = place()
-    hello([(None, chip_at(c, r), k, n) for r in (1, 2, 3)])
-    cps = [pltpu.make_async_copy(src.at[c if by_chip else 0], dst.at[c if by_chip else 0], loc)]
-    for r in (1, 2, 3):
-        cc = chip_at(c, r)
-        cps.append(remote(src.at[cc if by_chip else r], dst.at[c if by_chip else r], s_s.at[r - 1], s_r.at[r - 1], cc, k, n))
-    for cp in cps: cp.start()
-    for cp in cps: cp.wait()
-
-
-def exchange(x, cid, by_chip=False):
-    dma = pltpu.SemaphoreType.DMA
-    return pl.pallas_call(
-        functools.partial(exchange_kernel, by_chip),
-        out_shape=jax.ShapeDtypeStruct(x.shape, x.dtype), in_specs=[ANY], out_specs=ANY,
-        scratch_shapes=[dma, dma((3,)), dma((3,))],
-        compiler_params=pltpu.CompilerParams(collective_id=cid, has_side_effects=True),
-        name="exchange",
-    )(x)
-
-
-def plane_swap(x, cid):
-    return exchange(x, cid, True)
-
-
-def core_kernel(srcs, *refs):
-    src, dst = refs[:srcs], refs[srcs : 2 * srcs]
-    s_s, s_r = refs[2 * srcs :]
-    c, k, n = place()
-    hello([(None, c, 1 - k, n)])
-    cps = []
-    for m in range(srcs):
-        cp = remote(src[m].at[:, 1 - k], dst[m], s_s.at[m], s_r.at[m], c, 1 - k, n)
-        cp.start(); cps.append(cp)
-    for cp in cps: cp.wait()
-
-def core_exchange(xs, cid):
-    dma = pltpu.SemaphoreType.DMA
-    m = len(xs)
-    return pl.pallas_call(
-        functools.partial(core_kernel, m),
-        out_shape=tuple(jax.ShapeDtypeStruct((x.shape[0],) + x.shape[2:], x.dtype) for x in xs),
-        in_specs=[ANY] * m, out_specs=(ANY,) * m,
-        scratch_shapes=[dma((m,)), dma((m,))],
-        compiler_params=pltpu.CompilerParams(collective_id=cid, has_side_effects=True),
-        name="core_exchange",
-    )(*xs)
-
-
-def mlp_kernel(x, gy, gu_hbm, gd_hbm, x_all, mix_all, ggu_all, gx_parts, mlp_parts,
-               xs, gys, gu, gd, mix, ggu, gx, mo, load, ag_s, ag_r, rs_s, rs_r, own, out):
-    c, k, n = place()
+    f32, bf16 = jnp.float32, jnp.bfloat16
     slots, width = x.shape
     half = slots // 2
-    cols = gd.shape[-1]
-    hello([(None, chip_at(c, r), k, n) for r in (1, 2, 3)])
+    rows, cols = gd.shape[1:]
+    per_tile = nz
+    tile = nz * rows
+    hello([(None, chip_at(c, r), k, n) for r in (1, 2, 3)] + [(None, c, 1 - k, n)])
     loads = [pltpu.make_async_copy(x, xs.at[0], load.at[0])]
     sends = [remote(x, xs.at[r], ag_s.at[r], ag_r.at[r], chip_at(c, r), k, n) for r in (1, 2)]
     for cp in sends: cp.start()
@@ -595,6 +548,14 @@
               remote(xs.at[2, pl.ds(half, half)], xs.at[3, pl.ds(half, half)], ag_s.at[3], ag_r.at[3], chip_at(c, 1), k, n)]
     for cp in loads: cp.wait()
 
+    def columns(ref, at, size):
+        t = ref[:, :, pl.ds(at, size)]
+        return t.reshape(t.shape[0] * t.shape[1], size)
+
+    def some_rows(ref, i):
+        t = ref[pl.ds(i * (256 // rows), 256 // rows)]
+        return t.reshape(256, t.shape[2])
+
     def block(r, carry):
         @pl.when(r == 1)
         def _():
@@ -604,15 +565,15 @@
         def _():
             for cp in relays: cp.wait_recv()
         def chunk(col, w):
-            h = jnp.dot(xs[r], gu[:, pl.ds(2 * col, 2 * w)], preferred_element_type=jnp.float32)
-            gm = jnp.dot(gys[r], gd[:, pl.ds(col, w)], preferred_element_type=jnp.float32)
+            h = jnp.dot(xs[r], columns(gu, 2 * col, 2 * w), preferred_element_type=f32)
+            gm = jnp.dot(gys[r], columns(gd, col, w), preferred_element_type=f32)
             for q in range(w // 128):
                 gate, up, g = h[:, 256 * q : 256 * q + 128], h[:, 256 * q + 128 : 256 * q + 256], gm[:, 128 * q : 128 * q + 128]
                 sg = 1.0 / (1.0 + jnp.exp(-gate))
                 act = gate * sg
-                mix[r, :, pl.ds(col + 128 * q, 128)] = (act * up).astype(jnp.bfloat16)
-                ggu[r, :, pl.ds(2 * col + 256 * q, 128)] = (g * up * (sg * (1.0 + gate * (1.0 - sg)))).astype(jnp.bfloat16)
-                ggu[r, :, pl.ds(2 * col + 256 * q + 128, 128)] = (g * act).astype(jnp.bfloat16)
+                mix[r, :, pl.ds(col + 128 * q, 128)] = (act * up).astype(bf16)
+                ggu[r, :, pl.ds(2 * col + 256 * q, 128)] = (g * up * (sg * (1.0 + gate * (1.0 - sg)))).astype(bf16)
+                ggu[r, :, pl.ds(2 * col + 256 * q + 128, 128)] = (g * act).astype(bf16)
         def pair(j, carry):
             chunk(pl.multiple_of(j * 256, 256), 256)
             return carry
@@ -620,7 +581,7 @@
         if cols % 256: chunk(cols - 128, 128)
         def back(i, carry):
             at = pl.ds(pl.multiple_of(i * 256, 256), 256)
-            gx[r, :, at] = lax.dot_general(ggu[r], gu[at, :], contract_last, preferred_element_type=jnp.float32).astype(jnp.bfloat16)
+            gx[r, :, at] = lax.dot_general(ggu[r], some_rows(gu, i), contract_last, preferred_element_type=f32).astype(bf16)
             return carry
         lax.fori_loop(0, width // 256, back, 0)
         @pl.when(r == 0)
@@ -629,35 +590,85 @@
         def _(): remote(gx.at[r], gx_parts.at[r], rs_s.at[r], rs_r.at[r], chip_at(c, r), k, n).start()
         def down(i, carry):
             at = pl.ds(pl.multiple_of(i * 256, 256), 256)
-            mo[r, :, at] = lax.dot_general(mix[r], gd[at, :], contract_last, preferred_element_type=jnp.float32).astype(jnp.bfloat16)
+            mo[r, :, at] = lax.dot_general(mix[r], some_rows(gd, i), contract_last, preferred_element_type=f32).astype(bf16)
             return carry
         lax.fori_loop(0, width // 256, down, 0)
-        for i, (a, b) in enumerate(((xs, x_all), (mix, mix_all), (ggu, ggu_all), (mo, mlp_parts))):
-            pltpu.make_async_copy(a.at[r], b.at[r], out.at[i, r]).start()
+        pltpu.make_async_copy(mo.at[r], mlp_parts.at[r], out.at[r]).start()
         return carry
     lax.fori_loop(0, CHIPS, block, 0)
+
+    pl.semaphore_signal(ready, inc=1, device_id={"wide": c * CORES + 1 - k, "narrow": n}, device_id_type=MESH)
+    pl.semaphore_wait(ready, 1)
+    sent, came = 0, CHIPS * per_tile
+
+    def terms(t, kk, put):
+        at = pl.ds(pl.multiple_of((t * CORES + kk) * tile, 128), tile)
+        for src, right, ref in ((xs, ggu, gu), (gys, mix, gd)):
+            total = ref.shape[-1]
+            for r in range(CHIPS):
+                xt[:, r * slots : (r + 1) * slots] = src[r, :, at].T
+            def one(col, w):
+                b = right[:, :, pl.ds(col, w)].reshape(CHIPS * slots, w)
+                put(ref, t, col, w, jnp.dot(xt[...], b, preferred_element_type=f32))
+            def step(j, carry):
+                one(pl.multiple_of(j * 256, 256), 256)
+                return carry
+            lax.fori_loop(0, total // 256, step, 0)
+            if total % 256: one(total - 128, 128)
+
+    def to_core(ref, i, t):
+        return remote(ref.at[pl.ds(sent + t * per_tile, per_tile)], ref.at[pl.ds(came + t * per_tile, per_tile)],
+                      core_s.at[i, t], core_r.at[i, t], c, 1 - k, n)
+
+    def to_sums(ref, i, t):
+        first = 0 if i == 0 else cols
+        return pltpu.make_async_copy(ref.at[pl.ds(came + t * per_tile, per_tile)],
+                                     sums.at[:, t, :, pl.ds(first, ref.shape[-1])], done.at[i, t])
+
+    def theirs(t, carry):
+        def put(ref, t, col, w, v):
+            ref[pl.ds(sent + t * per_tile, per_tile), :, pl.ds(col, w)] = v.astype(bf16).reshape(per_tile, rows, w)
+        terms(t, 1 - k, put)
+        for i, ref in enumerate((gd, gu)): to_core(ref, i, t).start()
+        return carry
+    lax.fori_loop(0, CHIPS, theirs, 0)
+
+    def ours(t, carry):
+        for i, ref in enumerate((gd, gu)): to_core(ref, i, t).wait_recv()
+        def put(ref, t, col, w, v):
+            here = (pl.ds(came + t * per_tile, per_tile), slice(None), pl.ds(col, w))
+            ref[here] = (ref[here].astype(f32) + v.reshape(per_tile, rows, w)).astype(bf16)
+        terms(t, k, put)
+        for i, ref in enumerate((gd, gu)): to_sums(ref, i, t).start()
+        return carry
+    lax.fori_loop(0, CHIPS, ours, 0)
+
     for cp in sends + relays: cp.wait_send()
     pltpu.make_async_copy(gx.at[0], gx_parts.at[0], own).wait()
     for r in range(CHIPS):
-        for i, (a, b) in enumerate(((xs, x_all), (mix, mix_all), (ggu, ggu_all), (mo, mlp_parts))):
-            pltpu.make_async_copy(a.at[r], b.at[r], out.at[i, r]).wait()
+        pltpu.make_async_copy(mo.at[r], mlp_parts.at[r], out.at[r]).wait()
+    for t in range(CHIPS):
+        for i, ref in enumerate((gd, gu)):
+            to_core(ref, i, t).wait_send()
+            to_sums(ref, i, t).wait()
     for r in (1, 2, 3):
         remote(gx.at[r], gx_parts.at[r], rs_s.at[r], rs_r.at[r], chip_at(c, r), k, n).wait()
 
 
-def mlp_all(x, gy, gu, gd):
+def mlp_all(nz, x, gy, gu, gd):
     slots, width = x.shape
-    cols = gd.shape[1]
+    rows, cols = gd.shape[1:]
     bf, dma, vm = jnp.bfloat16, pltpu.SemaphoreType.DMA, pltpu.VMEM
     def blocks(w): return jax.ShapeDtypeStruct((CHIPS, slots, w), bf)
-    flops = 2 * 6 * CHIPS * slots * width * cols
+    flops = 2 * 9 * CHIPS * slots * width * cols
     return pl.pallas_call(
-        mlp_kernel,
-        out_shape=(blocks(width), blocks(cols), blocks(2 * cols), blocks(width), blocks(width)),
-        in_specs=[ANY] * 4, out_specs=(ANY,) * 5,
-        scratch_shapes=[vm((CHIPS, slots, width), bf), vm((CHIPS, slots, width), bf), vm((width, 2 * cols), bf), vm((width, cols), bf),
+        functools.partial(mlp_kernel, nz),
+        out_shape=(blocks(width), blocks(width), jax.ShapeDtypeStruct((nz, CHIPS, rows, 3 * cols), bf)),
+        in_specs=[ANY] * 4, out_specs=(ANY,) * 3,
+        scratch_shapes=[vm((CHIPS, slots, width), bf), vm((CHIPS, slots, width), bf), vm(gu.shape, bf), vm(gd.shape, bf),
                         vm((CHIPS, slots, cols), bf), vm((CHIPS, slots, 2 * cols), bf), vm((CHIPS, slots, width), bf),
-                        vm((CHIPS, slots, width), bf), dma((4,)), dma((4,)), dma((4,)), dma((4,)), dma((4,)), dma, dma((4, 4))],
+                        vm((CHIPS, slots, width), bf), vm((nz * rows, CHIPS * slots), bf), dma((4,)), dma((4,)), dma((4,)), dma((4,)), dma((4,)),
+                        dma, dma((4,)), dma((2, 4)), dma((2, 4)), pltpu.SemaphoreType.REGULAR, dma((2, 4))],
         compiler_params=pltpu.CompilerParams(collective_id=1, has_side_effects=True, vmem_limit_bytes=62 << 20),
         cost_estimate=pl.CostEstimate(flops=flops, bytes_accessed=60 << 20, transcendentals=CHIPS * slots * cols),
         name="mlp_all",
@@ -762,8 +773,16 @@
     )(qkv, qkv, qkv, tables)
 
 
-def attend_back_kernel(q_ref, k_ref, v_ref, lse_ref, gc_ref, tab_ref, gq_ref, gk_ref, gv_ref, ks, kt, vt, ds, pr, qs, gs):
+def attend_back_kernel(q_ref, k_ref, v_ref, lse_ref, gc_ref, tab_ref, part, gq_ref, gk_ref, gv_ref, parts,
+                       ks, kt, vt, ds, pr, qs, gs, loc, s_s, s_r):
     g = pl.program_id(0)
+    c, k, n = place()
+    copies = [pltpu.make_async_copy(part.at[0], parts.at[0], loc)]
+    copies += [remote(part.at[r], parts.at[r], s_s.at[r - 1], s_r.at[r - 1], chip_at(c, r), k, n) for r in (1, 2, 3)]
+    @pl.when(g == 0)
+    def _():
+        hello([(None, chip_at(c, r), k, n) for r in (1, 2, 3)])
+        for cp in copies: cp.start()
     f32, bf16 = jnp.float32, jnp.bfloat16
     slots = q_ref.shape[0]
     scale = HEAD_SIZE ** -0.5
@@ -808,9 +827,12 @@
         def _(): out[...] = x
         @pl.when(g % 2 == 1)
         def _(): out[...] = jnp.where(lane < HEAD_SIZE, out[...], pltpu.roll(x, HEAD_SIZE, 1))
-
-
-def attend_back_all(q, k, v, lse, grad_context, tables):
+    @pl.when(g == KEY_VALUE_HEADS - 1)
+    def _():
+        for cp in copies: cp.wait()
+
+
+def attend_back_all(q, k, v, lse, grad_context, tables, part):
     slots = q.shape[0]
     wide = REPEAT * HEAD_SIZE
     bf16, f32, vm = jnp.bfloat16, jnp.float32, pltpu.VMEM
@@ -823,13 +845,135 @@
         attend_back_kernel,
         grid=(KEY_VALUE_HEADS,),
         out_shape=(shape((slots, QUERY_HEADS * HEAD_SIZE), bf16), shape((slots, KEY_VALUE_HEADS * HEAD_SIZE), f32),
-                   shape((slots, KEY_VALUE_HEADS * HEAD_SIZE), f32)),
-        in_specs=[wide_spec, per_head, per_head, per_head, wide_spec, pl.BlockSpec((3, slots, PAIR), lambda g: (0, 0, 0))],
-        out_specs=(wide_spec, two, two),
-        scratch_shapes=[vm((2, keys, PAIR), bf16)] * 3 + [vm((2, PAIRS * slots, keys), bf16)] * 2 + [vm((PAIRS * slots, PAIR), bf16)] * 2,
-        compiler_params=pltpu.CompilerParams(vmem_limit_bytes=40 << 20),
+                   shape((slots, KEY_VALUE_HEADS * HEAD_SIZE), f32), shape(part.shape, part.dtype)),
+        in_specs=[wide_spec, per_head, per_head, per_head, wide_spec, pl.BlockSpec((3, slots, PAIR), lambda g: (0, 0, 0)), ANY],
+        out_specs=(wide_spec, two, two, ANY),
+        scratch_shapes=[vm((2, keys, PAIR), bf16)] * 3 + [vm((2, PAIRS * slots, keys), bf16)] * 2 + [vm((PAIRS * slots, PAIR), bf16)] * 2
+        + [pltpu.SemaphoreType.DMA, pltpu.SemaphoreType.DMA((3,)), pltpu.SemaphoreType.DMA((3,))],
+        compiler_params=pltpu.CompilerParams(collective_id=2, has_side_effects=True, vmem_limit_bytes=40 << 20),
         name="attend_back",
-    )(q, k, v, lse, grad_context, tables)
+    )(q, k, v, lse, grad_context, tables, part)
+
+
+def add_into(dst, *srcs):
+    rows = dst.shape[0]
+    step = 16
+    def body(i, carry):
+        at = pl.ds(pl.multiple_of(i * step, step), step)
+        total = dst[at, :].astype(jnp.float32)
+        for s in srcs: total = total + s[at, :].astype(jnp.float32)
+        dst[at, :] = total.astype(dst.dtype)
+        return carry
+    lax.fori_loop(0, rows // step, body, 0)
+
+
+def reduce_kernel(nz, items, *refs):
+    terms, ff = refs[:items], refs[items]
+    outs, ff_out = refs[items + 1 : 2 * items + 1], refs[2 * items + 1]
+    bufs = refs[2 * items + 2 :]
+    took, away, zbuf = bufs[:items], bufs[items : 2 * items], bufs[2 * items : 3 * items]
+    core_s, core_r, half_s, half_r, main_s, main_r, z_s, z_r, ff_s, ff_r, loc = bufs[3 * items :]
+    c, k, n = place()
+    left, right = n > 0, n < nz - 1
+    cx, cy, cd = (chip_at(c, r) for r in (1, 2, 3))
+    hello([(None, cc, k, n) for cc in (cx, cy, cd)] + [(None, c, 1 - k, n), (left, c, k, n - 1), (right, c, k, n + 1)])
+    rows = ff.shape[1]
+    part = nz * rows
+    half = part // 2
+    top, low = pl.ds(0, half), pl.ds(half, half)
+    def arrive(a, at, size): return zbuf[a].at[pl.ds(at, size)]
+    own = [pltpu.make_async_copy(terms[a].at[:, k], away[a], loc.at[a]) for a in range(items)]
+    swap = [remote(terms[a].at[:, 1 - k], took[a], core_s.at[a], core_r.at[a], c, 1 - k, n) for a in range(items)]
+    for cp in own + swap: cp.start()
+    cross = [[remote(away[a].at[cd, top], arrive(a, 2 * part, half), half_s.at[a, 0], half_r.at[a, 0], cx, k, n),
+              remote(away[a].at[cd, low], arrive(a, 2 * part + half, half), half_s.at[a, 1], half_r.at[a, 1], cy, k, n)]
+             for a in range(items)]
+    main = [[remote(away[a].at[cx, top], arrive(a, 0, half), main_s.at[a, 0], main_r.at[a, 0], cx, k, n),
+             remote(away[a].at[cy, low], arrive(a, part + half, half), main_s.at[a, 1], main_r.at[a, 1], cy, k, n),
+             remote(away[a].at[cx, low], arrive(a, half, half), main_s.at[a, 2], main_r.at[a, 2], cx, k, n),
+             remote(away[a].at[cy, top], arrive(a, part, half), main_s.at[a, 3], main_r.at[a, 3], cy, k, n)]
+            for a in range(items)]
+
+    def cores(a):
+        own[a].wait()
+        swap[a].wait_recv()
+        add_into(away[a].at[cd], took[a].at[cd])
+        for cp in cross[a]: cp.start()
+        for cc in (cx, cy, c): add_into(away[a].at[cc], took[a].at[cc])
+
+    def relay(a):
+        cross[a][0].wait_recv()
+        add_into(away[a].at[cy, top], arrive(a, 2 * part, half))
+        main[a][3].start()
+        cross[a][1].wait_recv()
+        add_into(away[a].at[cx, low], arrive(a, 2 * part + half, half))
+        for i in (2, 0, 1): main[a][i].start()
+
+    def mine(a):
+        for cp in main[a]: cp.wait_recv()
+        add_into(away[a].at[c], arrive(a, 0, part), arrive(a, part, part))
+
+    def slot(a, way, j): return arrive(a, pl.multiple_of(2 * part + 2 * half + (way * nz + j) * rows, rows), rows)
+    def piece(a, j): return away[a].at[c, pl.ds(pl.multiple_of(j * rows, rows), rows)]
+    def hop(a, way, j):
+        return remote(piece(a, j), slot(a, way, j), z_s.at[a, way, j], z_r.at[a, way, j], c, k, n + 1 if way == 0 else n - 1)
+
+    def along(some):
+        for t in range(nz):
+            for way in range(2):
+                hops = n if way == 0 else nz - 1 - n
+                j = jnp.clip(n + nz - 1 - t if way == 0 else t - hops, 0, nz - 1)
+                for a in some:
+                    @pl.when((hops > 0) & (t >= hops))
+                    def _():
+                        hop(a, way, j).wait_recv()
+                        add_into(piece(a, j), slot(a, way, j))
+                    @pl.when((t >= hops) & (j != n))
+                    def _(): hop(a, way, j).start()
+        done = [pltpu.make_async_copy(piece(a, n), outs[a], loc.at[a]) for a in some]
+        for cp in done: cp.start()
+        return done
+
+    stores = []
+    for a in range(items): cores(a)
+    for a in range(items): relay(a)
+    mine(0)
+    stores += along([0])
+    for a in range(1, items): mine(a)
+    swaps = [pltpu.make_async_copy(ff.at[c], ff_out.at[c], loc.at[items])]
+    for r, cc in enumerate((cx, cy, cd)):
+        swaps.append(remote(ff.at[cc], ff_out.at[c], ff_s.at[r], ff_r.at[r], cc, k, n))
+    for cp in swaps: cp.start()
+    stores += along(list(range(1, items)))
+    for cp in stores: cp.wait()
+    for cp in swaps: cp.wait()
+    for a in range(items):
+        swap[a].wait_send()
+        for cp in cross[a] + main[a]: cp.wait_send()
+        for j in range(nz):
+            for way in range(2):
+                @pl.when(n < j if way == 0 else n > j)
+                def _(): hop(a, way, j).wait_send()
+
+
+def reduce_all(nz, terms, ff, cid):
+    dma, vm = pltpu.SemaphoreType.DMA, pltpu.VMEM
+    m = len(terms)
+    rows = ff.shape[1]
+    part = nz * rows
+    shape = jax.ShapeDtypeStruct
+    terms = [t.reshape(CHIPS, CORES, part, t.shape[-1]) for t in terms]
+    blocks = [vm((CHIPS, part, t.shape[-1]), t.dtype) for t in terms]
+    return pl.pallas_call(
+        functools.partial(reduce_kernel, nz, m),
+        out_shape=tuple(shape((rows, t.shape[-1]), t.dtype) for t in terms) + (shape(ff.shape, ff.dtype),),
+        in_specs=[ANY] * (m + 1), out_specs=(ANY,) * (m + 1),
+        scratch_shapes=blocks + blocks + [vm((3 * part + 2 * nz * rows, t.shape[-1]), t.dtype) for t in terms]
+        + [dma((m,)), dma((m,)), dma((m, 2)), dma((m, 2)), dma((m, 4)), dma((m, 4)), dma((m, 2, nz)), dma((m, 2, nz)),
+           dma((3,)), dma((3,)), dma((m + 1,))],
+        compiler_params=pltpu.CompilerParams(collective_id=cid, has_side_effects=True, vmem_limit_bytes=60 << 20),
+        name="reduce_all",
+    )(*terms, ff)
 
 
 def fits(mesh):
@@ -869,7 +1013,7 @@
     w_qkv, w_out, gain_cols, ff_gate_up, ff_down, gy_all = gather_all(
         nz, w_query, w_key, w_value, w_output, gains, w_gate_up, w_down, grad_y_low
     )
-    ff_gate_up, ff_down = ff_gate_up.reshape(width, 2 * cols), ff_down.reshape(width, cols)
+    ff_gate_up, ff_down = (w.reshape(-1, rows, w.shape[-1]) for w in (ff_gate_up, ff_down))
     gain_attn = gain_cols[:, 0].astype(f32)
     gain_mlp = gain_cols[:, 1].astype(f32)
 
@@ -881,19 +1025,16 @@
     normed_mlp = normalize(hidden)
     scaled_mlp = (normed_mlp * gain_mlp).astype(bf16)
 
-    x_all, mixed, grad_gate_up, grad_x_parts, mlp_part = mlp_all(scaled_mlp, gy_all, ff_gate_up, ff_down)
-    x_all, mixed, grad_gate_up, gy_all = (t.reshape(CHIPS * slots, -1) for t in (x_all, mixed, grad_gate_up, gy_all))
-    mlp_parts = exchange(mlp_part, 3)
-    output = (valid_rows * (hidden + jnp.sum(mlp_parts.astype(f32), axis=0))).astype(bf16)
-
+    grad_x_parts, mlp_part, ff_sums = mlp_all(nz, scaled_mlp, gy_all, ff_gate_up, ff_down)
     grad_xn2 = jnp.sum(grad_x_parts.astype(f32), axis=0)
     grad_gain_mlp = jnp.sum(grad_xn2 * normed_mlp, axis=0)
     grad_hidden = grad_y + norm_back(grad_xn2 * gain_mlp, normed_mlp, hidden)
     grad_attn_low = grad_hidden.astype(bf16)
     grad_context = jnp.dot(grad_attn_low, w_out, preferred_element_type=f32).astype(bf16)
-    grad_query, grad_key, grad_value = attend_back_all(
-        query_rotated, key_rotated, value_reduced, log_totals, grad_context, tables
-    )
+    grad_query, grad_key, grad_value, mlp_parts = attend_back_all(
+        query_rotated, key_rotated, value_reduced, log_totals, grad_context, tables, mlp_part
+    )
+    output = (valid_rows * (hidden + jnp.sum(mlp_parts.astype(f32), axis=0))).astype(bf16)
     grad_qkv = jnp.concatenate([grad_query, grad_key.astype(bf16), grad_value.astype(bf16)], 1)
     grad_xn1 = lax.dot_general(grad_qkv, w_qkv, contract_last, preferred_element_type=f32)
     grad_gain_attn = jnp.sum(grad_xn1 * normed_attn, axis=0)
@@ -902,28 +1043,27 @@
     def over_rows(left, right):
         return lax.dot_general(left, right, contract_first, preferred_element_type=f32)
 
-    ff_terms = [
-        over_rows(a, b).astype(bf16).reshape(CHIPS, CORES, nz, rows, -1) for a, b in ((gy_all, mixed), (x_all, grad_gate_up))
-    ]
-    from_core = core_exchange(ff_terms, 4)
-    ff_sums = jnp.concatenate(
-        [lax.dynamic_index_in_dim(t, k, 1, False).astype(f32) + r.astype(f32) for t, r in zip(ff_terms, from_core)], 3
-    ).astype(bf16)
-    ff_sums = lax.psum_scatter(jnp.swapaxes(ff_sums, 0, 1), "narrow", scatter_dimension=0, tiled=True)
-    ff_sums = plane_swap(ff_sums.reshape(CHIPS, rows, 3 * cols), 5)
+    ff_sums = lax.psum_scatter(ff_sums, "narrow", scatter_dimension=0, tiled=True)
+    gain_terms = jnp.zeros((width, 128), f32).at[:, 0].set(grad_gain_attn).at[:, 1].set(grad_gain_mlp)
+    grad_w_output, grad_qkv_rows, gain_sums, ff_sums = reduce_all(
+        nz,
+        [
+            over_rows(grad_attn_low, context).astype(bf16),
+            over_rows(scaled_attn, grad_qkv).astype(bf16),
+            gain_terms.astype(bf16),
+        ],
+        ff_sums.reshape(CHIPS, rows, 3 * cols),
+        3,
+    )
     grad_w_down = jnp.swapaxes(ff_sums[:, :, :cols], 0, 1).reshape(rows, CHIPS * cols).astype(f32)
     grad_gate_up = jnp.swapaxes(ff_sums[:, :, cols:], 0, 1).reshape(rows, CHIPS * cols // 128, 2, 128).astype(f32)
     grad_w_gate = grad_gate_up[:, :, 0].reshape(rows, CHIPS * cols)
     grad_w_up = grad_gate_up[:, :, 1].reshape(rows, CHIPS * cols)
-    attn_terms = jnp.concatenate([over_rows(grad_attn_low, context), over_rows(scaled_attn, grad_qkv)], 1)
-    attn_sums = lax.psum_scatter(attn_terms.astype(bf16), ("wide", "narrow"), scatter_dimension=0, tiled=True).astype(f32)
-    grad_w_output = attn_sums[:, :query_width]
-    grad_w_query = attn_sums[:, query_width : 2 * query_width]
-    grad_w_key = attn_sums[:, 2 * query_width : 2 * query_width + key_width]
-    grad_w_value = attn_sums[:, 2 * query_width + key_width :]
-    grad_norm_attn, grad_norm_mlp = (
-        lax.psum_scatter(g, ("wide", "narrow"), scatter_dimension=0, tiled=True) for g in (grad_gain_attn, grad_gain_mlp)
-    )
+    grad_w_output = grad_w_output.astype(f32)
+    grad_w_query = grad_qkv_rows[:, :query_width].astype(f32)
+    grad_w_key = grad_qkv_rows[:, query_width : query_width + key_width].astype(f32)
+    grad_w_value = grad_qkv_rows[:, query_width + key_width :].astype(f32)
+    grad_norm_attn, grad_norm_mlp = gain_sums[:, 0].astype(f32), gain_sums[:, 1].astype(f32)
     return (
         output,
         grad_tokens,

time: 846 us -> 722 us (0.85)
  waiting for transfers between devices: 112 us -> 37.7 us
  Pallas kernels: 493 us -> 556 us
  blocking collectives: 37.6 us -> 0 us
  matrix products: 71.7 us -> 37.4 us
  other arithmetic: 56.4 us -> 32.8 us
  local copies, waits for them, and re-layouts: 52.8 us -> 36.5 us
    reduce_scatter x2 -> x1, waiting for transfers between devices: 112 us -> 37.7 us  [fast_device(): lax.psum_scatter(ff_sums, 'narrow', scatter_dimension=0, tiled=True)]
    unnamed x1 -> x0, blocking collectives: 37.6 us -> none
    pallas_call x1, Pallas kernels: 25 us -> 61 us  [attend_back_all(): pl.pallas_call(attend_back_kernel, grid=(KEY_VALUE_HEADS,), out_shape=(sh...]
    dot_general x4 -> x2, matrix products: 45.6 us -> 15.5 us  [over_rows(): lax.dot_general(left, right, contract_first, preferred_element_type=f32)]
    pallas_call x4 -> x2, Pallas kernels: 227 us -> 254 us  [the longest x1 136 us: mlp_all(): pl.pallas_call(functools.partial(mlp_kernel, nz), out_shape=(blocks(width...]
    another operation x3 -> x2, local copies, waits for them, and re-layouts: 12.6 us -> 0.23 us
    concatenate x1 -> x0, other arithmetic: 11.6 us -> none  [fast_device(): jnp.concatenate([over_rows(grad_attn_low, context), over_rows(scaled_attn...]
    another operation x6, other arithmetic: 14.7 us -> 5.21 us
  transfers between devices with their start and end apart: 2 -> 1, of which waited for: 1 -> 1; matrix products, arithmetic and copies ran while one was open for 11% -> 6% of each run, Pallas kernels for 14% -> 9%
where the time goes in v3:
time: 722 us; the launch traced here: 716 us
  Pallas kernels  556 us (77%)
  waiting for transfers between devices  37.7 us (5%)
  matrix products  37.4 us (5%)
  local copies, waits for them, and re-layouts  36.5 us (5%)
  other arithmetic  32.8 us (5%)
  between operations  15.4 us (2%)
    pallas_call x1, Pallas kernels, gather_all(): pl.pallas_call(functools.partial(gather_kernel, nz), out_shape=(jax.Shape...  219 us
    pallas_call x1, Pallas kernels, mlp_all(): pl.pallas_call(functools.partial(mlp_kernel, nz), out_shape=(blocks(width...  136 us
    pallas_call x1, Pallas kernels, reduce_all(): pl.pallas_call(functools.partial(reduce_kernel, nz, m), out_shape=tuple((...  118 us
    pallas_call x1, Pallas kernels, attend_back_all(): pl.pallas_call(attend_back_kernel, grid=(KEY_VALUE_HEADS,), out_shape=(sh...  61 us
    reduce_scatter x1, waiting for transfers between devices, fast_device(): lax.psum_scatter(ff_sums, 'narrow', scatter_dimension=0, tiled=True)  37.7 us
    pallas_call x1, Pallas kernels, attend_all(): pl.pallas_call(attend_kernel, grid=(KEY_VALUE_HEADS,), out_shape=(shape((...  22.8 us
    dot_general x2, matrix products, over_rows(): lax.dot_general(left, right, contract_first, preferred_element_type=f32)  15.5 us
  transfers between devices with their start and end apart: 1, of which 1 were waited for; matrix products, arithmetic and copies ran while one was open for 6% of the time, Pallas kernels for 9%

profile of v3, /device:TPU:0, one launch (start us, length us, event | category | flops | bytes accessed | tf_op | source)
XLA Modules:
  0.0 716.2 jit_solution(17505012388151524379)
XLA Ops:
  9.2 0.7 convert_element_type.124
  9.9 1.7 fusion.10
  11.6 1.3 fusion.21
  13.0 1.3 fusion.20
  15.3 1.5 stack_reshape.6
  17.4 1.5 copy.30
  18.8 2.0 reshape.221.wgu
  20.9 1.3 fusion.11.gy
  22.9 218.8 %gather_all.1 = (bf16[2048,2560]{1,0:T(8,128)(2,1)}, bf16[2048,2048]{1,0:T(8,128)(2,1)}, bf16[2048,128]{1,0:T(8,128)(2,1)}, bf16[4,8,64,2816]{3,2,1,0:T(8,128)(2...) custom-call(bf16[64,2048]{1,0:T(8,128)(2,1)} %wq.1, bf16[64,256]{1,0:T(8,128)(2,1)} %wk.1, ...), custom_call_target="tpu_custom_call" | custom-call | tf_op jit(solution)/shard_map/gather_all/pallas_call | solution.py:520
  241.7 1.8 convert_reduce_fusion.2
  243.9 6.7 fusion.16.q_ref.k_ref.v_ref
  250.6 22.8 %attend.1 = (bf16[320,2048]{1,0:T(8,128)(2,1)S(1)}, bf16[4,320,128]{2,1,0:T(8,128)(2,1)S(1)}, bf16[4,320,128]{2,1,0:T(8,128)(2,1)S(1)}, f32[4,320,128]{2,1,0:T(8,128)S(1)}, bf16[320,2048]{1,0:T(8,128)(2,1)S(1)}) custom-call(f32[320,2560]{1,0:T(8,128)S(1)} %fusion.16.q_ref.k_ref.v_ref, f32[320,2560]{1,0:T(8,128)S(1)} %fusion.16.q_ref.k_ref.v_ref, ...), custom_call_target="tpu_custom_call" | custom-call | tf_op jit(solution)/shard_map/attend/pallas_call | solution.py:760
  273.4 0.8 copy-done.1
  274.2 0.7 copy-done.3
  275.0 0.7 copy-done.5
  275.7 3.1 multiply_reduce_fusion.2
  278.8 1.5 copy-done.9
  280.3 1.3 multiply_convert_fusion.1.x
  281.7 135.8 %mlp_all.1 = (bf16[4,320,2048]{2,1,0:T(8,128)(2,1)}, bf16[4,320,2048]{2,1,0:T(8,128)(2,1)}, bf16[4,4,64,4224]{3,2,1,0:T(8,128)(2,1)}) custom-call(bf16[320,2048]{1,0:T(8,128)(2,1)} %multiply_convert_fusion.1.x, bf16[4,320,2048]{2,1,0:T(8,128)(2,1)} %get-tuple-element.89.gy, bf16[32,64,2816]{2,1,0:T(8,128)(2,1)} %bitcast.51, bf16[32,64,1408]{2,1,0:T(8,128)(2,1)} %bitcast.56), custom_call_target="tpu_custom_call" | custom-call | flops 66437775360 | bytes 62914560 | tf_op jit(solution)/shard_map/mlp_all/pallas_call | solution.py:664
  417.5 4.0 convert_reduce_fusion.1
  421.6 0.8 multiply_reduce_fusion
  422.4 0.9 copy-done.18
  423.3 0.8 multiply_add_fusion
  424.1 0.8 slice-done.3
  425.0 2.9 convolution_convert_fusion.2.gc_ref
  427.9 61.0 %attend_back.1 = (bf16[320,2048]{1,0:T(8,128)(2,1)S(1)}, f32[320,256]{1,0:T(8,128)S(1)}, f32[320,256]{1,0:T(8,128)S(1)}, bf16[4,320,2048]{2,1,0:T(8,128)(2,1)S(1)}) custom-call(bf16[320,2048]{1,0:T(8,128)(2,1)S(1)} %get-tuple-element.85.q_ref, bf16[4,320,128]{2,1,0:T(8,128)(2,1)S(1)} %copy-done.4, bf16[4,320,128]{2,1,0:T(8,128)(2,1)S(1)} %copy-done.6, ...), custom_call_target="tpu_custom_call" | custom-call | tf_op jit(solution)/shard_map/attend_back/pallas_call | solution.py:844
  488.9 2.3 copy-done
  491.3 9.2 %fusion.9 = (f32[2048]{0:T(1024)S(1)}, f32[320]{0:T(512)S(1)}, f32[320,2048]{1,0:T(8,128)}) fusion(bf16[320,2048]{1,0:T(8,128)(2,1)S(1)} %copy-done.15, f32[320]{0:T(512)S(1)} %add_rsqrt_fusion.1, f32[2048]{0:T(1024)S(1)} %get-tuple-element.110, bf16[2048,2560]{1,0:T(8,128)(2,1)} %get-tuple-element.82, bf16[320,256]{1,0:T(8,128)(2,1)S(1)} %convert_element_type.134, ...), kind=kOutput, calls=%fused_computation.18 | convolution fusion | flops 3364943616 | bytes 16075264 | tf_op jit(solution)/shard_map/dot_general | solution.py:1039
  502.0 1.0 copy.31
  503.0 3.9 convert_reduce_fusion
  506.9 6.8 convolution_convert_fusion.1
  513.7 1.3 multiply_convert_fusion
  515.3 1.0 copy-done.19
  516.3 2.2 fusion.8
  518.6 8.7 %convolution_convert_fusion = bf16[2048,2560]{1,0:T(8,128)(2,1)} fusion(bf16[320,256]{1,0:T(8,128)(2,1)S(1)} %convert_element_type.134, bf16[320,256]{1,0:T(8,128)(2,1)S(1)} %convert_element_type.133, bf16[320,2048]{1,0:T(8,128)(2,1)S(1)} %get-tuple-element.95, bf16[320,2048]{1,0:T(8,128)(2,1)S(1)} %copy-done.16, f32[2048]{0:T(1024)S(1)} %get-tuple-element.110, ...), kind=kOutput, calls=%fused_computation | convolution fusion | flops 3368222720 | bytes 13444352 | tf_op jit(solution)/shard_map/dot_general | solution.py:1044
  527.3 37.7 %reduce-scatter.2.cloned.1.call-done = bf16[1,4,64,4224]{3,2,1,0:T(8,128)(2,1)} async-done(((bf16[4,4,64,4224]{3,2,1,0:T(8,128)(2,1)}), bf16[1,4,64,4224]{3,2,1,0:T(8,128)(2,1)}) %reduce-scatter.2.cloned.1.call-update) | async-done | bytes 2162704 | tf_op jit(solution)/shard_map/reduce_scatter | solution.py:1046
  565.0 117.9 %reduce_all.1 = (bf16[64,2048]{1,0:T(8,128)(2,1)}, bf16[64,2560]{1,0:T(8,128)(2,1)}, bf16[64,128]{1,0:T(8,128)(2,1)}, bf16[4,64,4224]{2,1,0:T(8,128)(2,1)}) custom-call(bf16[4,2,256,2048]{3,2,1,0:T(8,128)(2,1)} %bitcast.41, bf16[4,2,256,2560]{3,2,1,0:T(8,128)(2,1)} %bitcast.40, bf16[4,2,256,128]{3,2,1,0:T(8,128)(2,1)} %bitcast.45, bf16[4,64,4224]{2,1,0:T(8,128)(2,1)} %bitcast.44), custom_call_target="tpu_custom_call" | custom-call | tf_op jit(solution)/shard_map/reduce_all/pallas_call | solution.py:967
  682.9 1.6 slice_convert_fusion.1
  684.5 1.8 slice_convert_fusion
  686.3 1.2 convert_bitcast_fusion.1
  688.2 0.7 convert_reduce_fusion.4
  688.9 0.8 convert_element_type.143
  689.7 1.2 copy.34
  691.0 3.4 copy.32
  694.4 4.0 reshape.234
  698.4 7.7 %slice_reduce_fusion = (f32[64,44,128]{2,1,0:T(8,128)S(1)}, f32[64,44,128]{2,1,0:T(8,128)S(1)}) fusion(f32[64,44,2,128]{3,2,1,0:T(2,128)S(1)} %reshape.234), kind=kLoop, calls=%fused_computation.32 | loop fusion | bytes 5767168 | tf_op jit(solution)/shard_map/slice | solution.py:1061
  706.1 1.5 copy.39
  707.6 1.5 copy.40
  (81 shorter events, 6.6 us)
Async XLA Ops:
  7.2 9.6 %copy-start.21 = (bf16[64,5632]{1,0:T(8,128)(2,1)S(1)}, bf16[64,5632]{1,0:T(8,128)(2,1)}, u32[]{:S(2)}) copy-start(bf16[64,5632]{1,0:T(8,128)(2,1)} %param.32) | copy-start | bytes 2162692
  7.2 557.8 %reduce-scatter.2.cloned.1.call-start = ((), (), s32[]{:S(2)}) async-start(), calls=%async_computation.1 | async-start | bytes 10813440 | tf_op jit(solution)/shard_map/reduce_scatter | solution.py:1046
  17.3 3.5 copy-start.17
  22.3 0.6 copy-start.23
  241.7 2.2 copy-start.14
  243.8 31.9 %slice-start = ((s8[8388608]{0:T(1024)(128)(4,1)}), s8[4194304]{0:T(1024)(128)(4,1)S(1)}, s32[]{:S(2)}) async-start(s8[8388608]{0:T(1024)(128)(4,1)} %bitcast.52), calls=%async_computation.2 | async-start | bytes 8388608
  243.9 31.8 %slice-start.1 = ((s8[8388608]{0:T(1024)(128)(4,1)}), s8[4194304]{0:T(1024)(128)(4,1)S(1)}, s32[]{:S(2)}) async-start(s8[8388608]{0:T(1024)(128)(4,1)} %bitcast.52), calls=%async_computation.3 | async-start | bytes 8388608
  273.4 0.8 copy-start.1
  274.2 0.7 copy-start.3
  275.0 0.7 copy-start.5
  275.7 3.1 copy-start.7
  278.8 1.5 copy-start.9
  417.5 4.1 copy-start.10
  417.5 6.6 slice-start.2
  421.6 1.7 copy-start.18
  421.6 3.4 slice-start.3
  425.0 2.9 copy-start.12
  425.0 2.9 copy-start.2
  425.0 2.9 copy-start.4
  425.0 2.9 copy-start.6
  427.9 63.4 %copy-start.15 = (bf16[320,2048]{1,0:T(8,128)(2,1)S(1)}, bf16[320,2048]{1,0:T(8,128)(2,1)}, u32[]{:S(2)}) copy-start(bf16[320,2048]{1,0:T(8,128)(2,1)} %param.21) | copy-start | bytes 3932164
  488.9 2.3 copy-start
  503.0 3.9 copy-start.8
  503.0 3.9 copy-start.13
  506.9 6.8 copy-start.11
  513.7 1.6 copy-start.16
  513.7 2.6 copy-start.19
  682.9 4.6 copy-start.20
  687.5 0.7 copy-start.24
  687.5 1.4 copy-start.22
Sparse Core Ops, SparseCore 0:
  417.6 147.3 reduce-scatter.1

commit v4 on v3

--- a/solution.py
+++ b/solution.py
@@ -408,128 +408,155 @@
             pl.when(cond)(sig); count = count + jnp.where(cond, 1, 0)
     pl.semaphore_wait(barrier, count)
 
-def gather_kernel(nz, wq, wk, wv, wo, gains, wgu, wd, gy, QKV, WO, GAIN, G0, G1, GY,
-                  loc, a2a_s, a2a_r, gy_s, gy_r, z_s, z_r, d_s, d_r, p_s, p_r, e_s, e_r):
-    c, k, n = place()
-    G = (G0, G1); W = (wgu, wd)
-    FF = len(G)
+class Line:
+    def __init__(self, nz, at, refs, send, recv, place_of):
+        self.nz, self.at, self.refs, self.send, self.recv, self.place_of = nz, at, refs, send, recv, place_of
+
+    def _copy(self, a, way, s, origin):
+        c, k, n = self.at
+        ref = self.place_of(self.refs[a], origin)
+        return remote(ref, ref, self.send.at[a, way, s], self.recv.at[a, way, s], c, k, n + 1 if way == 0 else n - 1)
+
+    def _origin(self, way, s):
+        n = self.at[2]
+        o = n - s if way == 0 else n + s
+        return (n >= s) if way == 0 else (n + s <= self.nz - 1), jnp.clip(o, 0, self.nz - 1)
+
+    def _sends(self, way, s):
+        n = self.at[2]
+        return self._origin(way, s)[0] & ((n < self.nz - 1) if way == 0 else (n > 0))
+
+    def start(self, a, s, way):
+        @pl.when(self._sends(way, s))
+        def _(): self._copy(a, way, s, self._origin(way, s)[1]).start()
+
+    def step(self, a, s, then=None):
+        for way in range(2):
+            came, origin = self._origin(way, s)
+            @pl.when(came)
+            def _(): self._copy(a, way, s - 1, origin).wait_recv()
+            if s < self.nz - 1: self.start(a, s, way)
+            if then is not None:
+                @pl.when(came)
+                def _(): then(origin)
+
+    def finish(self, a):
+        for s in range(self.nz - 1):
+            for way in range(2):
+                @pl.when(self._sends(way, s))
+                def _(): self._copy(a, way, s, self._origin(way, s)[1]).wait_send()
+
+
+def gather_kernel(nz, wq, wk, wv, wo, gains, wg, wu, wd, qkv, out, gain, gu, gd,
+                  loc, sw_s, sw_r, z_s, z_r, f_s, f_r, p_s, p_r, h_s, h_r, d_s, d_r, e_s, e_r):
+    c, k, n = at = place()
+    rows, q = wq.shape
+    kv = wk.shape[1]
+    cols = gd.shape[-1]
+    part = nz * rows
+    half = part // 2
+    kn = k * nz + n
+    cx, cy, cd = (chip_at(c, r) for r in (1, 2, 3))
+    hello([(None, cc, k, n) for cc in (cx, cy, cd)] + [(None, c, 1 - k, n), (n > 0, c, k, n - 1), (n < nz - 1, c, k, n + 1)])
+
+    def mycols(w, cc): return w.at[:, pl.ds(pl.multiple_of(cc * cols, 128), cols)]
+    def landing(i, cc): return gd.at[cc] if i == 2 else gu.at[cc, kn, :, pl.ds(i * cols, cols)]
+    whole = (qkv, out, gain)
+    def block(ref, z): return ref.at[pl.ds(pl.multiple_of(((c * CORES + k) * nz + z) * rows, rows), rows)]
+    own = [pltpu.make_async_copy(wq, block(qkv, n).at[:, pl.ds(0, q)], loc.at[0]),
+           pltpu.make_async_copy(wk, block(qkv, n).at[:, pl.ds(q, kv)], loc.at[1]),
+           pltpu.make_async_copy(wv, block(qkv, n).at[:, pl.ds(q + kv, kv)], loc.at[2]),
+           pltpu.make_async_copy(wo, block(out, n), loc.at[3]), pltpu.make_async_copy(gains, block(gain, n), loc.at[4])]
+    ownff = [pltpu.make_async_copy(mycols(w, c), landing(i, c), loc.at[5 + i]) for i, w in enumerate((wg, wu, wd))]
+    for cp in own + ownff: cp.start()
+    swap = [[remote(mycols(w, cc), landing(i, c), sw_s.at[i, r], sw_r.at[i, r], cc, k, n) for r, cc in enumerate((cx, cy, cd))]
+            for i, w in enumerate((wg, wu, wd))]
+    for i in range(3):
+        for cp in swap[i]: cp.start()
+    for cp in own: cp.wait()
+
+    line = Line(nz, at, whole, z_s, z_r, block)
+    for a in range(3):
+        for way in range(2): line.start(a, 0, way)
+
+    def span(ref, cc, first, size):
+        return ref.at[pl.ds(pl.multiple_of((cc * CORES + k) * part, part) + first, size)]
+    plane = [[remote(span(ref, c, 0, part), span(ref, c, 0, part), p_s.at[a, r], p_r.at[a, r], cc, k, n) for r, cc in enumerate((cx, cy))]
+             for a, ref in enumerate(whole)]
+    across = [[remote(span(ref, cx, 0, half), span(ref, cx, 0, half), h_s.at[a, 0], h_r.at[a, 0], cy, k, n),
+               remote(span(ref, cy, half, half), span(ref, cy, half, half), h_s.at[a, 1], h_r.at[a, 1], cx, k, n)]
+              for a, ref in enumerate(whole)]
+    cores = [[remote(span(ref, cc, 0, part), span(ref, cc, 0, part), d_s.at[a, r], d_r.at[a, r], c, 1 - k, n)
+              for r, cc in enumerate((c, cx, cy, cd))] for a, ref in enumerate(whole)]
+
+    def plane_start(a):
+        for cp in plane[a] + cores[a][:1]: cp.start()
+    def plane_next(a):
+        for i in range(2):
+            plane[a][i].wait_recv()
+            across[a][i].start()
+            cores[a][1 + i].start()
+    def plane_last(a):
+        for cp in across[a]: cp.wait_recv()
+        cores[a][3].start()
+
+    for s in range(1, nz):
+        for a in range(3):
+            line.step(a, s)
+            if s == nz - 1: plane_start(a)
+
+    ff = Line(nz, at, (gu,), f_s, f_r, lambda ref, z: ref.at[:, k * nz + z])
+    def twin(z):
+        ref = gu.at[:, k * nz + z]
+        return remote(ref, ref, e_s.at[z], e_r.at[z], c, 1 - k, n)
+    for i in range(2):
+        ownff[i].wait()
+        for cp in swap[i]: cp.wait_recv()
+    for way in range(2): ff.start(0, 0, way)
+    twin(n).start()
+    plane_next(0)
+    ff.step(0, 1, lambda z: twin(z).start())
+    for a in (1, 2): plane_next(a)
+    ff.step(0, 2, lambda z: twin(z).start())
+    for a in range(3): plane_last(a)
+    ownff[2].wait()
+    for cp in swap[2]: cp.wait_recv()
+    for s in range(3, nz): ff.step(0, s, lambda z: twin(z).start())
+    for a in range(3):
+        for cp in cores[a]: cp.wait_recv()
+    for z in range(nz): twin(z).wait()
+    for i in range(3):
+        for cp in swap[i]: cp.wait_send()
+    for a in range(3):
+        line.finish(a)
+        for cp in plane[a] + across[a] + cores[a]: cp.wait_send()
+    ff.finish(0)
+
+
+def gather_all(nz, wq, wk, wv, wo, gains, wg, wu, wd):
     rows = wq.shape[0]
-    other = 1 - k
-    left, right = n > 0, n < nz - 1
-    others = [chip_at(c, r) for r in range(1, CHIPS)]
-    hello([(None, cc, k, n) for cc in others] + [(None, c, other, n), (left, c, k, n - 1), (right, c, k, n + 1)])
-    kn = k * nz + n
-    b = (c * CORES + k) * nz + n
-    started = []
-    def start(cond, desc):
-        if cond is None: desc.start()
-        else: pl.when(cond)(lambda: desc.start())
-        started.append((cond, desc))
-    def recv(cond, desc):
-        if cond is None: desc.wait_recv()
-        else: pl.when(cond)(lambda: desc.wait_recv())
-    def blk(z): return pl.ds(pl.multiple_of(((c * CORES + k) * nz + z) * rows, rows), rows)
-    mine = blk(n)
-    def mycols(m, cc):
-        cols = G[m].shape[-1]
-        return W[m].at[:, pl.ds(pl.multiple_of(cc * cols, 128), cols)]
-    q, kv = wq.shape[1], wk.shape[1]
-    for i, cc in enumerate(others):
-        for m in range(FF):
-            start(None, remote(mycols(m, cc), G[m].at[c, kn], a2a_s.at[m, i], a2a_r.at[m, i], cc, k, n))
-    own = [pltpu.make_async_copy(wq, QKV.at[mine, pl.ds(0, q)], loc.at[0]),
-           pltpu.make_async_copy(wk, QKV.at[mine, pl.ds(q, kv)], loc.at[1]),
-           pltpu.make_async_copy(wv, QKV.at[mine, pl.ds(q + kv, kv)], loc.at[2]),
-           pltpu.make_async_copy(wo, WO.at[mine], loc.at[3]),
-           pltpu.make_async_copy(gains, GAIN.at[mine], loc.at[4])]
-    ownff = [pltpu.make_async_copy(mycols(m, c), G[m].at[c, kn], loc.at[5 + m]) for m in range(FF)]
-    owngy = pltpu.make_async_copy(gy, GY.at[0], loc.at[8])
-    for cp in own + ownff + [owngy]: cp.start()
-    for cp in own: cp.wait()
-    A = (QKV, WO, GAIN)
-    def zsend(item, ref, dirn, s):
-        cond = (right & (n - s >= 0)) if dirn == 0 else (left & (n + s <= nz - 1))
-        z = n + 1 if dirn == 0 else n - 1
-        return cond, remote(ref, ref, z_s.at[item, dirn, s], z_r.at[item, dirn, s], c, k, z)
-    def zrecv(item, ref, dirn, s):
-        cond = (n - s >= 0) if dirn == 0 else (n + s <= nz - 1)
-        return cond, remote(ref, ref, z_s.at[item, dirn, s - 1], z_r.at[item, dirn, s - 1], c, k, n)
-    def origin(dirn, s):
-        o = n - s if dirn == 0 else n + s
-        return jnp.clip(o, 0, nz - 1)
-    for a in range(3):
-        for dirn in range(2):
-            start(*zsend(a, A[a].at[mine], dirn, 0))
-    for i, cc in enumerate(others):
-        start(None, remote(gy, GY.at[1 + i], gy_s.at[i], gy_r.at[i], cc, k, n))
-    for s in range(1, nz):
-        for dirn in range(2):
-            for a in range(3):
-                ref = A[a].at[blk(origin(dirn, s))]
-                recv(*zrecv(a, ref, dirn, s))
-                if s < nz - 1: start(*zsend(a, ref, dirn, s))
-    def part(cc, kk): return pl.ds(pl.multiple_of((cc * CORES + kk) * nz * rows, rows), nz * rows)
-    for a in range(3):
-        for i, cc in enumerate(others):
-            start(None, remote(A[a].at[part(c, k)], A[a].at[part(c, k)], p_s.at[a, i], p_r.at[a, i], cc, k, n))
-        start(None, remote(A[a].at[part(c, k)], A[a].at[part(c, k)], d_s.at[a, 0], d_r.at[a, 0], c, other, n))
-    for m in range(FF):
-        ownff[m].wait()
-        for i in range(CHIPS - 1):
-            remote(G[m].at[c, kn], G[m].at[c, kn], a2a_s.at[m, i], a2a_r.at[m, i], c, k, n).wait_recv()
-        ref = G[m].at[:, kn]
-        for dirn in range(2): start(*zsend(3 + m, ref, dirn, 0))
-        start(None, remote(ref, ref, e_s.at[m, 0, 0], e_r.at[m, 0, 0], c, other, n))
-    for s in range(1, nz):
-        for dirn in range(2):
-            for m in range(FF):
-                ref = G[m].at[:, k * nz + origin(dirn, s)]
-                cond, d = zrecv(3 + m, ref, dirn, s)
-                recv(cond, d)
-                if s < nz - 1: start(*zsend(3 + m, ref, dirn, s))
-                start(cond, remote(ref, ref, e_s.at[m, dirn, s], e_r.at[m, dirn, s], c, other, n))
-    for i in range(CHIPS - 1):
-        cc = others[i]
-        for a in range(3):
-            ref = A[a].at[part(cc, k)]
-            remote(ref, ref, p_s.at[a, i], p_r.at[a, i], c, k, n).wait_recv()
-            start(None, remote(ref, ref, d_s.at[a, 1 + i], d_r.at[a, 1 + i], c, other, n))
-    owngy.wait()
-    for i in range(CHIPS - 1):
-        remote(gy, GY.at[1 + i], gy_s.at[i], gy_r.at[i], c, k, n).wait_recv()
-    for a in range(3):
-        for i in range(CHIPS):
-            remote(A[a].at[part(c, k)], A[a].at[part(c, k)], d_s.at[a, i], d_r.at[a, i], c, k, n).wait_recv()
-    for m in range(FF):
-        ref = G[m].at[:, kn]
-        remote(ref, ref, e_s.at[m, 0, 0], e_r.at[m, 0, 0], c, k, n).wait_recv()
-        for s in range(1, nz):
-            for dirn in range(2):
-                cond = (n - s >= 0) if dirn == 0 else (n + s <= nz - 1)
-                recv(cond, remote(ref, ref, e_s.at[m, dirn, s], e_r.at[m, dirn, s], c, k, n))
-    for cond, desc in started:
-        if cond is None: desc.wait_send()
-        else: pl.when(cond)(lambda desc=desc: desc.wait_send())
-
-def gather_all(nz, wq, wk, wv, wo, gains, wgu, wd, gy):
-    D = wq.shape[0] * CHIPS * CORES * nz
+    width = rows * CHIPS * CORES * nz
+    cols = wg.shape[1] // CHIPS
     bf = jnp.bfloat16
-    def ff(w):
-        return jax.ShapeDtypeStruct((CHIPS, CORES * nz, w.shape[0], w.shape[1] // CHIPS), bf)
+    shape = jax.ShapeDtypeStruct
     dma = pltpu.SemaphoreType.DMA
     return pl.pallas_call(
         functools.partial(gather_kernel, nz),
-        out_shape=(jax.ShapeDtypeStruct((D, wq.shape[1] + 2 * wk.shape[1]), bf), jax.ShapeDtypeStruct((D, wo.shape[1]), bf),
-                   jax.ShapeDtypeStruct((D, 128), bf), ff(wgu), ff(wd), jax.ShapeDtypeStruct((CHIPS,) + gy.shape, bf)),
-        in_specs=[ANY] * 8, out_specs=(ANY,) * 6,
-        scratch_shapes=[dma((9,)), dma((3, 3)), dma((3, 3)), dma((3,)), dma((3,)), dma((6, 2, nz)), dma((6, 2, nz)),
-                        dma((3, 4)), dma((3, 4)), dma((3, 3)), dma((3, 3)), dma((3, 2, nz)), dma((3, 2, nz))],
+        out_shape=(shape((width, wq.shape[1] + 2 * wk.shape[1]), bf), shape((width, wo.shape[1]), bf), shape((width, gains.shape[1]), bf),
+                   shape((CHIPS, CORES * nz, rows, 2 * cols), bf), shape((CHIPS, rows, cols), bf)),
+        in_specs=[ANY] * 8, out_specs=(ANY,) * 5,
+        scratch_shapes=[dma((8,)), dma((3, 3)), dma((3, 3)), dma((3, 2, nz)), dma((3, 2, nz)), dma((1, 2, nz)), dma((1, 2, nz)),
+                        dma((3, 2)), dma((3, 2)), dma((3, 2)), dma((3, 2)), dma((3, 4)), dma((3, 4)), dma((nz,)), dma((nz,))],
         compiler_params=pltpu.CompilerParams(collective_id=0, has_side_effects=True),
         name="gather_all",
-    )(wq, wk, wv, wo, gains, wgu, wd, gy)
-
-def mlp_kernel(nz, x, gy, gu_hbm, gd_hbm, gx_parts, mlp_parts, sums,
-               xs, gys, gu, gd, mix, ggu, gx, mo, xt, load, ag_s, ag_r, rs_s, rs_r, own, out, core_s, core_r, ready, done):
+    )(wq, wk, wv, wo, gains, wg, wu, wd)
+
+
+HALVES = ((0, 0), (0, 1), (1, 0), (2, 0), (1, 1), (2, 1), (3, 0), (3, 1))
+
+
+def mlp_kernel(nz, x, gy, gu_hbm, gd_hbm, gx_parts, mlp_parts, mlp_cross, sums,
+               xs, gys, gu, gd, mix, ggu, gx, mo, xt, load, ag_s, ag_r, rs_s, rs_r, mo_s, mo_r, out, core_s, core_r, ready, done):
     c, k, n = place()
     f32, bf16 = jnp.float32, jnp.bfloat16
     slots, width = x.shape
@@ -538,14 +565,24 @@
     per_tile = nz
     tile = nz * rows
     hello([(None, chip_at(c, r), k, n) for r in (1, 2, 3)] + [(None, c, 1 - k, n)])
-    loads = [pltpu.make_async_copy(x, xs.at[0], load.at[0])]
-    sends = [remote(x, xs.at[r], ag_s.at[r], ag_r.at[r], chip_at(c, r), k, n) for r in (1, 2)]
-    for cp in sends: cp.start()
-    loads += [pltpu.make_async_copy(gu_hbm, gu, load.at[1]), pltpu.make_async_copy(gd_hbm, gd, load.at[2]),
-              pltpu.make_async_copy(gy, gys, load.at[3])]
+    def half_of(ref, h): return ref.at[pl.ds(h * half, half)]
+    index = {place_: i for i, place_ in enumerate(HALVES)}
+    sends = {}
+    for h in range(2):
+        for r in (1, 2):
+            i = index[r, h]
+            sends[i] = remote(half_of(x, h), xs.at[i], ag_s.at[i], ag_r.at[i], chip_at(c, r), k, n)
+            sends[i].start()
+    loads = [pltpu.make_async_copy(half_of(x, h), xs.at[h], load.at[h]) for h in range(2)]
+    loads += [pltpu.make_async_copy(half_of(gy.at[r], h), gys.at[i], load.at[2 + i]) for i, (r, h) in enumerate(HALVES)]
     for cp in loads: cp.start()
-    relays = [remote(xs.at[1, pl.ds(0, half)], xs.at[3, pl.ds(0, half)], ag_s.at[0], ag_r.at[0], chip_at(c, 2), k, n),
-              remote(xs.at[2, pl.ds(half, half)], xs.at[3, pl.ds(half, half)], ag_s.at[3], ag_r.at[3], chip_at(c, 1), k, n)]
+    def weights(col, w, j):
+        return [pltpu.make_async_copy(a.at[:, :, pl.ds(first + col, w)], b.at[:, :, pl.ds(first + col, w)], load.at[10 + 3 * j + i])
+                for i, (a, b, first) in enumerate(((gu_hbm, gu, 0), (gu_hbm, gu, cols), (gd_hbm, gd, 0)))]
+    for j in range(-(-cols // 256)):
+        for cp in weights(j * 256, min(256, cols - j * 256), j): cp.start()
+    relays = {index[3, 0]: (index[1, 0], 2), index[3, 1]: (index[2, 1], 1)}
+    relays = {i: remote(xs.at[j], xs.at[i], ag_s.at[i], ag_r.at[i], chip_at(c, r), k, n) for i, (j, r) in relays.items()}
     for cp in loads: cp.wait()
 
     def columns(ref, at, size):
@@ -556,103 +593,128 @@
         t = ref[pl.ds(i * (256 // rows), 256 // rows)]
         return t.reshape(256, t.shape[2])
 
+    def to_owner(src, dst, i, s_s, s_r):
+        r, h = HALVES[i]
+        return remote(src.at[i], half_of(dst.at[r], h), s_s.at[i], s_r.at[i], chip_at(c, r), k, n)
+
+    def kept(src, dst, i, j):
+        return pltpu.make_async_copy(src.at[i], half_of(dst, HALVES[i][1]), out.at[j])
+
     def block(r, carry):
-        @pl.when(r == 1)
-        def _():
-            for cp in sends: cp.wait_recv()
-            for cp in relays: cp.start()
+        two = pl.ds(2 * r, 2)
+        for t in (1, 2):
+            @pl.when(r == t)
+            def _():
+                for i in (2 * t, 2 * t + 1): sends[i].wait_recv()
+                relays[{1: index[3, 0], 2: index[3, 1]}[t]].start()
         @pl.when(r == 3)
         def _():
-            for cp in relays: cp.wait_recv()
-        def chunk(col, w):
-            h = jnp.dot(xs[r], columns(gu, 2 * col, 2 * w), preferred_element_type=f32)
-            gm = jnp.dot(gys[r], columns(gd, col, w), preferred_element_type=f32)
+            for cp in relays.values(): cp.wait_recv()
+        def both(ref): return ref[two].reshape(slots, ref.shape[2])
+        def put(ref, at, v): ref[two, :, at] = v.astype(bf16).reshape(2, half, v.shape[1])
+        def chunk(col, w, j):
+            @pl.when(r == 0)
+            def _():
+                for cp in weights(col, w, j): cp.wait()
+            tokens = both(xs)
+            hg = jnp.dot(tokens, columns(gu, col, w), preferred_element_type=f32)
+            hu = jnp.dot(tokens, columns(gu, cols + col, w), preferred_element_type=f32)
+            gm = jnp.dot(both(gys), columns(gd, col, w), preferred_element_type=f32)
             for q in range(w // 128):
-                gate, up, g = h[:, 256 * q : 256 * q + 128], h[:, 256 * q + 128 : 256 * q + 256], gm[:, 128 * q : 128 * q + 128]
+                gate, up, g = (t[:, 128 * q : 128 * q + 128] for t in (hg, hu, gm))
                 sg = 1.0 / (1.0 + jnp.exp(-gate))
                 act = gate * sg
-                mix[r, :, pl.ds(col + 128 * q, 128)] = (act * up).astype(bf16)
-                ggu[r, :, pl.ds(2 * col + 256 * q, 128)] = (g * up * (sg * (1.0 + gate * (1.0 - sg)))).astype(bf16)
-                ggu[r, :, pl.ds(2 * col + 256 * q + 128, 128)] = (g * act).astype(bf16)
+                put(mix, pl.ds(col + 128 * q, 128), act * up)
+                put(ggu, pl.ds(col + 128 * q, 128), g * up * (sg * (1.0 + gate * (1.0 - sg))))
+                put(ggu, pl.ds(cols + col + 128 * q, 128), g * act)
         def pair(j, carry):
-            chunk(pl.multiple_of(j * 256, 256), 256)
+            chunk(pl.multiple_of(j * 256, 256), 256, j)
             return carry
         lax.fori_loop(0, cols // 256, pair, 0)
-        if cols % 256: chunk(cols - 128, 128)
+        if cols % 256: chunk(cols // 256 * 256, cols % 256, cols // 256)
         def back(i, carry):
             at = pl.ds(pl.multiple_of(i * 256, 256), 256)
-            gx[r, :, at] = lax.dot_general(ggu[r], some_rows(gu, i), contract_last, preferred_element_type=f32).astype(bf16)
+            put(gx, at, lax.dot_general(both(ggu), some_rows(gu, i), contract_last, preferred_element_type=f32))
             return carry
         lax.fori_loop(0, width // 256, back, 0)
-        @pl.when(r == 0)
-        def _(): pltpu.make_async_copy(gx.at[0], gx_parts.at[0], own).start()
-        @pl.when(r > 0)
-        def _(): remote(gx.at[r], gx_parts.at[r], rs_s.at[r], rs_r.at[r], chip_at(c, r), k, n).start()
+        for t in range(CHIPS):
+            @pl.when(r == t)
+            def _():
+                for i in (2 * t, 2 * t + 1):
+                    (to_owner(gx, gx_parts, i, rs_s, rs_r) if t else kept(gx, gx_parts.at[0], i, i)).start()
         def down(i, carry):
             at = pl.ds(pl.multiple_of(i * 256, 256), 256)
-            mo[r, :, at] = lax.dot_general(mix[r], some_rows(gd, i), contract_last, preferred_element_type=f32).astype(bf16)
+            put(mo, at, lax.dot_general(both(mix), some_rows(gd, i), contract_last, preferred_element_type=f32))
             return carry
         lax.fori_loop(0, width // 256, down, 0)
-        pltpu.make_async_copy(mo.at[r], mlp_parts.at[r], out.at[r]).start()
+        for t in range(CHIPS):
+            @pl.when(r == t)
+            def _():
+                for i in (2 * t, 2 * t + 1):
+                    (kept(mo, mlp_parts.at[0], i, 2 + i) if t == 0 else kept(mo, mlp_cross, i, i - 2) if t == 3
+                     else to_owner(mo, mlp_parts, i, mo_s, mo_r)).start()
         return carry
     lax.fori_loop(0, CHIPS, block, 0)
 
     pl.semaphore_signal(ready, inc=1, device_id={"wide": c * CORES + 1 - k, "narrow": n}, device_id_type=MESH)
     pl.semaphore_wait(ready, 1)
-    sent, came = 0, CHIPS * per_tile
-
-    def terms(t, kk, put):
-        at = pl.ds(pl.multiple_of((t * CORES + kk) * tile, 128), tile)
-        for src, right, ref in ((xs, ggu, gu), (gys, mix, gd)):
-            total = ref.shape[-1]
+    sent, came = pl.ds(0, CHIPS * nz), pl.ds(CHIPS * nz, CHIPS * nz)
+    pairs = ((gys, mix, gd), (xs, ggu, gu))
+
+    def tiles(total): return [(t * 256, min(256, total - t * 256)) for t in range(-(-total // 256))]
+
+    def to_core(i, col, w, sem):
+        ref = pairs[i][2]
+        return remote(ref.at[sent, :, pl.ds(col, w)], ref.at[came, :, pl.ds(col, w)], core_s.at[sem], core_r.at[sem], c, 1 - k, n)
+
+    def to_sums(i, t, sem):
+        ref = pairs[i][2]
+        return pltpu.make_async_copy(ref.at[pl.ds(CHIPS * nz + t * nz, nz)], sums.at[:, t, :, pl.ds(i * cols, ref.shape[-1])], done.at[sem])
+
+    def each(i, body):
+        total, base = pairs[i][2].shape[-1], 0 if i == 0 else len(tiles(cols))
+        def step(j, carry):
+            body(pl.multiple_of(j * 256, 256), 256, base + j)
+            return carry
+        lax.fori_loop(0, total // 256, step, 0)
+        if total % 256: body(total // 256 * 256, total % 256, base + total // 256)
+
+    def terms(i, kk, use):
+        src, right, ref = pairs[i]
+        for t in range(CHIPS):
+            at = pl.ds(pl.multiple_of((t * CORES + kk) * tile, 128), tile)
             for r in range(CHIPS):
-                xt[:, r * slots : (r + 1) * slots] = src[r, :, at].T
-            def one(col, w):
-                b = right[:, :, pl.ds(col, w)].reshape(CHIPS * slots, w)
-                put(ref, t, col, w, jnp.dot(xt[...], b, preferred_element_type=f32))
-            def step(j, carry):
-                one(pl.multiple_of(j * 256, 256), 256)
-                return carry
-            lax.fori_loop(0, total // 256, step, 0)
-            if total % 256: one(total - 128, 128)
-
-    def to_core(ref, i, t):
-        return remote(ref.at[pl.ds(sent + t * per_tile, per_tile)], ref.at[pl.ds(came + t * per_tile, per_tile)],
-                      core_s.at[i, t], core_r.at[i, t], c, 1 - k, n)
-
-    def to_sums(ref, i, t):
-        first = 0 if i == 0 else cols
-        return pltpu.make_async_copy(ref.at[pl.ds(came + t * per_tile, per_tile)],
-                                     sums.at[:, t, :, pl.ds(first, ref.shape[-1])], done.at[i, t])
-
-    def theirs(t, carry):
-        def put(ref, t, col, w, v):
-            ref[pl.ds(sent + t * per_tile, per_tile), :, pl.ds(col, w)] = v.astype(bf16).reshape(per_tile, rows, w)
-        terms(t, 1 - k, put)
-        for i, ref in enumerate((gd, gu)): to_core(ref, i, t).start()
-        return carry
-    lax.fori_loop(0, CHIPS, theirs, 0)
-
-    def ours(t, carry):
-        for i, ref in enumerate((gd, gu)): to_core(ref, i, t).wait_recv()
-        def put(ref, t, col, w, v):
-            here = (pl.ds(came + t * per_tile, per_tile), slice(None), pl.ds(col, w))
-            ref[here] = (ref[here].astype(f32) + v.reshape(per_tile, rows, w)).astype(bf16)
-        terms(t, k, put)
-        for i, ref in enumerate((gd, gu)): to_sums(ref, i, t).start()
-        return carry
-    lax.fori_loop(0, CHIPS, ours, 0)
-
-    for cp in sends + relays: cp.wait_send()
-    pltpu.make_async_copy(gx.at[0], gx_parts.at[0], own).wait()
-    for r in range(CHIPS):
-        pltpu.make_async_copy(mo.at[r], mlp_parts.at[r], out.at[r]).wait()
-    for t in range(CHIPS):
-        for i, ref in enumerate((gd, gu)):
-            to_core(ref, i, t).wait_send()
-            to_sums(ref, i, t).wait()
-    for r in (1, 2, 3):
-        remote(gx.at[r], gx_parts.at[r], rs_s.at[r], rs_r.at[r], chip_at(c, r), k, n).wait()
+                xt[t * tile : (t + 1) * tile, r * slots : (r + 1) * slots] = src[2 * r : 2 * r + 2, :, at].reshape(slots, tile).T
+        def body(col, w, sem):
+            b = right[:, :, pl.ds(col, w)].reshape(CHIPS * slots, w)
+            use(i, col, w, sem, jnp.dot(xt[...], b, preferred_element_type=f32).reshape(CHIPS * nz, rows, w))
+        each(i, body)
+
+    def theirs(i, col, w, sem, v):
+        pairs[i][2][sent, :, pl.ds(col, w)] = v.astype(bf16)
+        to_core(i, col, w, sem).start()
+
+    def ours(i, col, w, sem, v):
+        to_core(i, col, w, sem).wait_recv()
+        ref = pairs[i][2]
+        here = (came, slice(None), pl.ds(col, w))
+        ref[here] = (ref[here].astype(f32) + v).astype(bf16)
+
+    for i in range(2): terms(i, 1 - k, theirs)
+    for i in range(2):
+        terms(i, k, ours)
+        for t in range(CHIPS): to_sums(i, t, i * CHIPS + t).start()
+
+    for cp in (*sends.values(), *relays.values()): cp.wait_send()
+    for i in range(2):
+        kept(gx, gx_parts.at[0], i, i).wait()
+        kept(mo, mlp_parts.at[0], i, 2 + i).wait()
+        kept(mo, mlp_cross, 6 + i, 4 + i).wait()
+    for i in range(2):
+        each(i, lambda col, w, sem: to_core(i, col, w, sem).wait_send())
+        for t in range(CHIPS): to_sums(i, t, i * CHIPS + t).wait()
+    for i in range(2, 6): to_owner(mo, mlp_parts, i, mo_s, mo_r).wait()
+    for i in range(2, 8): to_owner(gx, gx_parts, i, rs_s, rs_r).wait()
 
 
 def mlp_all(nz, x, gy, gu, gd):
@@ -660,15 +722,16 @@
     rows, cols = gd.shape[1:]
     bf, dma, vm = jnp.bfloat16, pltpu.SemaphoreType.DMA, pltpu.VMEM
     def blocks(w): return jax.ShapeDtypeStruct((CHIPS, slots, w), bf)
+    def halves(w): return vm((2 * CHIPS, slots // 2, w), bf)
+    tiles = -(-cols // 256)
     flops = 2 * 9 * CHIPS * slots * width * cols
     return pl.pallas_call(
         functools.partial(mlp_kernel, nz),
-        out_shape=(blocks(width), blocks(width), jax.ShapeDtypeStruct((nz, CHIPS, rows, 3 * cols), bf)),
-        in_specs=[ANY] * 4, out_specs=(ANY,) * 3,
-        scratch_shapes=[vm((CHIPS, slots, width), bf), vm((CHIPS, slots, width), bf), vm(gu.shape, bf), vm(gd.shape, bf),
-                        vm((CHIPS, slots, cols), bf), vm((CHIPS, slots, 2 * cols), bf), vm((CHIPS, slots, width), bf),
-                        vm((CHIPS, slots, width), bf), vm((nz * rows, CHIPS * slots), bf), dma((4,)), dma((4,)), dma((4,)), dma((4,)), dma((4,)),
-                        dma, dma((4,)), dma((2, 4)), dma((2, 4)), pltpu.SemaphoreType.REGULAR, dma((2, 4))],
+        out_shape=(blocks(width), jax.ShapeDtypeStruct((3, slots, width), bf), jax.ShapeDtypeStruct((slots, width), bf), jax.ShapeDtypeStruct((nz, CHIPS, rows, 3 * cols), bf)),
+        in_specs=[ANY] * 4, out_specs=(ANY,) * 4,
+        scratch_shapes=[halves(width), halves(width), vm(gu.shape, bf), vm(gd.shape, bf), halves(cols), halves(2 * cols), halves(width),
+                        halves(width), vm((CHIPS * nz * rows, CHIPS * slots), bf), dma((10 + 3 * tiles,)), dma((8,)), dma((8,)), dma((8,)), dma((8,)),
+                        dma((8,)), dma((8,)), dma((6,)), dma((3 * tiles,)), dma((3 * tiles,)), pltpu.SemaphoreType.REGULAR, dma((8,))],
         compiler_params=pltpu.CompilerParams(collective_id=1, has_side_effects=True, vmem_limit_bytes=62 << 20),
         cost_estimate=pl.CostEstimate(flops=flops, bytes_accessed=60 << 20, transcendentals=CHIPS * slots * cols),
         name="mlp_all",
@@ -707,10 +770,32 @@
     return jnp.concatenate([s[:, :clear], last], 1) if clear else last
 
 
-def attend_kernel(q_ref, k_ref, v_ref, tab_ref, qr_ref, k_out, v_out, lse_ref, ctx_ref, ks, vs):
+def attend_kernel(nz, q_ref, k_ref, v_ref, tab_ref, gy, gd_own, qr_ref, k_out, v_out, lse_ref, ctx_ref, gys, gd, ks, vs,
+                  loc, g_s, g_r, h_s, h_r, f_s, f_r, e_s, e_r):
     g = pl.program_id(0)
     f32, bf16 = jnp.float32, jnp.bfloat16
     slots = q_ref.shape[0]
+    c, k, n = at = place()
+    mine = [pltpu.make_async_copy(gd_own, gd.at[:, k * nz + n], loc.at[0]), pltpu.make_async_copy(gy, gys.at[0], loc.at[1])]
+    line = Line(nz, at, (gd,), f_s, f_r, lambda ref, z: ref.at[:, k * nz + z])
+    half = slots // 2
+    sends = [remote(gy, gys.at[r], g_s.at[r], g_r.at[r], chip_at(c, r), k, n) for r in (1, 2)]
+    relays = [remote(gys.at[1, pl.ds(0, half)], gys.at[3, pl.ds(0, half)], h_s.at[0], h_r.at[0], chip_at(c, 2), k, n),
+              remote(gys.at[2, pl.ds(half, half)], gys.at[3, pl.ds(half, half)], h_s.at[1], h_r.at[1], chip_at(c, 1), k, n)]
+    def twin(z):
+        ref = gd.at[:, k * nz + z]
+        return remote(ref, ref, e_s.at[z], e_r.at[z], c, 1 - k, n)
+    @pl.when(g == 0)
+    def _():
+        hello([(None, chip_at(c, r), k, n) for r in (1, 2)]
+              + [(None, c, 1 - k, n), (n > 0, c, k, n - 1), (n < nz - 1, c, k, n + 1)])
+        for cp in mine + sends: cp.start()
+        mine[0].wait()
+        for way in range(2): line.start(0, 0, way)
+        twin(n).start()
+    @pl.when(g == KEY_VALUE_HEADS - 1)
+    def _():
+        line.step(0, 1, lambda z: twin(z).start())
     @pl.when(g == 0)
     def _():
         ks[...] = jnp.zeros_like(ks)
@@ -725,13 +810,13 @@
         x = x.astype(f32) * scale
         stack[0, 0:slots, :] = x.astype(bf16)
         stack[1, 0:slots, :] = pltpu.roll(x, HEAD_SIZE, 1).astype(bf16)
-    for at, size, keys in row_blocks(slots):
+    for start, size, keys in row_blocks(slots):
         below = lax.broadcasted_iota(jnp.int32, (size, 128), 0) >= lax.broadcasted_iota(jnp.int32, (size, 128), 1)
         lse = jnp.zeros((size, PAIR), f32)
         here = lane[0:size]
         for p in range(PAIRS):
             span = slice(p * PAIR, (p + 1) * PAIR)
-            rows = slice(at, at + size)
+            rows = slice(start, start + size)
             q = rotate(q_ref[rows, span], tuple(t[rows] for t in tables)).astype(bf16)
             qr_ref[rows, span] = q
             ctx = jnp.zeros((size, PAIR), f32)
@@ -745,12 +830,23 @@
                 probs = (e * (1.0 / total)).astype(bf16)
                 ctx = ctx + jnp.dot(probs, vs[h, 0:keys, :], preferred_element_type=f32)
             ctx_ref[rows, span] = ctx.astype(bf16)
-        lse_ref[0, at : at + size, :] = lse
-
-
-def attend_all(qkv, tables):
+        lse_ref[0, start : start + size, :] = lse
+    @pl.when(g == KEY_VALUE_HEADS - 1)
+    def _():
+        for cp in sends: cp.wait_recv()
+        for cp in relays: cp.start()
+        for s in range(2, nz): line.step(0, s, lambda z: twin(z).start())
+        for cp in relays: cp.wait()
+        for z in range(nz): twin(z).wait()
+        for cp in sends: cp.wait_send()
+        mine[1].wait()
+        line.finish(0)
+
+
+def attend_all(nz, qkv, tables, gy, gd_own):
     slots = qkv.shape[0]
     wide = REPEAT * HEAD_SIZE
+    dma = pltpu.SemaphoreType.DMA
     first = QUERY_HEADS * HEAD_SIZE // PAIR
     bf16 = jnp.bfloat16
     keys = -(-slots // 128) * 128
@@ -758,31 +854,32 @@
     per_head = pl.BlockSpec((1, slots, PAIR), lambda g: (g, 0, 0))
     wide_spec = pl.BlockSpec((slots, wide), lambda g: (0, g))
     return pl.pallas_call(
-        attend_kernel,
+        functools.partial(attend_kernel, nz),
         grid=(KEY_VALUE_HEADS,),
         out_shape=(shape((slots, QUERY_HEADS * HEAD_SIZE), bf16), shape((KEY_VALUE_HEADS, slots, PAIR), bf16),
                    shape((KEY_VALUE_HEADS, slots, PAIR), bf16), shape((KEY_VALUE_HEADS, slots, PAIR), jnp.float32),
-                   shape((slots, QUERY_HEADS * HEAD_SIZE), bf16)),
+                   shape((slots, QUERY_HEADS * HEAD_SIZE), bf16), shape((CHIPS,) + gy.shape, bf16),
+                   shape((CHIPS, CORES * nz) + gd_own.shape[1:], bf16)),
         in_specs=[wide_spec, pl.BlockSpec((slots, PAIR), lambda g: (0, first + g // 2)),
                   pl.BlockSpec((slots, PAIR), lambda g: (0, first + KEY_VALUE_HEADS // 2 + g // 2)),
-                  pl.BlockSpec((3, slots, PAIR), lambda g: (0, 0, 0))],
-        out_specs=(wide_spec, per_head, per_head, per_head, wide_spec),
-        scratch_shapes=[pltpu.VMEM((2, keys, PAIR), bf16), pltpu.VMEM((2, keys, PAIR), bf16)],
-        compiler_params=pltpu.CompilerParams(vmem_limit_bytes=32 << 20),
+                  pl.BlockSpec((3, slots, PAIR), lambda g: (0, 0, 0)), ANY, ANY],
+        out_specs=(wide_spec, per_head, per_head, per_head, wide_spec, ANY, ANY),
+        scratch_shapes=[pltpu.VMEM((2, keys, PAIR), bf16), pltpu.VMEM((2, keys, PAIR), bf16),
+                        dma((2,)), dma((3,)), dma((3,)), dma((2,)), dma((2,)), dma((1, 2, nz)), dma((1, 2, nz)), dma((nz,)), dma((nz,))],
+        compiler_params=pltpu.CompilerParams(collective_id=4, has_side_effects=True, vmem_limit_bytes=32 << 20),
         name="attend",
-    )(qkv, qkv, qkv, tables)
-
-
-def attend_back_kernel(q_ref, k_ref, v_ref, lse_ref, gc_ref, tab_ref, part, gq_ref, gk_ref, gv_ref, parts,
-                       ks, kt, vt, ds, pr, qs, gs, loc, s_s, s_r):
+    )(qkv, qkv, qkv, tables, gy, gd_own)
+
+
+def attend_back_kernel(q_ref, k_ref, v_ref, lse_ref, gc_ref, tab_ref, part, gq_ref, gk_ref, gv_ref, crossed,
+                       ks, kt, vt, ds, pr, qs, gs, s_s, s_r):
     g = pl.program_id(0)
     c, k, n = place()
-    copies = [pltpu.make_async_copy(part.at[0], parts.at[0], loc)]
-    copies += [remote(part.at[r], parts.at[r], s_s.at[r - 1], s_r.at[r - 1], chip_at(c, r), k, n) for r in (1, 2, 3)]
+    copy = remote(part, crossed, s_s, s_r, chip_at(c, 3), k, n)
     @pl.when(g == 0)
     def _():
-        hello([(None, chip_at(c, r), k, n) for r in (1, 2, 3)])
-        for cp in copies: cp.start()
+        hello([(None, chip_at(c, 3), k, n)])
+        copy.start()
     f32, bf16 = jnp.float32, jnp.bfloat16
     slots = q_ref.shape[0]
     scale = HEAD_SIZE ** -0.5
@@ -828,8 +925,7 @@
         @pl.when(g % 2 == 1)
         def _(): out[...] = jnp.where(lane < HEAD_SIZE, out[...], pltpu.roll(x, HEAD_SIZE, 1))
     @pl.when(g == KEY_VALUE_HEADS - 1)
-    def _():
-        for cp in copies: cp.wait()
+    def _(): copy.wait()
 
 
 def attend_back_all(q, k, v, lse, grad_context, tables, part):
@@ -849,7 +945,7 @@
         in_specs=[wide_spec, per_head, per_head, per_head, wide_spec, pl.BlockSpec((3, slots, PAIR), lambda g: (0, 0, 0)), ANY],
         out_specs=(wide_spec, two, two, ANY),
         scratch_shapes=[vm((2, keys, PAIR), bf16)] * 3 + [vm((2, PAIRS * slots, keys), bf16)] * 2 + [vm((PAIRS * slots, PAIR), bf16)] * 2
-        + [pltpu.SemaphoreType.DMA, pltpu.SemaphoreType.DMA((3,)), pltpu.SemaphoreType.DMA((3,))],
+        + [pltpu.SemaphoreType.DMA] * 2,
         compiler_params=pltpu.CompilerParams(collective_id=2, has_side_effects=True, vmem_limit_bytes=40 << 20),
         name="attend_back",
     )(q, k, v, lse, grad_context, tables, part)
@@ -868,16 +964,14 @@
 
 
 def reduce_kernel(nz, items, *refs):
-    terms, ff = refs[:items], refs[items]
-    outs, ff_out = refs[items + 1 : 2 * items + 1], refs[2 * items + 1]
-    bufs = refs[2 * items + 2 :]
+    terms, outs, bufs = refs[:items], refs[items : 2 * items], refs[2 * items :]
     took, away, zbuf = bufs[:items], bufs[items : 2 * items], bufs[2 * items : 3 * items]
-    core_s, core_r, half_s, half_r, main_s, main_r, z_s, z_r, ff_s, ff_r, loc = bufs[3 * items :]
+    core_s, core_r, half_s, half_r, main_s, main_r, z_s, z_r, loc = bufs[3 * items :]
     c, k, n = place()
     left, right = n > 0, n < nz - 1
     cx, cy, cd = (chip_at(c, r) for r in (1, 2, 3))
     hello([(None, cc, k, n) for cc in (cx, cy, cd)] + [(None, c, 1 - k, n), (left, c, k, n - 1), (right, c, k, n + 1)])
-    rows = ff.shape[1]
+    rows = outs[0].shape[0]
     part = nz * rows
     half = part // 2
     top, low = pl.ds(0, half), pl.ds(half, half)
@@ -940,13 +1034,8 @@
     mine(0)
     stores += along([0])
     for a in range(1, items): mine(a)
-    swaps = [pltpu.make_async_copy(ff.at[c], ff_out.at[c], loc.at[items])]
-    for r, cc in enumerate((cx, cy, cd)):
-        swaps.append(remote(ff.at[cc], ff_out.at[c], ff_s.at[r], ff_r.at[r], cc, k, n))
-    for cp in swaps: cp.start()
     stores += along(list(range(1, items)))
     for cp in stores: cp.wait()
-    for cp in swaps: cp.wait()
     for a in range(items):
         swap[a].wait_send()
         for cp in cross[a] + main[a]: cp.wait_send()
@@ -956,24 +1045,51 @@
                 def _(): hop(a, way, j).wait_send()
 
 
-def reduce_all(nz, terms, ff, cid):
+def reduce_all(nz, terms, cid):
     dma, vm = pltpu.SemaphoreType.DMA, pltpu.VMEM
     m = len(terms)
-    rows = ff.shape[1]
-    part = nz * rows
+    part = terms[0].shape[0] // (CHIPS * CORES)
+    rows = part // nz
     shape = jax.ShapeDtypeStruct
     terms = [t.reshape(CHIPS, CORES, part, t.shape[-1]) for t in terms]
     blocks = [vm((CHIPS, part, t.shape[-1]), t.dtype) for t in terms]
     return pl.pallas_call(
         functools.partial(reduce_kernel, nz, m),
-        out_shape=tuple(shape((rows, t.shape[-1]), t.dtype) for t in terms) + (shape(ff.shape, ff.dtype),),
-        in_specs=[ANY] * (m + 1), out_specs=(ANY,) * (m + 1),
+        out_shape=tuple(shape((rows, t.shape[-1]), t.dtype) for t in terms),
+        in_specs=[ANY] * m, out_specs=(ANY,) * m,
         scratch_shapes=blocks + blocks + [vm((3 * part + 2 * nz * rows, t.shape[-1]), t.dtype) for t in terms]
-        + [dma((m,)), dma((m,)), dma((m, 2)), dma((m, 2)), dma((m, 4)), dma((m, 4)), dma((m, 2, nz)), dma((m, 2, nz)),
-           dma((3,)), dma((3,)), dma((m + 1,))],
+        + [dma((m,)), dma((m,)), dma((m, 2)), dma((m, 2)), dma((m, 4)), dma((m, 4)), dma((m, 2, nz)), dma((m, 2, nz)), dma((m,))],
         compiler_params=pltpu.CompilerParams(collective_id=cid, has_side_effects=True, vmem_limit_bytes=60 << 20),
         name="reduce_all",
-    )(*terms, ff)
+    )(*terms)
+
+
+def spread_kernel(src, *refs):
+    outs, (s_s, s_r, loc) = refs[:3], refs[3:]
+    c, k, n = place()
+    cols = src.shape[-1] // 3
+    hello([(None, chip_at(c, r), k, n) for r in (1, 2, 3)])
+    at = pl.ds(pl.multiple_of(c * cols, 128), cols)
+    cps = []
+    for m in range(3):
+        cps.append(pltpu.make_async_copy(src.at[c, :, pl.ds(m * cols, cols)], outs[m].at[:, at], loc.at[m]))
+        for r in (1, 2, 3):
+            cc = chip_at(c, r)
+            cps.append(remote(src.at[cc, :, pl.ds(m * cols, cols)], outs[m].at[:, at], s_s.at[m, r - 1], s_r.at[m, r - 1], cc, k, n))
+    for cp in cps: cp.start()
+    for cp in cps: cp.wait()
+
+
+def spread(src, cid):
+    dma = pltpu.SemaphoreType.DMA
+    rows, cols = src.shape[1], src.shape[2] // 3
+    return pl.pallas_call(
+        spread_kernel,
+        out_shape=(jax.ShapeDtypeStruct((rows, CHIPS * cols), src.dtype),) * 3, in_specs=[ANY], out_specs=(ANY,) * 3,
+        scratch_shapes=[dma((3, 3)), dma((3, 3)), dma((3,))],
+        compiler_params=pltpu.CompilerParams(collective_id=cid, has_side_effects=True),
+        name="spread",
+    )(src)
 
 
 def fits(mesh):
@@ -1008,33 +1124,33 @@
     grad_y = cotangent.astype(f32) * valid_rows
     grad_y_low = grad_y.astype(bf16)
     gains = jnp.zeros((rows, 128), bf16).at[:, 0].set(norm_attn).at[:, 1].set(norm_mlp)
-    chunks = (rows, w_gate.shape[1] // 128, 128)
-    w_gate_up = jnp.stack([w_gate.reshape(chunks), w_up.reshape(chunks)], 2).reshape(rows, 2 * w_gate.shape[1])
-    w_qkv, w_out, gain_cols, ff_gate_up, ff_down, gy_all = gather_all(
-        nz, w_query, w_key, w_value, w_output, gains, w_gate_up, w_down, grad_y_low
-    )
-    ff_gate_up, ff_down = (w.reshape(-1, rows, w.shape[-1]) for w in (ff_gate_up, ff_down))
+    w_qkv, w_out, gain_cols, ff_gate_up, ff_down = gather_all(
+        nz, w_query, w_key, w_value, w_output, gains, w_gate, w_up, w_down
+    )
     gain_attn = gain_cols[:, 0].astype(f32)
     gain_mlp = gain_cols[:, 1].astype(f32)
 
     normed_attn = normalize(inputs)
     scaled_attn = (normed_attn * gain_attn).astype(bf16)
     qkv = jnp.dot(scaled_attn, w_qkv, preferred_element_type=f32)
-    query_rotated, key_rotated, value_reduced, log_totals, context = attend_all(qkv, tables)
+    query_rotated, key_rotated, value_reduced, log_totals, context, gy_all, ff_down = attend_all(
+        nz, qkv, tables, grad_y_low, ff_down
+    )
+    ff_gate_up, ff_down = (w.reshape(-1, rows, w.shape[-1]) for w in (ff_gate_up, ff_down))
     hidden = inputs + lax.dot_general(context, w_out, contract_last, preferred_element_type=f32)
     normed_mlp = normalize(hidden)
     scaled_mlp = (normed_mlp * gain_mlp).astype(bf16)
 
-    grad_x_parts, mlp_part, ff_sums = mlp_all(nz, scaled_mlp, gy_all, ff_gate_up, ff_down)
+    grad_x_parts, mlp_parts, mlp_cross, ff_sums = mlp_all(nz, scaled_mlp, gy_all, ff_gate_up, ff_down)
     grad_xn2 = jnp.sum(grad_x_parts.astype(f32), axis=0)
     grad_gain_mlp = jnp.sum(grad_xn2 * normed_mlp, axis=0)
     grad_hidden = grad_y + norm_back(grad_xn2 * gain_mlp, normed_mlp, hidden)
     grad_attn_low = grad_hidden.astype(bf16)
     grad_context = jnp.dot(grad_attn_low, w_out, preferred_element_type=f32).astype(bf16)
-    grad_query, grad_key, grad_value, mlp_parts = attend_back_all(
-        query_rotated, key_rotated, value_reduced, log_totals, grad_context, tables, mlp_part
-    )
-    output = (valid_rows * (hidden + jnp.sum(mlp_parts.astype(f32), axis=0))).astype(bf16)
+    grad_query, grad_key, grad_value, mlp_crossed = attend_back_all(
+        query_rotated, key_rotated, value_reduced, log_totals, grad_context, tables, mlp_cross
+    )
+    output = (valid_rows * (hidden + jnp.sum(mlp_parts.astype(f32), axis=0) + mlp_crossed.astype(f32))).astype(bf16)
     grad_qkv = jnp.concatenate([grad_query, grad_key.astype(bf16), grad_value.astype(bf16)], 1)
     grad_xn1 = lax.dot_general(grad_qkv, w_qkv, contract_last, preferred_element_type=f32)
     grad_gain_attn = jnp.sum(grad_xn1 * normed_attn, axis=0)
@@ -1045,20 +1161,16 @@
 
     ff_sums = lax.psum_scatter(ff_sums, "narrow", scatter_dimension=0, tiled=True)
     gain_terms = jnp.zeros((width, 128), f32).at[:, 0].set(grad_gain_attn).at[:, 1].set(grad_gain_mlp)
-    grad_w_output, grad_qkv_rows, gain_sums, ff_sums = reduce_all(
+    grad_w_output, grad_qkv_rows, gain_sums = reduce_all(
         nz,
         [
             over_rows(grad_attn_low, context).astype(bf16),
             over_rows(scaled_attn, grad_qkv).astype(bf16),
             gain_terms.astype(bf16),
         ],
-        ff_sums.reshape(CHIPS, rows, 3 * cols),
         3,
     )
-    grad_w_down = jnp.swapaxes(ff_sums[:, :, :cols], 0, 1).reshape(rows, CHIPS * cols).astype(f32)
-    grad_gate_up = jnp.swapaxes(ff_sums[:, :, cols:], 0, 1).reshape(rows, CHIPS * cols // 128, 2, 128).astype(f32)
-    grad_w_gate = grad_gate_up[:, :, 0].reshape(rows, CHIPS * cols)
-    grad_w_up = grad_gate_up[:, :, 1].reshape(rows, CHIPS * cols)
+    grad_w_down, grad_w_gate, grad_w_up = (g.astype(f32) for g in spread(ff_sums.reshape(CHIPS, rows, 3 * cols), 5))
     grad_w_output = grad_w_output.astype(f32)
     grad_w_query = grad_qkv_rows[:, :query_width].astype(f32)
     grad_w_key = grad_qkv_rows[:, query_width : query_width + key_width].astype(f32)

time: 722 us -> 642 us (0.89)
  waiting for transfers between devices: 37.7 us -> 0.02 us
  local copies, waits for them, and re-layouts: 36.5 us -> 9.15 us
  Pallas kernels: 556 us -> 531 us
  matrix products: 37.4 us -> 46.2 us
    reduce_scatter x1, waiting for transfers between devices: 37.7 us -> 0.01 us  [fast_device(): lax.psum_scatter(ff_sums, 'narrow', scatter_dimension=0, tiled=True)]
    pallas_call x1, Pallas kernels: 61 us -> 32 us  [attend_back_all(): pl.pallas_call(attend_back_kernel, grid=(KEY_VALUE_HEADS,), out_shape=(sh...]
    convert_element_type x3 -> x0, local copies, waits for them, and re-layouts: 8.63 us -> none  [the longest x2 7.4 us: fast_device(): jnp.swapaxes(ff_sums[:, :, cols:], 0, 1)]
    slice x1 -> x0, local copies, waits for them, and re-layouts: 7.7 us -> none  [fast_device(): grad_w_up = grad_gate_up[:, :, 1].reshape(rows, CHIPS * cols)]
    pallas_call x2 -> x3, Pallas kernels: 242 us -> 242 us  [the longest x1 162 us: gather_all(): pl.pallas_call(functools.partial(gather_kernel, nz), out_shape=(shape((wi...]
  transfers between devices with their start and end apart: 1 -> 1, of which waited for: 1 -> 0; matrix products, arithmetic and copies ran while one was open for 6% -> 8% of each run, Pallas kernels for 9% -> 24%
where the time goes in v4:
time: 642 us; the launch traced here: 638 us
  Pallas kernels  531 us (83%)
  matrix products  46.2 us (7%)
  other arithmetic  35.6 us (6%)
  between operations  15.4 us (2%)
  local copies, waits for them, and re-layouts  9.15 us (1%)
    pallas_call x1, Pallas kernels, gather_all(): pl.pallas_call(functools.partial(gather_kernel, nz), out_shape=(shape((wi...  162 us
    pallas_call x1, Pallas kernels, mlp_all(): pl.pallas_call(functools.partial(mlp_kernel, nz), out_shape=(blocks(width...  137 us
    pallas_call x1, Pallas kernels, reduce_all(): pl.pallas_call(functools.partial(reduce_kernel, nz, m), out_shape=tuple((...  120 us
    pallas_call x1, Pallas kernels, attend_all(): pl.pallas_call(functools.partial(attend_kernel, nz), grid=(KEY_VALUE_HEAD...  55.2 us
    pallas_call x1, Pallas kernels, attend_back_all(): pl.pallas_call(attend_back_kernel, grid=(KEY_VALUE_HEADS,), out_shape=(sh...  32 us
    pallas_call x1, Pallas kernels, spread(): pl.pallas_call(spread_kernel, out_shape=(jax.ShapeDtypeStruct((rows, CHIP...  24.6 us
    dot_general x2, matrix products, over_rows(): lax.dot_general(left, right, contract_first, preferred_element_type=f32)  17.4 us
  transfers between devices with their start and end apart: 1, of which 0 were waited for; matrix products, arithmetic and copies ran while one was open for 8% of the time, Pallas kernels for 24%

profile of v4, /device:TPU:0, one launch (start us, length us, event | category | flops | bytes accessed | tf_op | source)
XLA Modules:
  0.0 637.7 jit_solution(468564321677230631)
XLA Ops:
  7.2 0.6 compare_reduce_fusion.1
  7.9 0.6 compare_reduce_fusion
  9.2 0.7 convert_element_type.116
  9.9 1.7 fusion.10
  11.5 1.3 fusion.21
  13.0 1.3 fusion.20
  14.4 0.6 multiply_cosine_fusion
  15.1 0.2 maximum_bitcast_fusion
  15.4 0.6 copy-done.29
  16.0 162.4 %gather_all.1 = (bf16[2048,2560]{1,0:T(8,128)(2,1)}, bf16[2048,2048]{1,0:T(8,128)(2,1)}, bf16[2048,128]{1,0:T(8,128)(2,1)}, bf16[4,8,64,2816]{3,2,1,0:T(8,128)(2,1)}, bf16[4,64,1408]{2,1,0:T(8,128)(2,1)}) custom-call(bf16[64,2048]{1,0:T(8,128)(2,1)} %wq.1, bf16[64,256]{1,0:T(8,128)(2,1)} %wk.1, bf16[64,256]{1,0:T(8,128)(2,1)} %wv.1, bf16[64,2048]{1,0:T(8,128)(2,1)} %wo.1, ...), custom_call_target="tpu_custom_call" | custom-call | tf_op jit(solution)/shard_map/gather_all/pallas_call | solution.py:543
  178.5 1.7 convert_reduce_fusion.2
  180.5 0.3 fusion.11.gy
  180.8 0.7 copy-done.19
  181.5 6.6 %fusion.16.q_ref.k_ref.v_ref = f32[320,2560]{1,0:T(8,128)S(1)} fusion(bf16[2048,2560]{1,0:T(8,128)(2,1)} %get-tuple-element.86, bf16[320,2048]{1,0:T(8,128)(2,1)S(1)} %copy-done.19, f32[2048]{0:T(1024)S(1)} %get-tuple-element.116, f32[320]{0:T(512)S(1)} %add_rsqrt_fusion.1), kind=kOutput, calls=%fused_computation.34 | convolution fusion | flops 3358064640 | bytes 15082752 | tf_op jit(solution)/shard_map/dot_general | solution.py:1135
  188.1 55.2 %attend.1 = (bf16[320,2048]{1,0:T(8,128)(2,1)S(1)}, bf16[4,320,128]{2,1,0:T(8,128)(2,1)S(1)}, bf16[4,320,128]{2,1,0:T(8,128)(2,1)S(1)}, f32[4,320,128]{2,1,0:T(8...) custom-call(f32[320,2560]{1,0:T(8,128)S(1)} %fusion.16.q_ref.k_ref.v, ...), custom_call_target="tpu_custom_call" | custom-call | tf_op jit(solution)/shard_map/attend/pallas_call | solution.py:856
  243.4 0.7 copy-done.4
  244.1 0.7 copy-done.6
  244.8 9.6 %multiply_reduce_fusion.2 = (f32[320]{0:T(512)S(1)}, f32[320,2048]{1,0:T(8,128)S(1)}) fusion(bf16[320,2048]{1,0:T(8,128)(2,1)S(1)} %get-tuple-element.88, bf16[2048,2048]{1,0:T(8,128)(2,1)} %get-tuple-element.89, bf16[320,2048]{1,0:T(8,128)(2,1)S(1)} %copy-done.19), kind=kOutput, calls=%fused_computation.24 | convolution fusion | flops 2686975744 | bytes 13632768 | tf_op jit(solution)/shard_map/dot_general | solution.py:1140
  254.5 1.5 copy-done.14
  256.0 1.3 multiply_convert_fusion.1.x
  257.3 137.0 %mlp_all.1 = (bf16[4,320,2048]{2,1,0:T(8,128)(2,1)}, bf16[3,320,2048]{2,1,0:T(8,128)(2,1)}, bf16[320,2048]{1,0:T(8,128)(2,1)}, bf16[4,4,64,4224]{3,2,1,0:T(8,128)(2,1)}) custom-call(bf16[320,2048]{1,0:T(8,128)(2,1)} %multiply_convert_fusion.1.x, bf16[4,320,2048]{2,1,0:T(8,128)(2,1)} %copy-done.9, bf16[32,64,2816]{2,1,0:T(8,128)(2,1)} %bitcast.33, ...), custom_call_target="tpu_custom_call" | custom-call | flops 66437775360 | bytes 62914560 | tf_op jit(solution)/shard_map/mlp_all/pallas_call | solution.py:728
  394.4 4.0 convert_reduce_fusion
  398.4 0.8 multiply_reduce_fusion
  399.2 0.9 copy-done.24
  400.1 0.8 multiply_add_fusion
  400.9 0.9 slice-done.1
  401.8 3.0 convolution_convert_fusion.2.gc_ref
  404.9 32.0 %attend_back.1 = (bf16[320,2048]{1,0:T(8,128)(2,1)S(1)}, f32[320,256]{1,0:T(8,128)S(1)}, f32[320,256]{1,0:T(8,128)S(1)}, bf16[320,2048]{1,0:T(8,128)(2,1)S(1)}) custom-call(bf16[320,2048]{1,0:T(8,128)(2,1)S(1)} %get-tuple-element.94.q_ref, bf16[4,320,128]{2,1,0:T(8,128)(2,1)S(1)} %copy-done.5, bf16[4,320,128]{2,1,0:T(8,128)(2,1)S(1)} %copy-done.7, ...), custom_call_target="tpu_custom_call" | custom-call | tf_op jit(solution)/shard_map/attend_back/pallas_call | solution.py:940
  437.0 9.6 %fusion.9 = (f32[2048]{0:T(1024)S(1)}, f32[320]{0:T(512)S(1)}, f32[320,2048]{1,0:T(8,128)}) fusion(bf16[320,2048]{1,0:T(8,128)(2,1)S(1)} %copy-done.20, f32[320]{0:T(512)S(1)} %add_rsqrt_fusion.1, f32[2048]{0:T(1024)S(1)} %get-tuple-element.116, bf16[2048,2560]{1,0:T(8,128)(2,1)} %get-tuple-element.86, bf16[320,256]{1,0:T(8,128)(2,1)S(1)} %convert_element_type.129, ...), kind=kOutput, calls=%fused_computation.17 | convolution fusion | flops 3364943616 | bytes 16075264 | tf_op jit(solution)/shard_map/dot_general | solution.py:1155
  446.6 0.7 broadcast_select_fusion.1
  447.3 0.7 broadcast_select_fusion
  448.1 1.0 copy.28
  449.1 8.7 %convolution_convert_fusion.1 = bf16[2048,2048]{1,0:T(8,128)(2,1)} fusion(bf16[320,2048]{1,0:T(8,128)(2,1)S(1)} %copy-done.11, f32[320,2048]{1,0:T(8,128)} %copy-done.17), kind=kOutput, calls=%fused_computation.3 | convolution fusion | flops 2689204224 | bytes 12320768 | tf_op jit(solution)/shard_map/dot_general | solution.py:1160
  457.8 8.7 %convolution_convert_fusion = bf16[2048,2560]{1,0:T(8,128)(2,1)} fusion(bf16[320,256]{1,0:T(8,128)(2,1)S(1)} %convert_element_type.129, bf16[320,256]{1,0:T(8,128)(2,1)S(1)} %convert_element_type.128, bf16[320,2048]{1,0:T(8,128)(2,1)S(1)} %copy-done.13, bf16[320,2048]{1,0:T(8,128)(2,1)S(1)} %copy-done.21, f32[2048]{0:T(1024)S(1)} %get-tuple-element.116, ...), kind=kOutput, calls=%fused_computation | convolution fusion | flops 3368222720 | bytes 13444352 | tf_op jit(solution)/shard_map/dot_general | solution.py:1160
  466.5 120.1 %reduce_all.1 = (bf16[64,2048]{1,0:T(8,128)(2,1)}, bf16[64,2560]{1,0:T(8,128)(2,1)}, bf16[64,128]{1,0:T(8,128)(2,1)}) custom-call(bf16[4,2,256,2048]{3,2,1,0:T(8,128)(2,1)} %bitcast.28, bf16[4,2,256,2560]{3,2,1,0:T(8,128)(2,1)} %bitcast.27, bf16[4,2,256,128]{3,2,1,0:T(8,128)(2,1)} %bitcast.30), custom_call_target="tpu_custom_call" | custom-call | tf_op jit(solution)/shard_map/reduce_all/pallas_call | solution.py:1056
  586.6 1.8 convert_element_type.138
  588.4 1.5 convert_reduce_fusion.4
  589.9 1.4 slice_convert_fusion.1
  591.3 3.4 convert_reduce_fusion.1
  594.7 0.8 slice_convert_fusion
  595.6 1.9 multiply_convert_fusion
  597.5 0.7 copy-done.22
  598.2 0.8 copy-done.25
  599.0 2.3 fusion.8
  601.2 24.6 %spread.1 = (bf16[64,5632]{1,0:T(8,128)(2,1)}, bf16[64,5632]{1,0:T(8,128)(2,1)}, bf16[64,5632]{1,0:T(8,128)(2,1)}) custom-call(bf16[4,64,4224]{2,1,0:T(8,128)(2,1)} %bitcast.29), custom_call_target="tpu_custom_call" | custom-call | tf_op jit(solution)/shard_map/spread/pallas_call | solution.py:1086
  625.9 2.4 convert_element_type.141
  628.3 1.2 convert_element_type.142
  629.5 1.2 convert_element_type.143
  (77 shorter events, 1.1 us)
Async XLA Ops:
  7.2 594.1 %reduce-scatter.2.cloned.1.call-start = ((), (), s32[]{:S(2)}) async-start(), calls=%async_computation.1 | async-start | bytes 10813440 | tf_op jit(solution)/shard_map/reduce_scatter | solution.py:1162
  15.1 165.4 %copy-start.23 = (bf16[320,2048]{1,0:T(8,128)(2,1)S(1)}, bf16[320,2048]{1,0:T(8,128)(2,1)}, u32[]{:S(2)}) copy-start(bf16[320,2048]{1,0:T(8,128)(2,1)} %param.22) | copy-start | bytes 3932164
  15.4 0.6 copy-start.29
  180.2 1.3 copy-start.19
  181.5 6.6 %copy-start.1 = (bf16[4,64,1408]{2,1,0:T(8,128)(2,1)S(1)}, bf16[4,64,1408]{2,1,0:T(8,128)(2,1)}, u32[]{:S(2)}) copy-start(bf16[4,64,1408]{2,1,0:T(8,128)(2,1)} %get-tuple-element.87.gd_own) | copy-start | bytes 2162692
  243.4 0.7 copy-start.4
  244.1 0.7 copy-start.6
  244.8 9.7 %copy-start.2 = (f32[4,320,128]{2,1,0:T(8,128)}, f32[4,320,128]{2,1,0:T(8,128)S(1)}, u32[]{:S(2)}) copy-start(f32[4,320,128]{2,1,0:T(8,128)S(1)} %get-tuple-element.97.lse_ref) | copy-start | bytes 1966084
  244.8 9.7 %copy-start.8 = (bf16[4,8,64,1408]{3,2,1,0:T(8,128)(2,1)}, bf16[4,8,64,1408]{3,2,1,0:T(8,128)(2,1)S(1)}, u32[]{:S(2)}) copy-start(bf16[4,8,64,1408]{3,2,1,0:T(8,128)(2,1)S(1)} %get-tuple-element.92) | copy-start | bytes 17301508
  244.8 9.7 %copy-start.9 = (bf16[4,320,2048]{2,1,0:T(8,128)(2,1)}, bf16[4,320,2048]{2,1,0:T(8,128)(2,1)S(1)}, u32[]{:S(2)}) copy-start(bf16[4,320,2048]{2,1,0:T(8,128)(2,1)S(1)} %get-tuple-element.90.gy) | copy-start | bytes 15728644
  244.8 9.7 %copy-start.10 = (bf16[320,2048]{1,0:T(8,128)(2,1)}, bf16[320,2048]{1,0:T(8,128)(2,1)S(1)}, u32[]{:S(2)}) copy-start(bf16[320,2048]{1,0:T(8,128)(2,1)S(1)} %get-tuple-element.88) | copy-start | bytes 3932164
  254.5 1.5 copy-start.14
  394.3 4.1 copy-start.15
  394.3 6.6 %slice-start = ((s8[8388608]{0:T(1024)(128)(4,1)}), s8[4194304]{0:T(1024)(128)(4,1)S(1)}, s32[]{:S(2)}) async-start(s8[8388608]{0:T(1024)(128)(4,1)} %bitcast.34), calls=%async_computation.2 | async-start | bytes 8388608
  398.4 1.7 copy-start.24
  398.4 3.4 slice-start.1
  401.8 3.0 copy-start.17
  401.8 3.0 copy-start
  401.8 3.0 copy-start.3
  401.8 3.0 copy-start.5
  401.8 3.0 copy-start.7
  404.9 32.1 %copy-start.20 = (bf16[320,2048]{1,0:T(8,128)(2,1)S(1)}, bf16[320,2048]{1,0:T(8,128)(2,1)}, u32[]{:S(2)}) copy-start(bf16[320,2048]{1,0:T(8,128)(2,1)} %param.21) | copy-start | bytes 3932164
  436.9 9.7 %copy-start.12 = (bf16[320,2048]{1,0:T(8,128)(2,1)}, bf16[320,2048]{1,0:T(8,128)(2,1)S(1)}, u32[]{:S(2)}) copy-start(bf16[320,2048]{1,0:T(8,128)(2,1)S(1)} %get-tuple-element.101) | copy-start | bytes 3932164
  437.0 12.1 %copy-start.11 = (bf16[320,2048]{1,0:T(8,128)(2,1)S(1)}, bf16[320,2048]{1,0:T(8,128)(2,1)}, u32[]{:S(2)}) copy-start(bf16[320,2048]{1,0:T(8,128)(2,1)} %copy-done.10) | copy-start | bytes 3932164
  449.1 8.7 %copy-start.13 = (bf16[320,2048]{1,0:T(8,128)(2,1)S(1)}, bf16[320,2048]{1,0:T(8,128)(2,1)}, u32[]{:S(2)}) copy-start(bf16[320,2048]{1,0:T(8,128)(2,1)} %copy-done.12) | copy-start | bytes 3932164
  449.1 8.7 %copy-start.21 = (bf16[320,2048]{1,0:T(8,128)(2,1)S(1)}, bf16[320,2048]{1,0:T(8,128)(2,1)}, u32[]{:S(2)}) copy-start(bf16[320,2048]{1,0:T(8,128)(2,1)} %param.21) | copy-start | bytes 3932164
  591.3 3.4 copy-start.28
  591.3 4.2 copy-start.16
  595.6 1.9 copy-start.18
  595.6 2.6 copy-start.22
  595.6 3.4 copy-start.25
  625.8 2.4 copy-start.27
  625.8 3.6 copy-start.26
Sparse Core Ops, SparseCore 0:
  394.4 158.4 reduce-scatter.1

commit v5 on v4

--- a/solution.py
+++ b/solution.py
@@ -552,19 +552,31 @@
     )(wq, wk, wv, wo, gains, wg, wu, wd)
 
 
+def add_into(dst, *srcs):
+    rows = dst.shape[0]
+    step = 16
+    def body(i, carry):
+        at = pl.ds(pl.multiple_of(i * step, step), step)
+        total = dst[at, :].astype(jnp.float32)
+        for s in srcs: total = total + s[at, :].astype(jnp.float32)
+        dst[at, :] = total.astype(dst.dtype)
+        return carry
+    lax.fori_loop(0, rows // step, body, 0)
+
+
 HALVES = ((0, 0), (0, 1), (1, 0), (2, 0), (1, 1), (2, 1), (3, 0), (3, 1))
 
 
-def mlp_kernel(nz, x, gy, gu_hbm, gd_hbm, gx_parts, mlp_parts, mlp_cross, sums,
-               xs, gys, gu, gd, mix, ggu, gx, mo, xt, load, ag_s, ag_r, rs_s, rs_r, mo_s, mo_r, out, core_s, core_r, ready, done):
+def mlp_kernel(nz, x, gy, gu_hbm, gd_hbm, gx_parts, mlp_parts, mlp_cross, down_sums, sums,
+               xs, gys, gu, gd, mix, ggu, gx, mo, xt, zin, load, ag_s, ag_r, rs_s, rs_r, mo_s, mo_r, out, core_s, core_r, ready, done, z_s, z_r):
     c, k, n = place()
     f32, bf16 = jnp.float32, jnp.bfloat16
     slots, width = x.shape
     half = slots // 2
-    rows, cols = gd.shape[1:]
-    per_tile = nz
+    rows, cols = gd.shape[2:]
     tile = nz * rows
-    hello([(None, chip_at(c, r), k, n) for r in (1, 2, 3)] + [(None, c, 1 - k, n)])
+    hello([(None, chip_at(c, r), k, n) for r in (1, 2, 3)]
+          + [(None, c, 1 - k, n), (n > 0, c, k, n - 1), (n < nz - 1, c, k, n + 1)])
     def half_of(ref, h): return ref.at[pl.ds(h * half, half)]
     index = {place_: i for i, place_ in enumerate(HALVES)}
     sends = {}
@@ -572,12 +584,12 @@
         for r in (1, 2):
             i = index[r, h]
             sends[i] = remote(half_of(x, h), xs.at[i], ag_s.at[i], ag_r.at[i], chip_at(c, r), k, n)
-            sends[i].start()
+            if h == 0: sends[i].start()
     loads = [pltpu.make_async_copy(half_of(x, h), xs.at[h], load.at[h]) for h in range(2)]
     loads += [pltpu.make_async_copy(half_of(gy.at[r], h), gys.at[i], load.at[2 + i]) for i, (r, h) in enumerate(HALVES)]
     for cp in loads: cp.start()
     def weights(col, w, j):
-        return [pltpu.make_async_copy(a.at[:, :, pl.ds(first + col, w)], b.at[:, :, pl.ds(first + col, w)], load.at[10 + 3 * j + i])
+        return [pltpu.make_async_copy(a.at[:, :, :, pl.ds(first + col, w)], b.at[:, :, :, pl.ds(first + col, w)], load.at[10 + 3 * j + i])
                 for i, (a, b, first) in enumerate(((gu_hbm, gu, 0), (gu_hbm, gu, cols), (gd_hbm, gd, 0)))]
     for j in range(-(-cols // 256)):
         for cp in weights(j * 256, min(256, cols - j * 256), j): cp.start()
@@ -586,12 +598,9 @@
     for cp in loads: cp.wait()
 
     def columns(ref, at, size):
-        t = ref[:, :, pl.ds(at, size)]
-        return t.reshape(t.shape[0] * t.shape[1], size)
-
-    def some_rows(ref, i):
-        t = ref[pl.ds(i * (256 // rows), 256 // rows)]
-        return t.reshape(256, t.shape[2])
+        return ref[:, :, :, pl.ds(at, size)].reshape(width, size)
+
+    def some_rows(ref, i): return ref[i].reshape(tile, ref.shape[3])
 
     def to_owner(src, dst, i, s_s, s_r):
         r, h = HALVES[i]
@@ -602,11 +611,10 @@
 
     def block(r, carry):
         two = pl.ds(2 * r, 2)
-        for t in (1, 2):
-            @pl.when(r == t)
-            def _():
-                for i in (2 * t, 2 * t + 1): sends[i].wait_recv()
-                relays[{1: index[3, 0], 2: index[3, 1]}[t]].start()
+        @pl.when(r == 1)
+        def _():
+            for i in (2, 3): sends[i].wait_recv()
+            relays[index[3, 0]].start()
         @pl.when(r == 3)
         def _():
             for cp in relays.values(): cp.wait_recv()
@@ -632,21 +640,28 @@
             return carry
         lax.fori_loop(0, cols // 256, pair, 0)
         if cols % 256: chunk(cols // 256 * 256, cols % 256, cols // 256)
+        @pl.when(r == 0)
+        def _():
+            for i in (4, 5): sends[i].start()
+        @pl.when(r == 1)
+        def _():
+            for i in (4, 5): sends[i].wait_recv()
+            relays[index[3, 1]].start()
         def back(i, carry):
-            at = pl.ds(pl.multiple_of(i * 256, 256), 256)
+            at = pl.ds(pl.multiple_of(i * tile, 128), tile)
             put(gx, at, lax.dot_general(both(ggu), some_rows(gu, i), contract_last, preferred_element_type=f32))
             return carry
-        lax.fori_loop(0, width // 256, back, 0)
+        lax.fori_loop(0, CHIPS * CORES, back, 0)
         for t in range(CHIPS):
             @pl.when(r == t)
             def _():
                 for i in (2 * t, 2 * t + 1):
                     (to_owner(gx, gx_parts, i, rs_s, rs_r) if t else kept(gx, gx_parts.at[0], i, i)).start()
         def down(i, carry):
-            at = pl.ds(pl.multiple_of(i * 256, 256), 256)
+            at = pl.ds(pl.multiple_of(i * tile, 128), tile)
             put(mo, at, lax.dot_general(both(mix), some_rows(gd, i), contract_last, preferred_element_type=f32))
             return carry
-        lax.fori_loop(0, width // 256, down, 0)
+        lax.fori_loop(0, CHIPS * CORES, down, 0)
         for t in range(CHIPS):
             @pl.when(r == t)
             def _():
@@ -658,18 +673,16 @@
 
     pl.semaphore_signal(ready, inc=1, device_id={"wide": c * CORES + 1 - k, "narrow": n}, device_id_type=MESH)
     pl.semaphore_wait(ready, 1)
-    sent, came = pl.ds(0, CHIPS * nz), pl.ds(CHIPS * nz, CHIPS * nz)
+    sent, came = pl.ds(0, CHIPS), pl.ds(CHIPS, CHIPS)
     pairs = ((gys, mix, gd), (xs, ggu, gu))
 
     def tiles(total): return [(t * 256, min(256, total - t * 256)) for t in range(-(-total // 256))]
 
     def to_core(i, col, w, sem):
         ref = pairs[i][2]
-        return remote(ref.at[sent, :, pl.ds(col, w)], ref.at[came, :, pl.ds(col, w)], core_s.at[sem], core_r.at[sem], c, 1 - k, n)
-
-    def to_sums(i, t, sem):
-        ref = pairs[i][2]
-        return pltpu.make_async_copy(ref.at[pl.ds(CHIPS * nz + t * nz, nz)], sums.at[:, t, :, pl.ds(i * cols, ref.shape[-1])], done.at[sem])
+        return remote(ref.at[sent, :, :, pl.ds(col, w)], ref.at[came, :, :, pl.ds(col, w)], core_s.at[sem], core_r.at[sem], c, 1 - k, n)
+
+    def to_sums(t): return pltpu.make_async_copy(gu.at[CHIPS + t], sums.at[:, t], done.at[t])
 
     def each(i, body):
         total, base = pairs[i][2].shape[-1], 0 if i == 0 else len(tiles(cols))
@@ -687,39 +700,65 @@
                 xt[t * tile : (t + 1) * tile, r * slots : (r + 1) * slots] = src[2 * r : 2 * r + 2, :, at].reshape(slots, tile).T
         def body(col, w, sem):
             b = right[:, :, pl.ds(col, w)].reshape(CHIPS * slots, w)
-            use(i, col, w, sem, jnp.dot(xt[...], b, preferred_element_type=f32).reshape(CHIPS * nz, rows, w))
+            use(i, col, w, sem, jnp.dot(xt[...], b, preferred_element_type=f32).reshape(CHIPS, nz, rows, w))
         each(i, body)
 
     def theirs(i, col, w, sem, v):
-        pairs[i][2][sent, :, pl.ds(col, w)] = v.astype(bf16)
+        pairs[i][2][sent, :, :, pl.ds(col, w)] = v.astype(bf16)
         to_core(i, col, w, sem).start()
 
     def ours(i, col, w, sem, v):
         to_core(i, col, w, sem).wait_recv()
         ref = pairs[i][2]
-        here = (came, slice(None), pl.ds(col, w))
+        here = (came, slice(None), slice(None), pl.ds(col, w))
         ref[here] = (ref[here].astype(f32) + v).astype(bf16)
 
-    for i in range(2): terms(i, 1 - k, theirs)
-    for i in range(2):
-        terms(i, k, ours)
-        for t in range(CHIPS): to_sums(i, t, i * CHIPS + t).start()
+    def hop(way, j):
+        return remote(gd.at[came, j], zin.at[way, jnp.clip(j - n - 1 if way == 0 else n - 1 - j, 0, nz - 2)],
+                      z_s.at[way, j], z_r.at[way, j], c, k, n + 1 if way == 0 else n - 1)
+
+    def along(t):
+        for way in range(2):
+            hops = n if way == 0 else nz - 1 - n
+            j = jnp.clip(n + nz - 1 - t if way == 0 else t - hops, 0, nz - 1)
+            @pl.when((hops > 0) & (t >= hops))
+            def _():
+                hop(way, j).wait_recv()
+                for i in range(CHIPS):
+                    add_into(gd.at[CHIPS + i, j], zin.at[way, jnp.clip(j - n if way == 0 else n - j, 0, nz - 2), i])
+            @pl.when((t >= hops) & (j != n))
+            def _(): hop(way, j).start()
+
+    terms(0, 1 - k, theirs)
+    terms(0, k, ours)
+    along(0)
+    terms(1, 1 - k, theirs)
+    along(1)
+    terms(1, k, ours)
+    for t in range(CHIPS): to_sums(t).start()
+    for t in range(2, nz): along(t)
+    own_down = pltpu.make_async_copy(gd.at[came, n], down_sums, done.at[CHIPS])
+    own_down.start()
 
     for cp in (*sends.values(), *relays.values()): cp.wait_send()
     for i in range(2):
         kept(gx, gx_parts.at[0], i, i).wait()
         kept(mo, mlp_parts.at[0], i, 2 + i).wait()
         kept(mo, mlp_cross, 6 + i, 4 + i).wait()
-    for i in range(2):
-        each(i, lambda col, w, sem: to_core(i, col, w, sem).wait_send())
-        for t in range(CHIPS): to_sums(i, t, i * CHIPS + t).wait()
+    for i in range(2): each(i, lambda col, w, sem: to_core(i, col, w, sem).wait_send())
+    for t in range(CHIPS): to_sums(t).wait()
+    for j in range(nz):
+        for way in range(2):
+            @pl.when(n < j if way == 0 else n > j)
+            def _(): hop(way, j).wait_send()
+    own_down.wait()
     for i in range(2, 6): to_owner(mo, mlp_parts, i, mo_s, mo_r).wait()
     for i in range(2, 8): to_owner(gx, gx_parts, i, rs_s, rs_r).wait()
 
 
 def mlp_all(nz, x, gy, gu, gd):
     slots, width = x.shape
-    rows, cols = gd.shape[1:]
+    rows, cols = gd.shape[2:]
     bf, dma, vm = jnp.bfloat16, pltpu.SemaphoreType.DMA, pltpu.VMEM
     def blocks(w): return jax.ShapeDtypeStruct((CHIPS, slots, w), bf)
     def halves(w): return vm((2 * CHIPS, slots // 2, w), bf)
@@ -727,11 +766,12 @@
     flops = 2 * 9 * CHIPS * slots * width * cols
     return pl.pallas_call(
         functools.partial(mlp_kernel, nz),
-        out_shape=(blocks(width), jax.ShapeDtypeStruct((3, slots, width), bf), jax.ShapeDtypeStruct((slots, width), bf), jax.ShapeDtypeStruct((nz, CHIPS, rows, 3 * cols), bf)),
-        in_specs=[ANY] * 4, out_specs=(ANY,) * 4,
+        out_shape=(blocks(width), jax.ShapeDtypeStruct((3, slots, width), bf), jax.ShapeDtypeStruct((slots, width), bf),
+                   jax.ShapeDtypeStruct((CHIPS, rows, cols), bf), jax.ShapeDtypeStruct((nz, CHIPS, rows, 2 * cols), bf)),
+        in_specs=[ANY] * 4, out_specs=(ANY,) * 5,
         scratch_shapes=[halves(width), halves(width), vm(gu.shape, bf), vm(gd.shape, bf), halves(cols), halves(2 * cols), halves(width),
-                        halves(width), vm((CHIPS * nz * rows, CHIPS * slots), bf), dma((10 + 3 * tiles,)), dma((8,)), dma((8,)), dma((8,)), dma((8,)),
-                        dma((8,)), dma((8,)), dma((6,)), dma((3 * tiles,)), dma((3 * tiles,)), pltpu.SemaphoreType.REGULAR, dma((8,))],
+                        halves(width), vm((CHIPS * nz * rows, CHIPS * slots), bf), vm((2, nz - 1, CHIPS, rows, cols), bf), dma((10 + 3 * tiles,)), dma((8,)), dma((8,)), dma((8,)), dma((8,)),
+                        dma((8,)), dma((8,)), dma((6,)), dma((3 * tiles,)), dma((3 * tiles,)), pltpu.SemaphoreType.REGULAR, dma((CHIPS + 1,)), dma((2, nz)), dma((2, nz))],
         compiler_params=pltpu.CompilerParams(collective_id=1, has_side_effects=True, vmem_limit_bytes=62 << 20),
         cost_estimate=pl.CostEstimate(flops=flops, bytes_accessed=60 << 20, transcendentals=CHIPS * slots * cols),
         name="mlp_all",
@@ -951,64 +991,125 @@
     )(q, k, v, lse, grad_context, tables, part)
 
 
-def add_into(dst, *srcs):
-    rows = dst.shape[0]
-    step = 16
-    def body(i, carry):
-        at = pl.ds(pl.multiple_of(i * step, step), step)
-        total = dst[at, :].astype(jnp.float32)
-        for s in srcs: total = total + s[at, :].astype(jnp.float32)
-        dst[at, :] = total.astype(dst.dtype)
-        return carry
-    lax.fori_loop(0, rows // step, body, 0)
-
-
-def reduce_kernel(nz, items, *refs):
-    terms, outs, bufs = refs[:items], refs[items : 2 * items], refs[2 * items :]
-    took, away, zbuf = bufs[:items], bufs[items : 2 * items], bufs[2 * items : 3 * items]
-    core_s, core_r, half_s, half_r, main_s, main_r, z_s, z_r, loc = bufs[3 * items :]
+class Many:
+    def __init__(self, copies): self.copies = copies
+    def start(self):
+        for cp in self.copies: cp.start()
+    def wait(self):
+        for cp in self.copies: cp.wait()
+
+
+def columns_home(src, outs, c, k, n, send, recv, loc):
+    cols = src.shape[-1] // len(outs)
+    at = pl.ds(pl.multiple_of(c * cols, 128), cols)
+    local, away = [], []
+    for m, out in enumerate(outs):
+        local.append(pltpu.make_async_copy(src.at[c, :, pl.ds(m * cols, cols)], out.at[:, at], loc))
+        for r in (1, 2, 3):
+            cc = chip_at(c, r)
+            away.append(remote(src.at[cc, :, pl.ds(m * cols, cols)], out.at[:, at], send.at[m, r - 1], recv.at[m, r - 1], cc, k, n))
+    return away + [Many(local)]
+
+
+def gradient_kernel(nz, gal_hbm, ctx_hbm, xn_hbm, gq_hbm, wq_hbm, tok_hbm, gh_hbm, down, gain, gain_mlp,
+                    out0, out1, out2, grad_tokens, down_out,
+                    took0, took1, took2, away0, away1, away2, zbuf0, zbuf1, zbuf2, gal, ctx, xn, gq, wq, tok, gh, gx, xt, gain_row,
+                    core_s, core_r, half_s, half_r, main_s, main_r, z_s, z_r, ff_s, ff_r, load, loc):
+    f32, bf16 = jnp.float32, jnp.bfloat16
+    items = 3
+    outs, took, away, zbuf = (out0, out1, out2), (took0, took1, took2), (away0, away1, away2), (zbuf0, zbuf1, zbuf2)
     c, k, n = place()
     left, right = n > 0, n < nz - 1
     cx, cy, cd = (chip_at(c, r) for r in (1, 2, 3))
+    loads = [pltpu.make_async_copy(a, b, load.at[i]) for i, (a, b) in enumerate(
+        ((gal_hbm, gal), (ctx_hbm, ctx), (xn_hbm, xn), (gq_hbm, gq), (wq_hbm, wq), (tok_hbm, tok), (gh_hbm, gh)))]
+    for cp in loads: cp.start()
     hello([(None, cc, k, n) for cc in (cx, cy, cd)] + [(None, c, 1 - k, n), (left, c, k, n - 1), (right, c, k, n + 1)])
+    slots, width = gal.shape
     rows = outs[0].shape[0]
     part = nz * rows
     half = part // 2
     top, low = pl.ds(0, half), pl.ds(half, half)
     def arrive(a, at, size): return zbuf[a].at[pl.ds(at, size)]
-    own = [pltpu.make_async_copy(terms[a].at[:, k], away[a], loc.at[a]) for a in range(items)]
-    swap = [remote(terms[a].at[:, 1 - k], took[a], core_s.at[a], core_r.at[a], c, 1 - k, n) for a in range(items)]
-    for cp in own + swap: cp.start()
-    cross = [[remote(away[a].at[cd, top], arrive(a, 2 * part, half), half_s.at[a, 0], half_r.at[a, 0], cx, k, n),
-              remote(away[a].at[cd, low], arrive(a, 2 * part + half, half), half_s.at[a, 1], half_r.at[a, 1], cy, k, n)]
+    swap = [remote(away[a], took[a], core_s.at[a], core_r.at[a], c, 1 - k, n) for a in range(items)]
+    cross = [[remote(took[a].at[cd, top], arrive(a, 2 * part, half), half_s.at[a, 0], half_r.at[a, 0], cx, k, n),
+              remote(took[a].at[cd, low], arrive(a, 2 * part + half, half), half_s.at[a, 1], half_r.at[a, 1], cy, k, n)]
              for a in range(items)]
-    main = [[remote(away[a].at[cx, top], arrive(a, 0, half), main_s.at[a, 0], main_r.at[a, 0], cx, k, n),
-             remote(away[a].at[cy, low], arrive(a, part + half, half), main_s.at[a, 1], main_r.at[a, 1], cy, k, n),
-             remote(away[a].at[cx, low], arrive(a, half, half), main_s.at[a, 2], main_r.at[a, 2], cx, k, n),
-             remote(away[a].at[cy, top], arrive(a, part, half), main_s.at[a, 3], main_r.at[a, 3], cy, k, n)]
+    main = [[remote(took[a].at[cx, top], arrive(a, 0, half), main_s.at[a, 0], main_r.at[a, 0], cx, k, n),
+             remote(took[a].at[cy, low], arrive(a, part + half, half), main_s.at[a, 1], main_r.at[a, 1], cy, k, n),
+             remote(took[a].at[cx, low], arrive(a, half, half), main_s.at[a, 2], main_r.at[a, 2], cx, k, n),
+             remote(took[a].at[cy, top], arrive(a, part, half), main_s.at[a, 3], main_r.at[a, 3], cy, k, n)]
             for a in range(items)]
 
-    def cores(a):
-        own[a].wait()
+    def products(left_side, right_side, kk, put):
+        for t in range(CHIPS):
+            at = pl.ds(pl.multiple_of((t * CORES + kk) * part, 128), part)
+            xt[t * part : (t + 1) * part, :] = left_side[:, at].T
+        def step(j, carry):
+            at = pl.ds(pl.multiple_of(j * 256, 256), 256)
+            put(at, jnp.dot(xt[...], right_side[:, at], preferred_element_type=f32).reshape(CHIPS, part, 256))
+            return carry
+        lax.fori_loop(0, right_side.shape[1] // 256, step, 0)
+
+    def theirs(a, left_side, right_side):
+        def put(at, v): away[a][:, :, at] = v.astype(bf16)
+        products(left_side, right_side, 1 - k, put)
+        swap[a].start()
+
+    def ours(a, left_side, right_side):
         swap[a].wait_recv()
-        add_into(away[a].at[cd], took[a].at[cd])
+        def put(at, v): took[a][:, :, at] = (took[a][:, :, at].astype(f32) + v).astype(bf16)
+        products(left_side, right_side, k, put)
         for cp in cross[a]: cp.start()
-        for cc in (cx, cy, c): add_into(away[a].at[cc], took[a].at[cc])
+
+    def input_gradient():
+        loads[4].wait()
+        def step(j, carry):
+            at = pl.ds(pl.multiple_of(j * 256, 256), 256)
+            gx[:, at] = lax.dot_general(gq[...], wq[at, :], contract_last, preferred_element_type=f32)
+            return carry
+        lax.fori_loop(0, width // 256, step, 0)
+
+    def input_norm():
+        for cp in loads[5:]: cp.wait()
+        def step(j, total):
+            at = pl.ds(pl.multiple_of(j * 16, 16), 16)
+            x, g = tok[at, :].astype(f32), gx[at, :]
+            scale = lax.rsqrt(jnp.mean(x * x, axis=-1, keepdims=True) + norm_eps)
+            hat = x * scale
+            g1 = g * gain[...]
+            gh[at, :] = gh[at, :] + scale * (g1 - hat * jnp.mean(g1 * hat, axis=-1, keepdims=True))
+            t = g * hat
+            return total + t[0:8] + t[8:16]
+        total = lax.fori_loop(0, slots // 16, step, jnp.zeros((8, width), f32))
+        return jnp.sum(total, axis=0, keepdims=True)
+
+    def gains_swap(of_attn):
+        row = lax.broadcasted_iota(jnp.int32, (128, part), 0)
+        def columns_of(t, kk):
+            at = pl.ds(pl.multiple_of((t * CORES + kk) * part, 128), part)
+            return jnp.where(row == 0, gain_row[0:1, at], jnp.where(row == 1, gain_mlp[0:1, at], 0.0)).T
+        gain_row[0:1, :] = of_attn
+        for t in range(CHIPS): away[2][t] = columns_of(t, 1 - k).astype(bf16)
+        swap[2].start()
+        swap[2].wait_recv()
+        for t in range(CHIPS): took[2][t] = (took[2][t].astype(f32) + columns_of(t, k)).astype(bf16)
+        for cp in cross[2]: cp.start()
 
     def relay(a):
         cross[a][0].wait_recv()
-        add_into(away[a].at[cy, top], arrive(a, 2 * part, half))
+        add_into(took[a].at[cy, top], arrive(a, 2 * part, half))
         main[a][3].start()
         cross[a][1].wait_recv()
-        add_into(away[a].at[cx, low], arrive(a, 2 * part + half, half))
+        add_into(took[a].at[cx, low], arrive(a, 2 * part + half, half))
         for i in (2, 0, 1): main[a][i].start()
 
     def mine(a):
         for cp in main[a]: cp.wait_recv()
-        add_into(away[a].at[c], arrive(a, 0, part), arrive(a, part, part))
+        add_into(took[a].at[c], arrive(a, 0, part), arrive(a, part, part))
 
     def slot(a, way, j): return arrive(a, pl.multiple_of(2 * part + 2 * half + (way * nz + j) * rows, rows), rows)
-    def piece(a, j): return away[a].at[c, pl.ds(pl.multiple_of(j * rows, rows), rows)]
+    def piece(a, j): return took[a].at[c, pl.ds(pl.multiple_of(j * rows, rows), rows)]
     def hop(a, way, j):
         return remote(piece(a, j), slot(a, way, j), z_s.at[a, way, j], z_r.at[a, way, j], c, k, n + 1 if way == 0 else n - 1)
 
@@ -1028,14 +1129,25 @@
         for cp in done: cp.start()
         return done
 
-    stores = []
-    for a in range(items): cores(a)
-    for a in range(items): relay(a)
+    for cp in loads[:2]: cp.wait()
+    theirs(0, gal, ctx)
+    for cp in loads[2:4]: cp.wait()
+    theirs(1, xn, gq)
+    ours(0, gal, ctx)
+    ours(1, xn, gq)
+    input_gradient()
+    relay(0)
+    gains_swap(input_norm())
+    stores = [pltpu.make_async_copy(gh, grad_tokens, loc.at[items])]
+    stores[0].start()
+    for a in range(1, items): relay(a)
     mine(0)
     stores += along([0])
     for a in range(1, items): mine(a)
+    copies = columns_home(down, (down_out,), c, k, n, ff_s, ff_r, loc.at[items + 1])
+    for cp in copies: cp.start()
     stores += along(list(range(1, items)))
-    for cp in stores: cp.wait()
+    for cp in stores + copies: cp.wait()
     for a in range(items):
         swap[a].wait_send()
         for cp in cross[a] + main[a]: cp.wait_send()
@@ -1045,48 +1157,46 @@
                 def _(): hop(a, way, j).wait_send()
 
 
-def reduce_all(nz, terms, cid):
+def gradient_all(nz, gal, ctx, xn, gq, wq, tokens, grad_hidden, down, gain, gain_mlp, cid):
     dma, vm = pltpu.SemaphoreType.DMA, pltpu.VMEM
-    m = len(terms)
-    part = terms[0].shape[0] // (CHIPS * CORES)
+    bf16, f32 = jnp.bfloat16, jnp.float32
+    slots, width = gal.shape
+    m = 3
+    part = width // (CHIPS * CORES)
     rows = part // nz
+    widths = (ctx.shape[1], gq.shape[1], 128)
     shape = jax.ShapeDtypeStruct
-    terms = [t.reshape(CHIPS, CORES, part, t.shape[-1]) for t in terms]
-    blocks = [vm((CHIPS, part, t.shape[-1]), t.dtype) for t in terms]
+    blocks = [vm((CHIPS, part, w), bf16) for w in widths]
+    row = pl.BlockSpec((1, width), lambda: (0, 0))
     return pl.pallas_call(
-        functools.partial(reduce_kernel, nz, m),
-        out_shape=tuple(shape((rows, t.shape[-1]), t.dtype) for t in terms),
-        in_specs=[ANY] * m, out_specs=(ANY,) * m,
-        scratch_shapes=blocks + blocks + [vm((3 * part + 2 * nz * rows, t.shape[-1]), t.dtype) for t in terms]
-        + [dma((m,)), dma((m,)), dma((m, 2)), dma((m, 2)), dma((m, 4)), dma((m, 4)), dma((m, 2, nz)), dma((m, 2, nz)), dma((m,))],
-        compiler_params=pltpu.CompilerParams(collective_id=cid, has_side_effects=True, vmem_limit_bytes=60 << 20),
-        name="reduce_all",
-    )(*terms)
-
-
-def spread_kernel(src, *refs):
-    outs, (s_s, s_r, loc) = refs[:3], refs[3:]
+        functools.partial(gradient_kernel, nz),
+        out_shape=tuple(shape((rows, w), bf16) for w in widths) + (shape((slots, width), f32), shape((rows, CHIPS * down.shape[2]), bf16)),
+        in_specs=[ANY] * 8 + [row, row], out_specs=(ANY,) * (m + 2),
+        scratch_shapes=blocks + blocks + [vm((3 * part + 2 * nz * rows, w), bf16) for w in widths]
+        + [vm(gal.shape, bf16), vm(ctx.shape, bf16), vm(xn.shape, bf16), vm(gq.shape, bf16), vm(wq.shape, bf16), vm(tokens.shape, bf16),
+           vm((slots, width), f32), vm((slots, width), f32), vm((CHIPS * part, slots), bf16), vm((8, width), f32)]
+        + [dma((m,)), dma((m,)), dma((m, 2)), dma((m, 2)), dma((m, 4)), dma((m, 4)), dma((m, 2, nz)), dma((m, 2, nz)), dma((1, 3)), dma((1, 3)), dma((7,)), dma((m + 2,))],
+        compiler_params=pltpu.CompilerParams(collective_id=cid, has_side_effects=True, vmem_limit_bytes=62 << 20),
+        name="gradient_all",
+    )(gal, ctx, xn, gq, wq, tokens, grad_hidden, down, gain, gain_mlp)
+
+
+def spread_kernel(parts, src, *refs):
+    outs, (s_s, s_r, loc) = refs[:parts], refs[parts:]
     c, k, n = place()
-    cols = src.shape[-1] // 3
     hello([(None, chip_at(c, r), k, n) for r in (1, 2, 3)])
-    at = pl.ds(pl.multiple_of(c * cols, 128), cols)
-    cps = []
-    for m in range(3):
-        cps.append(pltpu.make_async_copy(src.at[c, :, pl.ds(m * cols, cols)], outs[m].at[:, at], loc.at[m]))
-        for r in (1, 2, 3):
-            cc = chip_at(c, r)
-            cps.append(remote(src.at[cc, :, pl.ds(m * cols, cols)], outs[m].at[:, at], s_s.at[m, r - 1], s_r.at[m, r - 1], cc, k, n))
+    cps = columns_home(src, outs, c, k, n, s_s, s_r, loc)
     for cp in cps: cp.start()
     for cp in cps: cp.wait()
 
 
-def spread(src, cid):
+def spread(src, parts, cid):
     dma = pltpu.SemaphoreType.DMA
-    rows, cols = src.shape[1], src.shape[2] // 3
+    rows, cols = src.shape[1], src.shape[2] // parts
     return pl.pallas_call(
-        spread_kernel,
-        out_shape=(jax.ShapeDtypeStruct((rows, CHIPS * cols), src.dtype),) * 3, in_specs=[ANY], out_specs=(ANY,) * 3,
-        scratch_shapes=[dma((3, 3)), dma((3, 3)), dma((3,))],
+        functools.partial(spread_kernel, parts),
+        out_shape=(jax.ShapeDtypeStruct((rows, CHIPS * cols), src.dtype),) * parts, in_specs=[ANY], out_specs=(ANY,) * parts,
+        scratch_shapes=[dma((parts, 3)), dma((parts, 3)), dma],
         compiler_params=pltpu.CompilerParams(collective_id=cid, has_side_effects=True),
         name="spread",
     )(src)
@@ -1136,12 +1246,12 @@
     query_rotated, key_rotated, value_reduced, log_totals, context, gy_all, ff_down = attend_all(
         nz, qkv, tables, grad_y_low, ff_down
     )
-    ff_gate_up, ff_down = (w.reshape(-1, rows, w.shape[-1]) for w in (ff_gate_up, ff_down))
+    ff_gate_up, ff_down = (w.reshape(CHIPS * CORES, nz, rows, w.shape[-1]) for w in (ff_gate_up, ff_down))
     hidden = inputs + lax.dot_general(context, w_out, contract_last, preferred_element_type=f32)
     normed_mlp = normalize(hidden)
     scaled_mlp = (normed_mlp * gain_mlp).astype(bf16)
 
-    grad_x_parts, mlp_parts, mlp_cross, ff_sums = mlp_all(nz, scaled_mlp, gy_all, ff_gate_up, ff_down)
+    grad_x_parts, mlp_parts, mlp_cross, down_sums, ff_sums = mlp_all(nz, scaled_mlp, gy_all, ff_gate_up, ff_down)
     grad_xn2 = jnp.sum(grad_x_parts.astype(f32), axis=0)
     grad_gain_mlp = jnp.sum(grad_xn2 * normed_mlp, axis=0)
     grad_hidden = grad_y + norm_back(grad_xn2 * gain_mlp, normed_mlp, hidden)
@@ -1152,25 +1262,12 @@
     )
     output = (valid_rows * (hidden + jnp.sum(mlp_parts.astype(f32), axis=0) + mlp_crossed.astype(f32))).astype(bf16)
     grad_qkv = jnp.concatenate([grad_query, grad_key.astype(bf16), grad_value.astype(bf16)], 1)
-    grad_xn1 = lax.dot_general(grad_qkv, w_qkv, contract_last, preferred_element_type=f32)
-    grad_gain_attn = jnp.sum(grad_xn1 * normed_attn, axis=0)
-    grad_tokens = grad_hidden + norm_back(grad_xn1 * gain_attn, normed_attn, inputs)
-
-    def over_rows(left, right):
-        return lax.dot_general(left, right, contract_first, preferred_element_type=f32)
-
     ff_sums = lax.psum_scatter(ff_sums, "narrow", scatter_dimension=0, tiled=True)
-    gain_terms = jnp.zeros((width, 128), f32).at[:, 0].set(grad_gain_attn).at[:, 1].set(grad_gain_mlp)
-    grad_w_output, grad_qkv_rows, gain_sums = reduce_all(
-        nz,
-        [
-            over_rows(grad_attn_low, context).astype(bf16),
-            over_rows(scaled_attn, grad_qkv).astype(bf16),
-            gain_terms.astype(bf16),
-        ],
-        3,
-    )
-    grad_w_down, grad_w_gate, grad_w_up = (g.astype(f32) for g in spread(ff_sums.reshape(CHIPS, rows, 3 * cols), 5))
+    grad_w_output, grad_qkv_rows, gain_sums, grad_tokens, grad_w_down = gradient_all(
+        nz, grad_attn_low, context, scaled_attn, grad_qkv, w_qkv, tokens, grad_hidden, down_sums, gain_attn[None], grad_gain_mlp[None], 3
+    )
+    grad_w_gate, grad_w_up = (g.astype(f32) for g in spread(ff_sums.reshape(CHIPS, rows, 2 * cols), 2, 5))
+    grad_w_down = grad_w_down.astype(f32)
     grad_w_output = grad_w_output.astype(f32)
     grad_w_query = grad_qkv_rows[:, :query_width].astype(f32)
     grad_w_key = grad_qkv_rows[:, query_width : query_width + key_width].astype(f32)

time: 642 us -> 621 us (0.967)
  matrix products: 46.2 us -> 19.3 us
    dot_general x3 -> x0, matrix products: 27 us -> none  [the longest x2 17.4 us: over_rows(): lax.dot_general(left, right, contract_first, preferred_element_type=f32)]
  transfers between devices with their start and end apart: 1 -> 1, of which waited for: 0 -> 0; matrix products, arithmetic and copies ran while one was open for 8% -> 4% of each run, Pallas kernels for 24% -> 25%
where the time goes in v5:
time: 621 us; the launch traced here: 612 us
  Pallas kernels  535 us (86%)
  other arithmetic  35.6 us (6%)
  matrix products  19.3 us (3%)
  between operations  15.6 us (3%)
  local copies, waits for them, and re-layouts  6.95 us (1%)
    pallas_call x1, Pallas kernels, gather_all(): pl.pallas_call(functools.partial(gather_kernel, nz), out_shape=(shape((wi...  162 us
    pallas_call x1, Pallas kernels, mlp_all(): pl.pallas_call(functools.partial(mlp_kernel, nz), out_shape=(blocks(width...  143 us
    pallas_call x1, Pallas kernels, gradient_all(): pl.pallas_call(functools.partial(gradient_kernel, nz), out_shape=tuple((s...  125 us
    pallas_call x1, Pallas kernels, attend_all(): pl.pallas_call(functools.partial(attend_kernel, nz), grid=(KEY_VALUE_HEAD...  55.2 us
    pallas_call x1, Pallas kernels, attend_back_all(): pl.pallas_call(attend_back_kernel, grid=(KEY_VALUE_HEADS,), out_shape=(sh...  30.3 us
    pallas_call x1, Pallas kernels, spread(): pl.pallas_call(functools.partial(spread_kernel, parts), out_shape=(jax.Sh...  18.5 us
  transfers between devices with their start and end apart: 1, of which 0 were waited for; matrix products, arithmetic and copies ran while one was open for 4% of the time, Pallas kernels for 25%

profile of v5, /device:TPU:0, one launch (start us, length us, event | category | flops | bytes accessed | tf_op | source)
XLA Modules:
  0.0 612.4 jit_solution(11831180667321894505)
XLA Ops:
  7.2 0.0 reduce-scatter.2.cloned.1.call-start
  7.2 0.6 compare_reduce_fusion.1
  7.9 0.6 compare_reduce_fusion
  9.2 0.7 convert_element_type.116
  9.9 1.7 fusion
  11.5 1.3 fusion.6
  12.9 0.1 copy.26
  13.0 1.3 fusion.7
  14.3 0.1 copy.27
  14.4 0.6 multiply_cosine_fusion
  15.1 0.2 maximum_bitcast_fusion
  15.3 0.1 scatter.9.gains
  15.4 0.6 copy-done.25
  16.0 162.4 %gather_all.1 = (bf16[2048,2560]{1,0:T(8,128)(2,1)}, bf16[2048,2048]{1,0:T(8,128)(2,1)}, bf16[2048,128]{1,0:T(8,128)(2,1)}, bf16[4,8,64,2816]{3,2,1,0:T(8,128)(2,1)}, bf16[4,64,1408]{2,1,0:T(8,128)(2,1)}) custom-call(bf16[64,2048]{1,0:T(8,128)(2,1)} %wq.1, bf16[64,256]{1,0:T(8,128)(2,1)} %wk.1, bf16[64,256]{1,0:T(8,128)(2,1)} %wv.1, bf16[64,2048]{1,0:T(8,128)(2,1)} %wo.1, ...), custom_call_target="tpu_custom_call" | custom-call | tf_op jit(solution)/shard_map/gather_all/pallas_call | solution.py:543
  178.5 1.8 convert_reduce_fusion.2
  180.3 0.1 negate_select_fusion
  180.4 0.2 maximum_bitcast_fusion.1
  180.6 0.3 fusion.3.gy
  180.9 0.4 fusion.2.xn_hbm
  181.3 6.7 %fusion.9.q_ref.k_ref.v_ref = f32[320,2560]{1,0:T(8,128)S(1)} fusion(bf16[320,2048]{1,0:T(8,128)(2,1)S(1)} %fusion.2.xn_hbm, bf16[2048,2560]{1,0:T(8,128)(2,1)} %get-tuple-element.64.wq_hbm), kind=kOutput, calls=%fused_computation.49 | convolution fusion | flops 3355443200 | bytes 15073280 | tf_op jit(solution)/shard_map/dot_general | solution.py:1245
  188.1 55.2 %attend.1 = (bf16[320,2048]{1,0:T(8,128)(2,1)S(1)}, bf16[4,320,128]{2,1,0:T(8,128)(2,1)S(1)}, bf16[4,320,128]{2,1,0:T(8,128)(2,1)S(1)}, f32[4,320,128]{2,1,0:T(8...) custom-call(f32[320,2560]{1,0:T(8,128)S(1)} %fusion.9.q_ref.k_ref.v_, ...), custom_call_target="tpu_custom_call" | custom-call | tf_op jit(solution)/shard_map/attend/pallas_call | solution.py:896
  243.3 1.0 copy-done.1
  244.4 0.7 copy-done.7
  245.1 0.7 copy-done.9
  245.8 9.7 %multiply_reduce_fusion.2 = (f32[320]{0:T(512)S(1)}, f32[320,2048]{1,0:T(8,128)S(1)}) fusion(bf16[320,2048]{1,0:T(8,128)(2,1)S(1)} %get-tuple-element.66.ctx_hbm, bf16[2048,2048]{1,0:T(8,128)(2,1)} %get-tuple-element.67, bf16[320,2048]{1,0:T(8,128)(2,1)S(1)} %copy-done.16), kind=kOutput, calls=%fused_computation.14 | convolution fusion | flops 2686975744 | bytes 13632768 | tf_op jit(solution)/shard_map/dot_general | solution.py:1250
  255.6 1.5 copy-done.13
  257.1 1.3 multiply_convert_fusion.1.x
  258.4 143.3 %mlp_all.1 = (bf16[4,320,2048]{2,1,0:T(8,128)(2,1)}, bf16[3,320,2048]{2,1,0:T(8,128)(2,1)}, bf16[320,2048]{1,0:T(8,128)(2,1)}, bf16[4,64,1408]{2,1,0:T(8,128)(2,1)}, bf16[4,4,64,2816]{3,2,1,0:T(8,128)(2,1)}) custom-call(bf16[320,2048]{1,0:T(8,128)(2,1)} %multiply_convert_fusion.1.x, bf16[4,320,2048]{2,1,0:T(8,128)(2,1)} %copy-done.12, ...), custom_call_target="tpu_custom_call" | custom-call | flops 66437775360 | bytes 62914560 | tf_op jit(solution)/shard_map/mlp_all/pallas_call | solution.py:767
  401.7 0.0 reduce-scatter.2.cloned.1.call-update
  401.8 4.0 convert_reduce_fusion
  405.8 1.3 multiply_reduce_fusion
  407.1 0.4 copy-done.20
  407.5 2.4 fusion.8
  410.0 2.9 convolution_convert_fusion.gc_ref
  413.0 30.3 %attend_back.1 = (bf16[320,2048]{1,0:T(8,128)(2,1)S(1)}, f32[320,256]{1,0:T(8,128)S(1)}, f32[320,256]{1,0:T(8,128)S(1)}, bf16[320,2048]{1,0:T(8,128)(2,1)S(1)}) custom-call(bf16[320,2048]{1,0:T(8,128)(2,1)S(1)} %copy-done.2, bf16[4,320,128]{2,1,0:T(8,128)(2,1)S(1)} %copy-done.8, bf16[4,320,128]{2,1,0:T(8,128)(2,1)S(1)} %copy-done.10, ...), custom_call_target="tpu_custom_call" | custom-call | tf_op jit(solution)/shard_map/attend_back/pallas_call | solution.py:980
  443.4 1.4 pad_maximum_fusion.gq_hbm
  444.8 125.2 %gradient_all.1 = (bf16[64,2048]{1,0:T(8,128)(2,1)}, bf16[64,2560]{1,0:T(8,128)(2,1)}, bf16[64,128]{1,0:T(8,128)(2,1)}, f32[320,2048]{1,0:T(8,128)}, bf16[64,5632]{1,0:T(8,128)(2,1)}) custom-call(bf16[320,2048]{1,0:T(8,128)(2,1)} %copy-done.17, bf16[320,2048]{1,0:T(8,128)(2,1)} %copy-done, bf16[320,2048]{1,0:T(8,128)(2,1)} %copy-done.18, ...), custom_call_target="tpu_custom_call" | custom-call | tf_op jit(solution)/shard_map/gradient_all/pallas_call | solution.py:1171
  570.0 1.8 convert_element_type.137
  571.8 2.3 convert_element_type.142
  574.1 0.7 convert_reduce_fusion.4
  574.8 0.7 slice_convert_fusion.1
  575.5 3.4 convert_reduce_fusion.1
  578.9 0.8 slice_convert_fusion
  579.7 1.8 multiply_convert_fusion
  581.6 18.5 %spread.1 = (bf16[64,5632]{1,0:T(8,128)(2,1)}, bf16[64,5632]{1,0:T(8,128)(2,1)}) custom-call(bf16[4,64,2816]{2,1,0:T(8,128)(2,1)} %bitcast.24), custom_call_target="tpu_custom_call" | custom-call | tf_op jit(solution)/shard_map/spread/pallas_call | solution.py:1196
  600.0 2.4 convert_element_type.140
  602.4 1.2 convert_element_type.141
  603.6 1.5 copy.31
  (64 shorter events, 0.2 us)
Async XLA Ops:
  7.2 574.4 %reduce-scatter.2.cloned.1.call-start = ((), (), s32[]{:S(2)}) async-start(), calls=%async_computation.1 | async-start | bytes 7208960 | tf_op jit(solution)/shard_map/reduce_scatter | solution.py:1265
  15.1 165.6 %copy-start.19 = (bf16[320,2048]{1,0:T(8,128)(2,1)S(1)}, bf16[320,2048]{1,0:T(8,128)(2,1)}, u32[]{:S(2)}) copy-start(bf16[320,2048]{1,0:T(8,128)(2,1)} %param.18) | copy-start | bytes 3932164
  15.4 0.6 copy-start.25
  178.5 2.4 copy-start.16
  180.3 1.0 copy-start.24
  181.3 6.8 %copy-start.18 = (bf16[320,2048]{1,0:T(8,128)(2,1)}, bf16[320,2048]{1,0:T(8,128)(2,1)S(1)}, u32[]{:S(2)}) copy-start(bf16[320,2048]{1,0:T(8,128)(2,1)S(1)} %fusion.2.xn_hbm) | copy-start | bytes 3932164
  181.3 6.8 %copy-start.4 = (bf16[4,64,1408]{2,1,0:T(8,128)(2,1)S(1)}, bf16[4,64,1408]{2,1,0:T(8,128)(2,1)}, u32[]{:S(2)}) copy-start(bf16[4,64,1408]{2,1,0:T(8,128)(2,1)} %get-tuple-element.65.gd_own) | copy-start | bytes 2162692
  243.3 1.1 copy-start.1
  244.4 0.7 copy-start.7
  245.1 0.7 copy-start.9
  245.8 9.7 %copy-start = (bf16[320,2048]{1,0:T(8,128)(2,1)}, bf16[320,2048]{1,0:T(8,128)(2,1)S(1)}, u32[]{:S(2)}) copy-start(bf16[320,2048]{1,0:T(8,128)(2,1)S(1)} %get-tuple-element.66.ctx_hbm) | copy-start | bytes 3932164
  245.8 9.7 %copy-start.5 = (f32[4,320,128]{2,1,0:T(8,128)}, f32[4,320,128]{2,1,0:T(8,128)S(1)}, u32[]{:S(2)}) copy-start(f32[4,320,128]{2,1,0:T(8,128)S(1)} %get-tuple-element.75.lse_ref) | copy-start | bytes 1966084
  245.8 9.7 %copy-start.11 = (bf16[4,8,64,1408]{3,2,1,0:T(8,128)(2,1)}, bf16[4,8,64,1408]{3,2,1,0:T(8,128)(2,1)S(1)}, u32[]{:S(2)}) copy-start(bf16[4,8,64,1408]{3,2,1,0:T(8,128)(2,1)S(1)} %get-tuple-element.70) | copy-start | bytes 17301508
  245.8 9.7 %copy-start.12 = (bf16[4,320,2048]{2,1,0:T(8,128)(2,1)}, bf16[4,320,2048]{2,1,0:T(8,128)(2,1)S(1)}, u32[]{:S(2)}) copy-start(bf16[4,320,2048]{2,1,0:T(8,128)(2,1)S(1)} %get-tuple-element.68.gy) | copy-start | bytes 15728644
  255.6 1.5 copy-start.13
  401.7 4.1 copy-start.14
  401.7 8.2 %slice-start = ((s8[8388608]{0:T(1024)(128)(4,1)}), s8[4194304]{0:T(1024)(128)(4,1)S(1)}, s32[]{:S(2)}) async-start(s8[8388608]{0:T(1024)(128)(4,1)} %bitcast.28), calls=%async_computation.2 | async-start | bytes 8388608
  405.8 1.7 copy-start.20
  405.8 4.2 slice-start.1
  410.0 3.0 copy-start.17
  410.0 3.0 copy-start.2
  410.0 3.0 copy-start.3
  410.0 3.0 copy-start.6
  410.0 3.0 copy-start.8
  410.0 3.0 copy-start.10
  570.0 4.2 copy-start.26
  570.0 4.8 copy-start.23
  575.5 4.2 copy-start.15
  581.6 22.1 %copy-start.21 = (f32[320,2048]{1,0:T(8,128)S(1)}, f32[320,2048]{1,0:T(8,128)}, u32[]{:S(2)}) copy-start(f32[320,2048]{1,0:T(8,128)} %get-tuple-element.121) | copy-start | bytes 7864324
  600.0 2.4 copy-start.22
Sparse Core Ops, SparseCore 0:
  401.9 100.7 reduce-scatter.1

commit v6 on v5

--- a/solution.py
+++ b/solution.py
@@ -380,6 +380,7 @@
 
 MESH = pl.DeviceIdType.MESH
 ANY = pl.BlockSpec(memory_space=pl.ANY)
+VMEM = pl.BlockSpec(memory_space=pltpu.VMEM)
 
 CHIPS, CORES = 4, 2
 
@@ -544,7 +545,7 @@
         functools.partial(gather_kernel, nz),
         out_shape=(shape((width, wq.shape[1] + 2 * wk.shape[1]), bf), shape((width, wo.shape[1]), bf), shape((width, gains.shape[1]), bf),
                    shape((CHIPS, CORES * nz, rows, 2 * cols), bf), shape((CHIPS, rows, cols), bf)),
-        in_specs=[ANY] * 8, out_specs=(ANY,) * 5,
+        in_specs=[VMEM] * 8, out_specs=(ANY,) * 5,
         scratch_shapes=[dma((8,)), dma((3, 3)), dma((3, 3)), dma((3, 2, nz)), dma((3, 2, nz)), dma((1, 2, nz)), dma((1, 2, nz)),
                         dma((3, 2)), dma((3, 2)), dma((3, 2)), dma((3, 2)), dma((3, 4)), dma((3, 4)), dma((nz,)), dma((nz,))],
         compiler_params=pltpu.CompilerParams(collective_id=0, has_side_effects=True),
@@ -810,39 +811,62 @@
     return jnp.concatenate([s[:, :clear], last], 1) if clear else last
 
 
-def attend_kernel(nz, q_ref, k_ref, v_ref, tab_ref, gy, gd_own, qr_ref, k_out, v_out, lse_ref, ctx_ref, gys, gd, ks, vs,
-                  loc, g_s, g_r, h_s, h_r, f_s, f_r, e_s, e_r):
+def scaled(x, gain):
+    return (x * lax.rsqrt(jnp.mean(x * x, axis=-1, keepdims=True) + norm_eps) * gain).astype(jnp.bfloat16)
+
+
+def attend_kernel(nz, tok, gain1, gain2, tab_ref, wq_hbm, wo_hbm, gy, gd_own,
+                  qr_ref, k_out, v_out, lse_ref, ctx_ref, xn1, hidden, xn2, gys, gd, ks, vs, wq, wo, qkv,
+                  load, loc, g_s, g_r, h_s, h_r, f_s, f_r, e_s, e_r):
     g = pl.program_id(0)
     f32, bf16 = jnp.float32, jnp.bfloat16
-    slots = q_ref.shape[0]
+    slots, width = tok.shape
     c, k, n = at = place()
     mine = [pltpu.make_async_copy(gd_own, gd.at[:, k * nz + n], loc.at[0]), pltpu.make_async_copy(gy, gys.at[0], loc.at[1])]
     line = Line(nz, at, (gd,), f_s, f_r, lambda ref, z: ref.at[:, k * nz + z])
     half = slots // 2
-    sends = [remote(gy, gys.at[r], g_s.at[r], g_r.at[r], chip_at(c, r), k, n) for r in (1, 2)]
+    sends = [remote(gy, gys.at[r], g_s.at[r - 1], g_r.at[r - 1], chip_at(c, r), k, n) for r in (1, 2)]
     relays = [remote(gys.at[1, pl.ds(0, half)], gys.at[3, pl.ds(0, half)], h_s.at[0], h_r.at[0], chip_at(c, 2), k, n),
               remote(gys.at[2, pl.ds(half, half)], gys.at[3, pl.ds(half, half)], h_s.at[1], h_r.at[1], chip_at(c, 1), k, n)]
     def twin(z):
         ref = gd.at[:, k * nz + z]
         return remote(ref, ref, e_s.at[z], e_r.at[z], c, 1 - k, n)
+    def load_q(j):
+        at = pl.ds(j * 256 if isinstance(j, int) else pl.multiple_of(j * 256, 256), 256)
+        return pltpu.make_async_copy(wq_hbm.at[:, at], wq.at[:, at], load.at[j])
     @pl.when(g == 0)
     def _():
         hello([(None, chip_at(c, r), k, n) for r in (1, 2)]
               + [(None, c, 1 - k, n), (n > 0, c, k, n - 1), (n < nz - 1, c, k, n + 1)])
         for cp in mine + sends: cp.start()
+        for j in range(wq.shape[1] // 256): load_q(j).start()
+        pltpu.make_async_copy(wo_hbm, wo, loc.at[2]).start()
         mine[0].wait()
         for way in range(2): line.start(0, 0, way)
         twin(n).start()
-    @pl.when(g == KEY_VALUE_HEADS - 1)
-    def _():
-        line.step(0, 1, lambda z: twin(z).start())
+        def norm(i, carry):
+            at = pl.ds(pl.multiple_of(i * 16, 16), 16)
+            xn1[at, :] = scaled(tok[at, :].astype(f32), gain1[...])
+            return carry
+        lax.fori_loop(0, slots // 16, norm, 0)
+        def project(j, carry):
+            load_q(j).wait()
+            at = pl.ds(pl.multiple_of(j * 256, 256), 256)
+            qkv[:, at] = jnp.dot(xn1[...], wq[:, at], preferred_element_type=f32)
+            return carry
+        lax.fori_loop(0, wq.shape[1] // 256, project, 0)
+    @pl.when(g == KEY_VALUE_HEADS - 2)
+    def _(): line.step(0, 1, lambda z: twin(z).start())
     @pl.when(g == 0)
     def _():
         ks[...] = jnp.zeros_like(ks)
         vs[...] = jnp.zeros_like(vs)
     lane = lax.broadcasted_iota(jnp.int32, (slots, PAIR), 1)
     tables = (tab_ref[0], tab_ref[1], tab_ref[2])
-    key, val = rotate(k_ref[...], tables), v_ref[...]
+    first = QUERY_HEADS * HEAD_SIZE
+    def pair_at(at): return pl.ds(pl.multiple_of(at, PAIR), PAIR)
+    key = rotate(qkv[:, pair_at(first + g // 2 * PAIR)], tables)
+    val = qkv[:, pair_at(first + KEY_VALUE_HEADS * HEAD_SIZE + g // 2 * PAIR)]
     odd = g % 2 == 1
     for x, own, stack, scale in ((key, k_out, ks, HEAD_SIZE ** -0.5), (val, v_out, vs, 1.0)):
         x = jnp.where(lane < HEAD_SIZE, jnp.where(odd, pltpu.roll(x, HEAD_SIZE, 1), x), 0.0).astype(bf16)
@@ -857,7 +881,7 @@
         for p in range(PAIRS):
             span = slice(p * PAIR, (p + 1) * PAIR)
             rows = slice(start, start + size)
-            q = rotate(q_ref[rows, span], tuple(t[rows] for t in tables)).astype(bf16)
+            q = rotate(qkv[rows, pair_at(g * REPEAT * HEAD_SIZE + p * PAIR)], tuple(t[rows] for t in tables)).astype(bf16)
             qr_ref[rows, span] = q
             ctx = jnp.zeros((size, PAIR), f32)
             for h in range(2):
@@ -869,13 +893,25 @@
                 lse = jnp.where(here == 2 * p + h, peak + jnp.log(total), lse)
                 probs = (e * (1.0 / total)).astype(bf16)
                 ctx = ctx + jnp.dot(probs, vs[h, 0:keys, :], preferred_element_type=f32)
-            ctx_ref[rows, span] = ctx.astype(bf16)
+            ctx_ref[rows, pair_at(g * REPEAT * HEAD_SIZE + p * PAIR)] = ctx.astype(bf16)
         lse_ref[0, start : start + size, :] = lse
     @pl.when(g == KEY_VALUE_HEADS - 1)
     def _():
         for cp in sends: cp.wait_recv()
         for cp in relays: cp.start()
-        for s in range(2, nz): line.step(0, s, lambda z: twin(z).start())
+        line.step(0, 2, lambda z: twin(z).start())
+        pltpu.make_async_copy(wo_hbm, wo, loc.at[2]).wait()
+        def project(j, carry):
+            at = pl.ds(pl.multiple_of(j * 256, 256), 256)
+            hidden[:, at] = tok[:, at].astype(f32) + lax.dot_general(ctx_ref[...], wo[at, :], contract_last, preferred_element_type=f32)
+            return carry
+        lax.fori_loop(0, width // 256, project, 0)
+        def norm(i, carry):
+            at = pl.ds(pl.multiple_of(i * 16, 16), 16)
+            xn2[at, :] = scaled(hidden[at, :], gain2[...])
+            return carry
+        lax.fori_loop(0, slots // 16, norm, 0)
+        for s in range(3, nz): line.step(0, s, lambda z: twin(z).start())
         for cp in relays: cp.wait()
         for z in range(nz): twin(z).wait()
         for cp in sends: cp.wait_send()
@@ -883,32 +919,32 @@
         line.finish(0)
 
 
-def attend_all(nz, qkv, tables, gy, gd_own):
-    slots = qkv.shape[0]
-    wide = REPEAT * HEAD_SIZE
-    dma = pltpu.SemaphoreType.DMA
-    first = QUERY_HEADS * HEAD_SIZE // PAIR
-    bf16 = jnp.bfloat16
+def attend_all(nz, tokens, gain1, gain2, tables, w_qkv, w_out, gy, gd_own):
+    slots, width = tokens.shape
+    dma, vm = pltpu.SemaphoreType.DMA, pltpu.VMEM
+    bf16, f32 = jnp.bfloat16, jnp.float32
     keys = -(-slots // 128) * 128
+    heads = QUERY_HEADS * HEAD_SIZE
     shape = jax.ShapeDtypeStruct
+    def fixed(*dims): return pl.BlockSpec(dims, lambda g: (0,) * len(dims))
     per_head = pl.BlockSpec((1, slots, PAIR), lambda g: (g, 0, 0))
-    wide_spec = pl.BlockSpec((slots, wide), lambda g: (0, g))
+    per_head_shape = (KEY_VALUE_HEADS, slots, PAIR)
     return pl.pallas_call(
         functools.partial(attend_kernel, nz),
         grid=(KEY_VALUE_HEADS,),
-        out_shape=(shape((slots, QUERY_HEADS * HEAD_SIZE), bf16), shape((KEY_VALUE_HEADS, slots, PAIR), bf16),
-                   shape((KEY_VALUE_HEADS, slots, PAIR), bf16), shape((KEY_VALUE_HEADS, slots, PAIR), jnp.float32),
-                   shape((slots, QUERY_HEADS * HEAD_SIZE), bf16), shape((CHIPS,) + gy.shape, bf16),
-                   shape((CHIPS, CORES * nz) + gd_own.shape[1:], bf16)),
-        in_specs=[wide_spec, pl.BlockSpec((slots, PAIR), lambda g: (0, first + g // 2)),
-                  pl.BlockSpec((slots, PAIR), lambda g: (0, first + KEY_VALUE_HEADS // 2 + g // 2)),
-                  pl.BlockSpec((3, slots, PAIR), lambda g: (0, 0, 0)), ANY, ANY],
-        out_specs=(wide_spec, per_head, per_head, per_head, wide_spec, ANY, ANY),
-        scratch_shapes=[pltpu.VMEM((2, keys, PAIR), bf16), pltpu.VMEM((2, keys, PAIR), bf16),
-                        dma((2,)), dma((3,)), dma((3,)), dma((2,)), dma((2,)), dma((1, 2, nz)), dma((1, 2, nz)), dma((nz,)), dma((nz,))],
-        compiler_params=pltpu.CompilerParams(collective_id=4, has_side_effects=True, vmem_limit_bytes=32 << 20),
+        out_shape=(shape((slots, heads), bf16), shape(per_head_shape, bf16), shape(per_head_shape, bf16), shape(per_head_shape, f32),
+                   shape((slots, heads), bf16), shape((slots, width), bf16), shape((slots, width), f32), shape((slots, width), bf16),
+                   shape((CHIPS,) + gy.shape, bf16), shape((CHIPS, CORES * nz) + gd_own.shape[1:], bf16)),
+        in_specs=[fixed(slots, width), fixed(1, width), fixed(1, width), fixed(3, slots, PAIR), ANY, ANY, fixed(*gy.shape), fixed(*gd_own.shape)],
+        out_specs=(pl.BlockSpec((slots, REPEAT * HEAD_SIZE), lambda g: (0, g)), per_head, per_head, per_head,
+                   fixed(slots, heads), fixed(slots, width), fixed(slots, width), fixed(slots, width), ANY, ANY),
+        scratch_shapes=[vm((2, keys, PAIR), bf16), vm((2, keys, PAIR), bf16), vm(w_qkv.shape, bf16), vm(w_out.shape, bf16),
+                        vm((slots, w_qkv.shape[1]), f32), dma((w_qkv.shape[1] // 256,)), dma((3,)), dma((2,)), dma((2,)), dma((2,)), dma((2,)),
+                        dma((1, 2, nz)), dma((1, 2, nz)), dma((nz,)), dma((nz,))],
+        compiler_params=pltpu.CompilerParams(collective_id=4, has_side_effects=True, vmem_limit_bytes=56 << 20),
+        cost_estimate=pl.CostEstimate(flops=4 * slots * width * heads, bytes_accessed=40 << 20, transcendentals=QUERY_HEADS * slots * slots),
         name="attend",
-    )(qkv, qkv, qkv, tables, gy, gd_own)
+    )(tokens, gain1, gain2, tables, w_qkv, w_out, gy, gd_own)
 
 
 def attend_back_kernel(q_ref, k_ref, v_ref, lse_ref, gc_ref, tab_ref, part, gq_ref, gk_ref, gv_ref, crossed,
@@ -1171,7 +1207,7 @@
     return pl.pallas_call(
         functools.partial(gradient_kernel, nz),
         out_shape=tuple(shape((rows, w), bf16) for w in widths) + (shape((slots, width), f32), shape((rows, CHIPS * down.shape[2]), bf16)),
-        in_specs=[ANY] * 8 + [row, row], out_specs=(ANY,) * (m + 2),
+        in_specs=[ANY] * 7 + [VMEM, row, row], out_specs=(ANY,) * (m + 2),
         scratch_shapes=blocks + blocks + [vm((3 * part + 2 * nz * rows, w), bf16) for w in widths]
         + [vm(gal.shape, bf16), vm(ctx.shape, bf16), vm(xn.shape, bf16), vm(gq.shape, bf16), vm(wq.shape, bf16), vm(tokens.shape, bf16),
            vm((slots, width), f32), vm((slots, width), f32), vm((CHIPS * part, slots), bf16), vm((8, width), f32)]
@@ -1195,7 +1231,7 @@
     rows, cols = src.shape[1], src.shape[2] // parts
     return pl.pallas_call(
         functools.partial(spread_kernel, parts),
-        out_shape=(jax.ShapeDtypeStruct((rows, CHIPS * cols), src.dtype),) * parts, in_specs=[ANY], out_specs=(ANY,) * parts,
+        out_shape=(jax.ShapeDtypeStruct((rows, CHIPS * cols), src.dtype),) * parts, in_specs=[VMEM], out_specs=(ANY,) * parts,
         scratch_shapes=[dma((parts, 3)), dma((parts, 3)), dma],
         compiler_params=pltpu.CompilerParams(collective_id=cid, has_side_effects=True),
         name="spread",
@@ -1228,7 +1264,6 @@
     rows = w_query.shape[0]
     query_width, key_width = w_query.shape[1], w_key.shape[1]
     cols = w_gate.shape[1] // CHIPS
-    inputs = tokens.astype(f32)
     valid_rows = (jnp.arange(slots) < lengths[0]).astype(f32)[:, None]
     tables = lane_tables(positions)
     grad_y = cotangent.astype(f32) * valid_rows
@@ -1240,17 +1275,11 @@
     gain_attn = gain_cols[:, 0].astype(f32)
     gain_mlp = gain_cols[:, 1].astype(f32)
 
-    normed_attn = normalize(inputs)
-    scaled_attn = (normed_attn * gain_attn).astype(bf16)
-    qkv = jnp.dot(scaled_attn, w_qkv, preferred_element_type=f32)
-    query_rotated, key_rotated, value_reduced, log_totals, context, gy_all, ff_down = attend_all(
-        nz, qkv, tables, grad_y_low, ff_down
+    query_rotated, key_rotated, value_reduced, log_totals, context, scaled_attn, hidden, scaled_mlp, gy_all, ff_down = attend_all(
+        nz, tokens, gain_attn[None], gain_mlp[None], tables, w_qkv, w_out, grad_y_low, ff_down
     )
     ff_gate_up, ff_down = (w.reshape(CHIPS * CORES, nz, rows, w.shape[-1]) for w in (ff_gate_up, ff_down))
-    hidden = inputs + lax.dot_general(context, w_out, contract_last, preferred_element_type=f32)
     normed_mlp = normalize(hidden)
-    scaled_mlp = (normed_mlp * gain_mlp).astype(bf16)
-
     grad_x_parts, mlp_parts, mlp_cross, down_sums, ff_sums = mlp_all(nz, scaled_mlp, gy_all, ff_gate_up, ff_down)
     grad_xn2 = jnp.sum(grad_x_parts.astype(f32), axis=0)
     grad_gain_mlp = jnp.sum(grad_xn2 * normed_mlp, axis=0)

time: 621 us -> 594 us (0.957)
  matrix products: 19.3 us -> 2.96 us
    pallas_call x1, Pallas kernels: 162 us -> 145 us  [gather_all(): pl.pallas_call(functools.partial(gather_kernel, nz), out_shape=(shape((wi...]
    dot_general x2 -> x0, matrix products: 16.4 us -> none  [the longest x1 9.67 us: fast_device(): lax.dot_general(context, w_out, contract_last, preferred_element_type=f32)]
    pallas_call x1, Pallas kernels: 55.2 us -> 63.3 us  [attend_all(): pl.pallas_call(functools.partial(attend_kernel, nz), grid=(KEY_VALUE_HEAD...]
  transfers between devices with their start and end apart: 1 -> 1, of which waited for: 0 -> 0; matrix products, arithmetic and copies ran while one was open for 4% -> 4% of each run, Pallas kernels for 25% -> 27%
where the time goes in v6:
time: 594 us; the launch traced here: 588 us
  Pallas kernels  530 us (89%)
  other arithmetic  34.8 us (6%)
  between operations  15.4 us (3%)
    pallas_call x1, Pallas kernels, gather_all(): pl.pallas_call(functools.partial(gather_kernel, nz), out_shape=(shape((wi...  145 us
    pallas_call x1, Pallas kernels, mlp_all(): pl.pallas_call(functools.partial(mlp_kernel, nz), out_shape=(blocks(width...  143 us
    pallas_call x1, Pallas kernels, gradient_all(): pl.pallas_call(functools.partial(gradient_kernel, nz), out_shape=tuple((s...  126 us
    pallas_call x1, Pallas kernels, attend_all(): pl.pallas_call(functools.partial(attend_kernel, nz), grid=(KEY_VALUE_HEAD...  63.3 us
    pallas_call x1, Pallas kernels, attend_back_all(): pl.pallas_call(attend_back_kernel, grid=(KEY_VALUE_HEADS,), out_shape=(sh...  32.1 us
    pallas_call x1, Pallas kernels, spread(): pl.pallas_call(functools.partial(spread_kernel, parts), out_shape=(jax.Sh...  19.9 us
  transfers between devices with their start and end apart: 1, of which 0 were waited for; matrix products, arithmetic and copies ran while one was open for 4% of the time, Pallas kernels for 27%

profile of v6, /device:TPU:0, one launch (start us, length us, event | category | flops | bytes accessed | tf_op | source)
XLA Modules:
  0.0 588.1 jit_solution(15909081498719491218)
XLA Ops:
  7.2 0.0 reduce-scatter.2.cloned.1.call-start
  7.2 0.6 compare_reduce_fusion.1
  7.9 0.6 compare_reduce_fusion
  9.2 0.7 convert_element_type.110
  9.9 1.3 fusion.3
  11.2 0.1 copy.26
  11.3 1.3 fusion.4
  12.6 0.1 copy.27
  12.7 0.6 multiply_cosine_fusion
  13.4 0.0 copy-start.9
  13.4 0.2 maximum_bitcast_fusion
  13.6 0.1 scatter.9.gains
  13.7 0.0 copy-start.15
  13.8 0.6 copy-done.15
  14.4 145.4 %gather_all.1 = (bf16[2048,2560]{1,0:T(8,128)(2,1)}, bf16[2048,2048]{1,0:T(8,128)(2,1)}, bf16[2048,128]{1,0:T(8,128)(2,1)}, bf16[4,8,64,2816]{3,2,1,0:T(8,128)(2,1)}, bf16[4,64,1408]{2,1,0:T(8,128)(2,1)}) custom-call(bf16[64,2048]{1,0:T(8,128)(2,1)} %wq.1, bf16[64,256]{1,0:T(8,128)(2,1)} %wk.1, bf16[64,256]{1,0:T(8,128)(2,1)} %wv.1, bf16[64,2048]{1,0:T(8,128)(2,1)} %wo.1, ...), custom_call_target="tpu_custom_call" | custom-call | tf_op jit(solution)/shard_map/gather_all/pallas_call | solution.py:544
  159.8 2.3 convert_reduce_fusion.2
  162.1 0.1 negate_select_fusion
  162.2 0.2 maximum_bitcast_fusion.1
  162.4 1.3 fusion.gy
  163.8 0.8 pad_maximum_fusion.1.tab_ref
  164.6 63.3 %attend.1 = (bf16[320,2048]{1,0:T(8,128)(2,1)}, bf16[4,320,128]{2,1,0:T(8,128)(2,1)}, bf16[4,320,128]{2,1,0:T(8,128)(2,1)}, f32[4,320,128]{2,1,0:T(8,128)}, bf16...) custom-call(bf16[320,2048]{1,0:T(8,128)(2,1)} %tok_hbm.1, ...), custom_call_target="tpu_custom_call" | custom-call | flops 5368709120 | bytes 41943040 | tf_op jit(solution)/shard_map/attend/pallas_call | solution.py:932
  227.8 143.3 %mlp_all.1 = (bf16[4,320,2048]{2,1,0:T(8,128)(2,1)}, bf16[3,320,2048]{2,1,0:T(8,128)(2,1)}, bf16[320,2048]{1,0:T(8,128)(2,1)}, bf16[4,64,1408]{2,1,0:T(8,128)(2,1)}, bf16[4,4,64,2816]{3,2,1,0:T(8,128)(2,1)}) custom-call(bf16[320,2048]{1,0:T(8,128)(2,1)} %get-tuple-element.71.x, bf16[4,320,2048]{2,1,0:T(8,128)(2,1)} %get-tuple-element.72.gy, ...), custom_call_target="tpu_custom_call" | custom-call | flops 66437775360 | bytes 62914560 | tf_op jit(solution)/shard_map/mlp_all/pallas_call | solution.py:768
  371.1 0.0 reduce-scatter.2.cloned.1.call-update
  371.2 1.7 copy-done.6
  372.9 0.3 multiply_reduce_fusion.2
  373.1 0.0 copy-start.10
  373.2 4.0 convert_reduce_fusion
  377.2 0.0 slice-start
  377.2 1.3 multiply_reduce_fusion
  378.5 0.0 copy-done.10
  378.5 2.4 fusion.5
  381.0 0.5 slice-done.1
  381.5 3.0 convolution_convert_fusion.gc_ref
  384.5 0.0 copy-done.8
  384.6 32.1 %attend_back.1 = (bf16[320,2048]{1,0:T(8,128)(2,1)S(1)}, f32[320,256]{1,0:T(8,128)S(1)}, f32[320,256]{1,0:T(8,128)S(1)}, bf16[320,2048]{1,0:T(8,128)(2,1)S(1)}) custom-call(bf16[320,2048]{1,0:T(8,128)(2,1)S(1)} %copy-done.1, bf16[4,320,128]{2,1,0:T(8,128)(2,1)S(1)} %copy-done.4, bf16[4,320,128]{2,1,0:T(8,128)(2,1)S(1)} %copy-done.5, ...), custom_call_target="tpu_custom_call" | custom-call | tf_op jit(solution)/shard_map/attend_back/pallas_call | solution.py:1016
  416.7 1.4 pad_maximum_fusion.gq_hbm
  418.1 126.1 %gradient_all.1 = (bf16[64,2048]{1,0:T(8,128)(2,1)}, bf16[64,2560]{1,0:T(8,128)(2,1)}, bf16[64,128]{1,0:T(8,128)(2,1)}, f32[320,2048]{1,0:T(8,128)}, bf16[64,5632]{1,0:T(8,128)(2,1)}) custom-call(bf16[320,2048]{1,0:T(8,128)(2,1)} %copy-done.8, bf16[320,2048]{1,0:T(8,128)(2,1)} %get-tuple-element.83.ctx_hbm, bf16[320,2048]{1,0:T(8,128)(2,1)} %get-tuple-element.84.xn_hbm, ...), custom_call_target="tpu_custom_call" | custom-call | tf_op jit(solution)/shard_map/gradient_all/pallas_call | solution.py:1207
  544.2 1.8 convert_element_type.128
  546.0 2.3 convert_element_type.133
  548.4 0.7 convert_reduce_fusion.4
  549.1 0.7 slice_convert_fusion.1
  549.7 3.4 convert_reduce_fusion.1
  553.1 0.8 slice_convert_fusion
  553.9 1.9 multiply_convert_fusion
  555.8 19.9 %spread.1 = (bf16[64,5632]{1,0:T(8,128)(2,1)}, bf16[64,5632]{1,0:T(8,128)(2,1)}) custom-call(bf16[4,64,2816]{2,1,0:T(8,128)(2,1)} %bitcast.22), custom_call_target="tpu_custom_call" | custom-call | tf_op jit(solution)/shard_map/spread/pallas_call | solution.py:1232
  575.7 2.4 convert_element_type.131
  578.1 1.2 convert_element_type.132
  579.3 1.5 copy.31
  (39 shorter events, 0.1 us)
Async XLA Ops:
  7.2 548.6 %reduce-scatter.2.cloned.1.call-start = ((), (), s32[]{:S(2)}) async-start(), calls=%async_computation.1 | async-start | bytes 7208960 | tf_op jit(solution)/shard_map/reduce_scatter | solution.py:1294
  13.4 149.0 %copy-start.9 = (bf16[320,2048]{1,0:T(8,128)(2,1)S(1)}, bf16[320,2048]{1,0:T(8,128)(2,1)}, u32[]{:S(2)}) copy-start(bf16[320,2048]{1,0:T(8,128)(2,1)} %param.18) | copy-start | bytes 3932164
  13.7 0.6 copy-start.15
  371.1 1.7 copy-start.6
  373.1 4.1 copy-start.14
  373.1 5.4 copy-start.10
  377.2 3.8 slice-start
  378.5 3.0 slice-start.1
  381.0 3.5 copy-start.8
  381.5 3.0 copy-start
  381.5 3.0 copy-start.1
  381.5 3.0 copy-start.2
  381.5 3.0 copy-start.3
  381.5 3.0 copy-start.4
  381.5 3.0 copy-start.5
  544.2 4.2 copy-start.16
  544.2 4.8 copy-start.13
  549.7 4.2 copy-start.7
  555.8 23.5 %copy-start.11 = (f32[320,2048]{1,0:T(8,128)S(1)}, f32[320,2048]{1,0:T(8,128)}, u32[]{:S(2)}) copy-start(f32[320,2048]{1,0:T(8,128)} %get-tuple-element.125) | copy-start | bytes 7864324
  575.7 2.4 copy-start.12
Sparse Core Ops, SparseCore 0:
  371.3 100.9 reduce-scatter.1

commit v7 on v6

--- a/solution.py
+++ b/solution.py
@@ -855,7 +855,7 @@
             qkv[:, at] = jnp.dot(xn1[...], wq[:, at], preferred_element_type=f32)
             return carry
         lax.fori_loop(0, wq.shape[1] // 256, project, 0)
-    @pl.when(g == KEY_VALUE_HEADS - 2)
+    @pl.when(g == 1)
     def _(): line.step(0, 1, lambda z: twin(z).start())
     @pl.when(g == 0)
     def _():
@@ -1027,30 +1027,40 @@
     )(q, k, v, lse, grad_context, tables, part)
 
 
-class Many:
-    def __init__(self, copies): self.copies = copies
-    def start(self):
-        for cp in self.copies: cp.start()
-    def wait(self):
-        for cp in self.copies: cp.wait()
-
-
-def columns_home(src, outs, c, k, n, send, recv, loc):
-    cols = src.shape[-1] // len(outs)
-    at = pl.ds(pl.multiple_of(c * cols, 128), cols)
-    local, away = [], []
-    for m, out in enumerate(outs):
-        local.append(pltpu.make_async_copy(src.at[c, :, pl.ds(m * cols, cols)], out.at[:, at], loc))
-        for r in (1, 2, 3):
-            cc = chip_at(c, r)
-            away.append(remote(src.at[cc, :, pl.ds(m * cols, cols)], out.at[:, at], send.at[m, r - 1], recv.at[m, r - 1], cc, k, n))
-    return away + [Many(local)]
-
-
-def gradient_kernel(nz, gal_hbm, ctx_hbm, xn_hbm, gq_hbm, wq_hbm, tok_hbm, gh_hbm, down, gain, gain_mlp,
-                    out0, out1, out2, grad_tokens, down_out,
+class SumLine:
+    def __init__(self, nz, at, piece, slot, send, recv):
+        self.nz, self.at, self.piece, self.slot, self.send, self.recv = nz, at, piece, slot, send, recv
+
+    def _hop(self, a, way, j):
+        c, k, n = self.at
+        i = jnp.clip(j - n - 1 if way == 0 else n - 1 - j, 0, self.nz - 2)
+        return remote(self.piece(a, j), self.slot(a, way, i), self.send.at[a, way, j], self.recv.at[a, way, j],
+                      c, k, n + 1 if way == 0 else n - 1)
+
+    def step(self, some, t):
+        nz, n = self.nz, self.at[2]
+        for way in range(2):
+            hops = n if way == 0 else nz - 1 - n
+            j = jnp.clip(n + nz - 1 - t if way == 0 else t - hops, 0, nz - 1)
+            for a in some:
+                @pl.when((hops > 0) & (t >= hops))
+                def _():
+                    self._hop(a, way, j).wait_recv()
+                    add_into(self.piece(a, j), self.slot(a, way, jnp.clip(j - n if way == 0 else n - j, 0, nz - 2)))
+                @pl.when((t >= hops) & (j != n))
+                def _(): self._hop(a, way, j).start()
+
+    def finish(self, a):
+        n = self.at[2]
+        for j in range(self.nz):
+            for way in range(2):
+                @pl.when(n < j if way == 0 else n > j)
+                def _(): self._hop(a, way, j).wait_send()
+
+
+def gradient_kernel(nz, gal_hbm, ctx_hbm, xn_hbm, gq_hbm, wq_hbm, tok_hbm, gh_hbm, gain, gain_mlp, out0, out1, out2, grad_tokens,
                     took0, took1, took2, away0, away1, away2, zbuf0, zbuf1, zbuf2, gal, ctx, xn, gq, wq, tok, gh, gx, xt, gain_row,
-                    core_s, core_r, half_s, half_r, main_s, main_r, z_s, z_r, ff_s, ff_r, load, loc):
+                    core_s, core_r, half_s, half_r, main_s, main_r, z_s, z_r, load, loc):
     f32, bf16 = jnp.float32, jnp.bfloat16
     items = 3
     outs, took, away, zbuf = (out0, out1, out2), (took0, took1, took2), (away0, away1, away2), (zbuf0, zbuf1, zbuf2)
@@ -1062,7 +1072,7 @@
     for cp in loads: cp.start()
     hello([(None, cc, k, n) for cc in (cx, cy, cd)] + [(None, c, 1 - k, n), (left, c, k, n - 1), (right, c, k, n + 1)])
     slots, width = gal.shape
-    rows = outs[0].shape[0]
+    rows = out0.shape[0]
     part = nz * rows
     half = part // 2
     top, low = pl.ds(0, half), pl.ds(half, half)
@@ -1144,26 +1154,8 @@
         for cp in main[a]: cp.wait_recv()
         add_into(took[a].at[c], arrive(a, 0, part), arrive(a, part, part))
 
-    def slot(a, way, j): return arrive(a, pl.multiple_of(2 * part + 2 * half + (way * nz + j) * rows, rows), rows)
-    def piece(a, j): return took[a].at[c, pl.ds(pl.multiple_of(j * rows, rows), rows)]
-    def hop(a, way, j):
-        return remote(piece(a, j), slot(a, way, j), z_s.at[a, way, j], z_r.at[a, way, j], c, k, n + 1 if way == 0 else n - 1)
-
-    def along(some):
-        for t in range(nz):
-            for way in range(2):
-                hops = n if way == 0 else nz - 1 - n
-                j = jnp.clip(n + nz - 1 - t if way == 0 else t - hops, 0, nz - 1)
-                for a in some:
-                    @pl.when((hops > 0) & (t >= hops))
-                    def _():
-                        hop(a, way, j).wait_recv()
-                        add_into(piece(a, j), slot(a, way, j))
-                    @pl.when((t >= hops) & (j != n))
-                    def _(): hop(a, way, j).start()
-        done = [pltpu.make_async_copy(piece(a, n), outs[a], loc.at[a]) for a in some]
-        for cp in done: cp.start()
-        return done
+    line = SumLine(nz, (c, k, n), lambda a, j: took[a].at[c, pl.ds(pl.multiple_of(j * rows, rows), rows)],
+                   lambda a, way, i: arrive(a, pl.multiple_of(2 * part + 2 * half + (way * (nz - 1) + i) * rows, rows), rows), z_s, z_r)
 
     for cp in loads[:2]: cp.wait()
     theirs(0, gal, ctx)
@@ -1178,22 +1170,21 @@
     stores[0].start()
     for a in range(1, items): relay(a)
     mine(0)
-    stores += along([0])
-    for a in range(1, items): mine(a)
-    copies = columns_home(down, (down_out,), c, k, n, ff_s, ff_r, loc.at[items + 1])
-    for cp in copies: cp.start()
-    stores += along(list(range(1, items)))
-    for cp in stores + copies: cp.wait()
+    for t in range(nz): line.step([0], t)
+    stores.append(pltpu.make_async_copy(line.piece(0, n), outs[0], loc.at[0]))
+    stores[-1].start()
+    for a in range(1, items):
+        mine(a)
+        stores.append(pltpu.make_async_copy(took[a].at[c], outs[a], loc.at[a]))
+        stores[-1].start()
+    for cp in stores: cp.wait()
     for a in range(items):
         swap[a].wait_send()
         for cp in cross[a] + main[a]: cp.wait_send()
-        for j in range(nz):
-            for way in range(2):
-                @pl.when(n < j if way == 0 else n > j)
-                def _(): hop(a, way, j).wait_send()
-
-
-def gradient_all(nz, gal, ctx, xn, gq, wq, tokens, grad_hidden, down, gain, gain_mlp, cid):
+    line.finish(0)
+
+
+def gradient_all(nz, gal, ctx, xn, gq, wq, tokens, grad_hidden, gain, gain_mlp, cid):
     dma, vm = pltpu.SemaphoreType.DMA, pltpu.VMEM
     bf16, f32 = jnp.bfloat16, jnp.float32
     slots, width = gal.shape
@@ -1206,36 +1197,79 @@
     row = pl.BlockSpec((1, width), lambda: (0, 0))
     return pl.pallas_call(
         functools.partial(gradient_kernel, nz),
-        out_shape=tuple(shape((rows, w), bf16) for w in widths) + (shape((slots, width), f32), shape((rows, CHIPS * down.shape[2]), bf16)),
-        in_specs=[ANY] * 7 + [VMEM, row, row], out_specs=(ANY,) * (m + 2),
+        out_shape=(shape((rows, widths[0]), bf16),) + tuple(shape((part, w), bf16) for w in widths[1:]) + (shape((slots, width), f32),),
+        in_specs=[ANY] * 7 + [row, row], out_specs=(ANY,) * (m + 1),
         scratch_shapes=blocks + blocks + [vm((3 * part + 2 * nz * rows, w), bf16) for w in widths]
         + [vm(gal.shape, bf16), vm(ctx.shape, bf16), vm(xn.shape, bf16), vm(gq.shape, bf16), vm(wq.shape, bf16), vm(tokens.shape, bf16),
            vm((slots, width), f32), vm((slots, width), f32), vm((CHIPS * part, slots), bf16), vm((8, width), f32)]
-        + [dma((m,)), dma((m,)), dma((m, 2)), dma((m, 2)), dma((m, 4)), dma((m, 4)), dma((m, 2, nz)), dma((m, 2, nz)), dma((1, 3)), dma((1, 3)), dma((7,)), dma((m + 2,))],
+        + [dma((m,)), dma((m,)), dma((m, 2)), dma((m, 2)), dma((m, 4)), dma((m, 4)), dma((m, 2, nz)), dma((m, 2, nz)), dma((7,)), dma((m + 1,))],
         compiler_params=pltpu.CompilerParams(collective_id=cid, has_side_effects=True, vmem_limit_bytes=62 << 20),
         name="gradient_all",
-    )(gal, ctx, xn, gq, wq, tokens, grad_hidden, down, gain, gain_mlp)
-
-
-def spread_kernel(parts, src, *refs):
-    outs, (s_s, s_r, loc) = refs[:parts], refs[parts:]
+    )(gal, ctx, xn, gq, wq, tokens, grad_hidden, gain, gain_mlp)
+
+
+def finish_kernel(nz, down, gu, part1, part2, out_q, out_k, out_v, out_gain, out_d, out_g, out_u,
+                  acc1, acc2, in1, in2, ff, wide1, wide2, wide_ff, z_s, z_r, ff_s, ff_r, load, loc):
+    f32 = jnp.float32
     c, k, n = place()
-    hello([(None, chip_at(c, r), k, n) for r in (1, 2, 3)])
-    cps = columns_home(src, outs, c, k, n, s_s, s_r, loc)
-    for cp in cps: cp.start()
-    for cp in cps: cp.wait()
-
-
-def spread(src, parts, cid):
-    dma = pltpu.SemaphoreType.DMA
-    rows, cols = src.shape[1], src.shape[2] // parts
+    rows, cols = down.shape[1:]
+    loads = [pltpu.make_async_copy(a, b, load.at[i]) for i, (a, b) in enumerate(((part1, acc1), (part2, acc2)))]
+    for cp in loads: cp.start()
+    hello([(None, chip_at(c, r), k, n) for r in (1, 2, 3)] + [(n > 0, c, k, n - 1), (n < nz - 1, c, k, n + 1)])
+    acc, came = (acc1, acc2), (in1, in2)
+    line = SumLine(nz, (c, k, n), lambda a, j: acc[a].at[pl.ds(pl.multiple_of(j * rows, rows), rows)],
+                   lambda a, way, i: came[a].at[way, i], z_s, z_r)
+    def term(m, cc): return down.at[cc] if m == 0 else gu.at[cc, :, pl.ds((m - 1) * cols, cols)]
+    home = [[remote(term(m, chip_at(c, r)), ff.at[m, r - 1], ff_s.at[m, r - 1], ff_r.at[m, r - 1], chip_at(c, r), k, n)
+             for r in (1, 2, 3)] for m in range(3)]
+    for cps in home:
+        for cp in cps: cp.start()
+    for cp in loads: cp.wait()
+    line.step([0, 1], 0)
+    stores = []
+    def store(src, dst, i):
+        stores.append(pltpu.make_async_copy(src, dst, loc.at[i]))
+        stores[-1].start()
+    outs = (out_d, out_g, out_u)
+    def put(m, r, value):
+        wide_ff[m, r] = value.astype(f32)
+        at = pl.ds(pl.multiple_of(chip_at(c, r) * cols, 128), cols)
+        store(wide_ff.at[m, r], outs[m].at[:, at], 4 + m * CHIPS + r)
+    for m in range(3): put(m, 0, term(m, c)[...])
+    for t in range(1, nz): line.step([0, 1], t)
+    for m in range(3):
+        for r in (1, 2, 3):
+            home[m][r - 1].wait_recv()
+            put(m, r, ff[m, r - 1])
+    wide1[...] = line.piece(0, n)[...].astype(f32)
+    wide2[...] = line.piece(1, n)[...].astype(f32)
+    first = 0
+    for i, out in enumerate((out_q, out_k, out_v)):
+        store(wide1.at[:, pl.ds(first, out.shape[1])], out, i)
+        first += out.shape[1]
+    store(wide2, out_gain, 3)
+    for cp in stores: cp.wait()
+    for cps in home:
+        for cp in cps: cp.wait_send()
+    for a in range(2): line.finish(a)
+
+
+def finish_all(nz, down, gu, part1, part2, key_width, cid):
+    dma, vm = pltpu.SemaphoreType.DMA, pltpu.VMEM
+    bf16, f32 = jnp.bfloat16, jnp.float32
+    rows, cols = down.shape[1:]
+    w1, w2 = part1.shape[1], part2.shape[1]
+    def out(w): return jax.ShapeDtypeStruct((rows, w), f32)
     return pl.pallas_call(
-        functools.partial(spread_kernel, parts),
-        out_shape=(jax.ShapeDtypeStruct((rows, CHIPS * cols), src.dtype),) * parts, in_specs=[VMEM], out_specs=(ANY,) * parts,
-        scratch_shapes=[dma((parts, 3)), dma((parts, 3)), dma],
-        compiler_params=pltpu.CompilerParams(collective_id=cid, has_side_effects=True),
-        name="spread",
-    )(src)
+        functools.partial(finish_kernel, nz),
+        out_shape=(out(w1 - 2 * key_width), out(key_width), out(key_width), out(w2)) + (out(CHIPS * cols),) * 3,
+        in_specs=[VMEM, VMEM, ANY, ANY], out_specs=(ANY,) * 7,
+        scratch_shapes=[vm(part1.shape, bf16), vm(part2.shape, bf16), vm((2, nz - 1, rows, w1), bf16), vm((2, nz - 1, rows, w2), bf16),
+                        vm((3, CHIPS - 1, rows, cols), bf16), vm((rows, w1), f32), vm((rows, w2), f32), vm((3, CHIPS, rows, cols), f32),
+                        dma((2, 2, nz)), dma((2, 2, nz)), dma((3, 3)), dma((3, 3)), dma((2,)), dma((4 + 3 * CHIPS,))],
+        compiler_params=pltpu.CompilerParams(collective_id=cid, has_side_effects=True, vmem_limit_bytes=40 << 20),
+        name="finish_all",
+    )(down, gu, part1, part2)
 
 
 def fits(mesh):
@@ -1292,16 +1326,14 @@
     output = (valid_rows * (hidden + jnp.sum(mlp_parts.astype(f32), axis=0) + mlp_crossed.astype(f32))).astype(bf16)
     grad_qkv = jnp.concatenate([grad_query, grad_key.astype(bf16), grad_value.astype(bf16)], 1)
     ff_sums = lax.psum_scatter(ff_sums, "narrow", scatter_dimension=0, tiled=True)
-    grad_w_output, grad_qkv_rows, gain_sums, grad_tokens, grad_w_down = gradient_all(
-        nz, grad_attn_low, context, scaled_attn, grad_qkv, w_qkv, tokens, grad_hidden, down_sums, gain_attn[None], grad_gain_mlp[None], 3
-    )
-    grad_w_gate, grad_w_up = (g.astype(f32) for g in spread(ff_sums.reshape(CHIPS, rows, 2 * cols), 2, 5))
-    grad_w_down = grad_w_down.astype(f32)
+    grad_w_output, qkv_part, gain_part, grad_tokens = gradient_all(
+        nz, grad_attn_low, context, scaled_attn, grad_qkv, w_qkv, tokens, grad_hidden, gain_attn[None], grad_gain_mlp[None], 3
+    )
     grad_w_output = grad_w_output.astype(f32)
-    grad_w_query = grad_qkv_rows[:, :query_width].astype(f32)
-    grad_w_key = grad_qkv_rows[:, query_width : query_width + key_width].astype(f32)
-    grad_w_value = grad_qkv_rows[:, query_width + key_width :].astype(f32)
-    grad_norm_attn, grad_norm_mlp = gain_sums[:, 0].astype(f32), gain_sums[:, 1].astype(f32)
+    grad_w_query, grad_w_key, grad_w_value, gain_sums, grad_w_down, grad_w_gate, grad_w_up = finish_all(
+        nz, down_sums, ff_sums.reshape(CHIPS, rows, 2 * cols), qkv_part, gain_part, key_width, 5
+    )
+    grad_norm_attn, grad_norm_mlp = gain_sums[:, 0], gain_sums[:, 1]
     return (
         output,
         grad_tokens,

time: 594 us -> 574 us (0.966)
  Pallas kernels: 530 us -> 510 us
  other arithmetic: 34.8 us -> 26.8 us
  local copies, waits for them, and re-layouts: 4.79 us -> 12.2 us
    pallas_call x2, Pallas kernels: 146 us -> 127 us  [the longest x1 97 us: gradient_all(): pl.pallas_call(functools.partial(gradient_kernel, nz), out_shape=(shape((...]
    convert_element_type x6 -> x0, other arithmetic: 8.05 us -> none  [the longest x2 3.57 us: fast_device(): g.astype(f32)]
    unnamed x39 -> x51, local copies, waits for them, and re-layouts: 4.41 us -> 11.1 us
  transfers between devices with their start and end apart: 1 -> 1, of which waited for: 0 -> 0; matrix products, arithmetic and copies ran while one was open for 4% -> 3% of each run, Pallas kernels for 27% -> 23%
where the time goes in v7:
time: 574 us; the launch traced here: 567 us
  Pallas kernels  510 us (89%)
  other arithmetic  26.8 us (5%)
  between operations  15.5 us (3%)
  local copies, waits for them, and re-layouts  12.2 us (2%)
    pallas_call x1, Pallas kernels, gather_all(): pl.pallas_call(functools.partial(gather_kernel, nz), out_shape=(shape((wi...  146 us
    pallas_call x1, Pallas kernels, mlp_all(): pl.pallas_call(functools.partial(mlp_kernel, nz), out_shape=(blocks(width...  144 us
    pallas_call x1, Pallas kernels, gradient_all(): pl.pallas_call(functools.partial(gradient_kernel, nz), out_shape=(shape((...  97 us
    pallas_call x1, Pallas kernels, attend_all(): pl.pallas_call(functools.partial(attend_kernel, nz), grid=(KEY_VALUE_HEAD...  61.2 us
    pallas_call x1, Pallas kernels, attend_back_all(): pl.pallas_call(attend_back_kernel, grid=(KEY_VALUE_HEADS,), out_shape=(sh...  32 us
    pallas_call x1, Pallas kernels, finish_all(): pl.pallas_call(functools.partial(finish_kernel, nz), out_shape=(out(w1 -...  30.4 us
  transfers between devices with their start and end apart: 1, of which 0 were waited for; matrix products, arithmetic and copies ran while one was open for 3% of the time, Pallas kernels for 23%

profile of v7, /device:TPU:0, one launch (start us, length us, event | category | flops | bytes accessed | tf_op | source)
XLA Modules:
  0.0 567.5 jit_solution(3853483971045858075)
XLA Ops:
  7.2 0.0 reduce-scatter.2.cloned.1.call-start
  7.2 0.6 compare_reduce_fusion.1
  7.9 0.6 compare_reduce_fusion
  9.2 0.0 copy-start.18
  9.2 0.7 convert_element_type.80
  9.9 1.3 fusion.3
  11.2 0.1 copy.26
  11.3 1.3 fusion.4
  12.6 0.1 copy.27
  12.7 0.6 multiply_cosine_fusion
  13.4 0.0 copy-start.13
  13.4 0.2 maximum_bitcast_fusion
  13.6 0.1 scatter.9.gains
  13.8 0.0 copy-start.17
  13.8 0.6 copy-done.17
  14.4 145.7 %gather_all.1 = (bf16[2048,2560]{1,0:T(8,128)(2,1)}, bf16[2048,2048]{1,0:T(8,128)(2,1)}, bf16[2048,128]{1,0:T(8,128)(2,1)}, bf16[4,8,64,2816]{3,2,1,0:T(8,128)(2,1)}, bf16[4,64,1408]{2,1,0:T(8,128)(2,1)}) custom-call(bf16[64,2048]{1,0:T(8,128)(2,1)} %wq.1, bf16[64,256]{1,0:T(8,128)(2,1)} %wk.1, bf16[64,256]{1,0:T(8,128)(2,1)} %wv.1, bf16[64,2048]{1,0:T(8,128)(2,1)} %wo.1, ...), custom_call_target="tpu_custom_call" | custom-call | tf_op jit(solution)/shard_map/gather_all/pallas_call | solution.py:544
  160.1 2.3 convert_reduce_fusion.2
  162.4 0.1 negate_select_fusion
  162.5 0.2 maximum_bitcast_fusion.1
  162.7 1.3 fusion.gy
  164.0 0.8 pad_maximum_fusion.1.tab_ref
  164.8 61.2 %attend.1 = (bf16[320,2048]{1,0:T(8,128)(2,1)}, bf16[4,320,128]{2,1,0:T(8,128)(2,1)}, bf16[4,320,128]{2,1,0:T(8,128)(2,1)}, f32[4,320,128]{2,1,0:T(8,128)}, bf16...) custom-call(bf16[320,2048]{1,0:T(8,128)(2,1)} %tok_hbm.1, ...), custom_call_target="tpu_custom_call" | custom-call | flops 5368709120 | bytes 41943040 | tf_op jit(solution)/shard_map/attend/pallas_call | solution.py:932
  226.0 143.7 %mlp_all.1 = (bf16[4,320,2048]{2,1,0:T(8,128)(2,1)}, bf16[3,320,2048]{2,1,0:T(8,128)(2,1)}, bf16[320,2048]{1,0:T(8,128)(2,1)}, bf16[4,64,1408]{2,1,0:T(8,128)(2,1)}, bf16[4,4,64,2816]{3,2,1,0:T(8,128)(2,1)}) custom-call(bf16[320,2048]{1,0:T(8,128)(2,1)} %get-tuple-element.75.x, bf16[4,320,2048]{2,1,0:T(8,128)(2,1)} %get-tuple-element.76.gy, ...), custom_call_target="tpu_custom_call" | custom-call | flops 66437775360 | bytes 62914560 | tf_op jit(solution)/shard_map/mlp_all/pallas_call | solution.py:768
  369.8 0.0 reduce-scatter.2.cloned.1.call-update
  369.8 1.7 copy-done.10
  371.5 0.3 multiply_reduce_fusion.2
  371.8 0.0 copy-start.14
  371.8 4.1 convert_reduce_fusion
  375.9 1.3 multiply_reduce_fusion
  377.2 2.4 fusion.5
  379.7 0.5 slice-done.1
  380.2 3.0 convolution_convert_fusion.gc_ref
  383.3 32.0 %attend_back.1 = (bf16[320,2048]{1,0:T(8,128)(2,1)S(1)}, f32[320,256]{1,0:T(8,128)S(1)}, f32[320,256]{1,0:T(8,128)S(1)}, bf16[320,2048]{1,0:T(8,128)(2,1)S(1)}) custom-call(bf16[320,2048]{1,0:T(8,128)(2,1)S(1)} %copy-done.3, bf16[4,320,128]{2,1,0:T(8,128)(2,1)S(1)} %copy-done.7, bf16[4,320,128]{2,1,0:T(8,128)(2,1)S(1)} %copy-done.8, ...), custom_call_target="tpu_custom_call" | custom-call | tf_op jit(solution)/shard_map/attend_back/pallas_call | solution.py:1016
  415.3 1.4 pad_maximum_fusion.gq_hbm
  416.7 97.0 %gradient_all.1 = (bf16[64,2048]{1,0:T(8,128)(2,1)}, bf16[256,2560]{1,0:T(8,128)(2,1)}, bf16[256,128]{1,0:T(8,128)(2,1)}, f32[320,2048]{1,0:T(8,128)}) custom-call(bf16[320,2048]{1,0:T(8,128)(2,1)} %copy-done.12, bf16[320,2048]{1,0:T(8,128)(2,1)} %get-tuple-element.87.ctx_hbm, bf16[320,2048]{1,0:T(8,128)(2,1)} %get-tuple-element.88.xn_hbm, ...), custom_call_target="tpu_custom_call" | custom-call | tf_op jit(solution)/shard_map/gradient_all/pallas_call | solution.py:1198
  513.7 1.8 convert_element_type.93
  515.5 3.4 convert_reduce_fusion.1
  518.9 1.9 multiply_convert_fusion
  520.9 1.4 copy-done.1
  522.2 30.4 %finish_all.1 = (f32[64,2048]{1,0:T(8,128)S(1)}, f32[64,256]{1,0:T(8,128)S(1)}, f32[64,256]{1,0:T(8,128)S(1)}, f32[64,128]{1,0:T(8,128)S(1)}, f32[64,5632]{1,0:T...) custom-call(bf16[4,64,1408]{2,1,0:T(8,128)(2,1)S(1)} %copy-done.5, bf16[4,64,2816]{2,1,0:T(8,128)(2,1)S(1)} %bitcast.20, ...), custom_call_target="tpu_custom_call" | custom-call | tf_op jit(solution)/shard_map/finish_all/pallas_call | solution.py:1263
  552.6 0.7 slice_reduce_fusion
  553.3 1.5 copy.37
  554.8 0.8 copy.38
  555.6 0.6 copy.39
  556.2 0.6 copy.40
  556.9 1.1 copy.41
  558.0 1.1 copy.42
  559.1 1.1 copy.43
  (46 shorter events, 0.1 us)
Async XLA Ops:
  7.2 513.7 %reduce-scatter.2.cloned.1.call-start = ((), (), s32[]{:S(2)}) async-start(), calls=%async_computation.1 | async-start | bytes 7208960 | tf_op jit(solution)/shard_map/reduce_scatter | solution.py:1328
  9.2 368.0 %copy-start.18 = (f32[320]{0:T(512)}, f32[320]{0:T(512)S(1)}, u32[]{:S(2)}) copy-start(f32[320]{0:T(512)S(1)} %fusion.2) | copy-start | bytes 3844
  13.4 149.3 %copy-start.13 = (bf16[320,2048]{1,0:T(8,128)(2,1)S(1)}, bf16[320,2048]{1,0:T(8,128)(2,1)}, u32[]{:S(2)}) copy-start(bf16[320,2048]{1,0:T(8,128)(2,1)} %param.18) | copy-start | bytes 3932164
  13.8 0.6 copy-start.17
  369.7 1.7 copy-start.10
  371.8 4.1 copy-start.16
  371.8 5.4 copy-start.14
  375.9 3.8 slice-start
  377.2 3.0 slice-start.1
  379.7 3.5 copy-start.12
  380.2 3.0 copy-start
  380.2 3.0 copy-start.3
  380.2 3.0 copy-start.4
  380.2 3.0 copy-start.6
  380.2 3.0 copy-start.7
  380.2 3.0 copy-start.8
  515.5 3.4 copy-start.11
  515.5 3.4 copy-start.19
  518.9 1.9 copy-start.2
  518.9 1.9 copy-start.5
  518.9 1.9 copy-start.9
  520.8 1.4 copy-start.1
  522.2 31.1 %copy-start.15 = (f32[320,2048]{1,0:T(8,128)S(1)}, f32[320,2048]{1,0:T(8,128)}, u32[]{:S(2)}) copy-start(f32[320,2048]{1,0:T(8,128)} %get-tuple-element.131) | copy-start | bytes 7864324
Sparse Core Ops, SparseCore 0:
  369.9 100.8 reduce-scatter.1

commit v8 on v7

--- a/solution.py
+++ b/solution.py
@@ -947,15 +947,46 @@
     )(tokens, gain1, gain2, tables, w_qkv, w_out, gy, gd_own)
 
 
-def attend_back_kernel(q_ref, k_ref, v_ref, lse_ref, gc_ref, tab_ref, part, gq_ref, gk_ref, gv_ref, crossed,
-                       ks, kt, vt, ds, pr, qs, gs, s_s, s_r):
+def products(left_side, right_side, kk, xt, put):
+    part = xt.shape[0] // CHIPS
+    for t in range(CHIPS):
+        at = pl.ds(pl.multiple_of((t * CORES + kk) * part, 128), part)
+        xt[t * part : (t + 1) * part, :] = left_side[:, at].T
+    def step(j, carry):
+        at = pl.ds(pl.multiple_of(j * 256, 256), 256)
+        put(at, jnp.dot(xt[...], right_side[:, at], preferred_element_type=jnp.float32).reshape(CHIPS, part, 256))
+        return carry
+    lax.fori_loop(0, right_side.shape[1] // 256, step, 0)
+
+
+def to_their_core(left_side, right_side, k, xt, away, swap):
+    def put(at, v): away[:, :, at] = v.astype(jnp.bfloat16)
+    products(left_side, right_side, 1 - k, xt, put)
+    swap.start()
+
+
+def with_their_core(left_side, right_side, k, xt, took, swap):
+    swap.wait_recv()
+    def put(at, v): took[:, :, at] = (took[:, :, at].astype(jnp.float32) + v).astype(jnp.bfloat16)
+    products(left_side, right_side, k, xt, put)
+
+
+def attend_back_kernel(q_ref, k_ref, v_ref, lse_ref, gc_ref, tab_ref, part, gal, ctx, gq_ref, gk_ref, gv_ref, crossed, core_sums,
+                       ks, kt, vt, ds, pr, qs, gs, away, took, xt, s_s, s_r, core_s, core_r, done):
     g = pl.program_id(0)
     c, k, n = place()
     copy = remote(part, crossed, s_s, s_r, chip_at(c, 3), k, n)
+    swap = remote(away, took, core_s, core_r, c, 1 - k, n)
+    store = pltpu.make_async_copy(took, core_sums, done)
     @pl.when(g == 0)
     def _():
-        hello([(None, chip_at(c, 3), k, n)])
+        hello([(None, chip_at(c, 3), k, n), (None, c, 1 - k, n)])
         copy.start()
+        to_their_core(gal, ctx, k, xt, away, swap)
+    @pl.when(g == KEY_VALUE_HEADS - 1)
+    def _():
+        with_their_core(gal, ctx, k, xt, took, swap)
+        store.start()
     f32, bf16 = jnp.float32, jnp.bfloat16
     slots = q_ref.shape[0]
     scale = HEAD_SIZE ** -0.5
@@ -1001,11 +1032,15 @@
         @pl.when(g % 2 == 1)
         def _(): out[...] = jnp.where(lane < HEAD_SIZE, out[...], pltpu.roll(x, HEAD_SIZE, 1))
     @pl.when(g == KEY_VALUE_HEADS - 1)
-    def _(): copy.wait()
-
-
-def attend_back_all(q, k, v, lse, grad_context, tables, part):
-    slots = q.shape[0]
+    def _():
+        copy.wait()
+        swap.wait_send()
+        store.wait()
+
+
+def attend_back_all(q, k, v, lse, grad_context, tables, part, gal, ctx):
+    slots, width = gal.shape
+    block = (CHIPS, width // (CHIPS * CORES), ctx.shape[1])
     wide = REPEAT * HEAD_SIZE
     bf16, f32, vm = jnp.bfloat16, jnp.float32, pltpu.VMEM
     keys = -(-slots // 128) * 128
@@ -1017,14 +1052,15 @@
         attend_back_kernel,
         grid=(KEY_VALUE_HEADS,),
         out_shape=(shape((slots, QUERY_HEADS * HEAD_SIZE), bf16), shape((slots, KEY_VALUE_HEADS * HEAD_SIZE), f32),
-                   shape((slots, KEY_VALUE_HEADS * HEAD_SIZE), f32), shape(part.shape, part.dtype)),
-        in_specs=[wide_spec, per_head, per_head, per_head, wide_spec, pl.BlockSpec((3, slots, PAIR), lambda g: (0, 0, 0)), ANY],
-        out_specs=(wide_spec, two, two, ANY),
+                   shape((slots, KEY_VALUE_HEADS * HEAD_SIZE), f32), shape(part.shape, part.dtype), shape(block, bf16)),
+        in_specs=[wide_spec, per_head, per_head, per_head, wide_spec, pl.BlockSpec((3, slots, PAIR), lambda g: (0, 0, 0)), ANY,
+                  pl.BlockSpec(gal.shape, lambda g: (0, 0)), pl.BlockSpec(ctx.shape, lambda g: (0, 0))],
+        out_specs=(wide_spec, two, two, ANY, ANY),
         scratch_shapes=[vm((2, keys, PAIR), bf16)] * 3 + [vm((2, PAIRS * slots, keys), bf16)] * 2 + [vm((PAIRS * slots, PAIR), bf16)] * 2
-        + [pltpu.SemaphoreType.DMA] * 2,
-        compiler_params=pltpu.CompilerParams(collective_id=2, has_side_effects=True, vmem_limit_bytes=40 << 20),
+        + [vm(block, bf16), vm(block, bf16), vm((CHIPS * block[1], slots), bf16)] + [pltpu.SemaphoreType.DMA] * 5,
+        compiler_params=pltpu.CompilerParams(collective_id=2, has_side_effects=True, vmem_limit_bytes=48 << 20),
         name="attend_back",
-    )(q, k, v, lse, grad_context, tables, part)
+    )(q, k, v, lse, grad_context, tables, part, gal, ctx)
 
 
 class SumLine:
@@ -1058,26 +1094,26 @@
                 def _(): self._hop(a, way, j).wait_send()
 
 
-def gradient_kernel(nz, gal_hbm, ctx_hbm, xn_hbm, gq_hbm, wq_hbm, tok_hbm, gh_hbm, gain, gain_mlp, out0, out1, out2, grad_tokens,
-                    took0, took1, took2, away0, away1, away2, zbuf0, zbuf1, zbuf2, gal, ctx, xn, gq, wq, tok, gh, gx, xt, gain_row,
+def gradient_kernel(nz, sums_hbm, xn_hbm, gq_hbm, wq_hbm, tok_hbm, gh_hbm, gain, gain_mlp, out0, out1, out2, grad_tokens,
+                    took0, took1, took2, away1, away2, zbuf0, zbuf1, zbuf2, xn, gq, wq, tok, gh, gx, xt, gain_row,
                     core_s, core_r, half_s, half_r, main_s, main_r, z_s, z_r, load, loc):
     f32, bf16 = jnp.float32, jnp.bfloat16
     items = 3
-    outs, took, away, zbuf = (out0, out1, out2), (took0, took1, took2), (away0, away1, away2), (zbuf0, zbuf1, zbuf2)
+    outs, took, away, zbuf = (out0, out1, out2), (took0, took1, took2), (None, away1, away2), (zbuf0, zbuf1, zbuf2)
     c, k, n = place()
     left, right = n > 0, n < nz - 1
     cx, cy, cd = (chip_at(c, r) for r in (1, 2, 3))
     loads = [pltpu.make_async_copy(a, b, load.at[i]) for i, (a, b) in enumerate(
-        ((gal_hbm, gal), (ctx_hbm, ctx), (xn_hbm, xn), (gq_hbm, gq), (wq_hbm, wq), (tok_hbm, tok), (gh_hbm, gh)))]
+        ((sums_hbm, took0), (xn_hbm, xn), (gq_hbm, gq), (wq_hbm, wq), (tok_hbm, tok), (gh_hbm, gh)))]
     for cp in loads: cp.start()
     hello([(None, cc, k, n) for cc in (cx, cy, cd)] + [(None, c, 1 - k, n), (left, c, k, n - 1), (right, c, k, n + 1)])
-    slots, width = gal.shape
+    slots, width = xn.shape
     rows = out0.shape[0]
     part = nz * rows
     half = part // 2
     top, low = pl.ds(0, half), pl.ds(half, half)
     def arrive(a, at, size): return zbuf[a].at[pl.ds(at, size)]
-    swap = [remote(away[a], took[a], core_s.at[a], core_r.at[a], c, 1 - k, n) for a in range(items)]
+    swap = [a and remote(away[a], took[a], core_s.at[a - 1], core_r.at[a - 1], c, 1 - k, n) for a in range(items)]
     cross = [[remote(took[a].at[cd, top], arrive(a, 2 * part, half), half_s.at[a, 0], half_r.at[a, 0], cx, k, n),
               remote(took[a].at[cd, low], arrive(a, 2 * part + half, half), half_s.at[a, 1], half_r.at[a, 1], cy, k, n)]
              for a in range(items)]
@@ -1087,29 +1123,8 @@
              remote(took[a].at[cy, top], arrive(a, part, half), main_s.at[a, 3], main_r.at[a, 3], cy, k, n)]
             for a in range(items)]
 
-    def products(left_side, right_side, kk, put):
-        for t in range(CHIPS):
-            at = pl.ds(pl.multiple_of((t * CORES + kk) * part, 128), part)
-            xt[t * part : (t + 1) * part, :] = left_side[:, at].T
-        def step(j, carry):
-            at = pl.ds(pl.multiple_of(j * 256, 256), 256)
-            put(at, jnp.dot(xt[...], right_side[:, at], preferred_element_type=f32).reshape(CHIPS, part, 256))
-            return carry
-        lax.fori_loop(0, right_side.shape[1] // 256, step, 0)
-
-    def theirs(a, left_side, right_side):
-        def put(at, v): away[a][:, :, at] = v.astype(bf16)
-        products(left_side, right_side, 1 - k, put)
-        swap[a].start()
-
-    def ours(a, left_side, right_side):
-        swap[a].wait_recv()
-        def put(at, v): took[a][:, :, at] = (took[a][:, :, at].astype(f32) + v).astype(bf16)
-        products(left_side, right_side, k, put)
-        for cp in cross[a]: cp.start()
-
     def input_gradient():
-        loads[4].wait()
+        loads[3].wait()
         def step(j, carry):
             at = pl.ds(pl.multiple_of(j * 256, 256), 256)
             gx[:, at] = lax.dot_general(gq[...], wq[at, :], contract_last, preferred_element_type=f32)
@@ -1117,7 +1132,7 @@
         lax.fori_loop(0, width // 256, step, 0)
 
     def input_norm():
-        for cp in loads[5:]: cp.wait()
+        for cp in loads[4:]: cp.wait()
         def step(j, total):
             at = pl.ds(pl.multiple_of(j * 16, 16), 16)
             x, g = tok[at, :].astype(f32), gx[at, :]
@@ -1157,14 +1172,14 @@
     line = SumLine(nz, (c, k, n), lambda a, j: took[a].at[c, pl.ds(pl.multiple_of(j * rows, rows), rows)],
                    lambda a, way, i: arrive(a, pl.multiple_of(2 * part + 2 * half + (way * (nz - 1) + i) * rows, rows), rows), z_s, z_r)
 
-    for cp in loads[:2]: cp.wait()
-    theirs(0, gal, ctx)
-    for cp in loads[2:4]: cp.wait()
-    theirs(1, xn, gq)
-    ours(0, gal, ctx)
-    ours(1, xn, gq)
+    loads[0].wait()
+    for cp in cross[0]: cp.start()
+    for cp in loads[1:3]: cp.wait()
+    to_their_core(xn, gq, k, xt, away[1], swap[1])
+    relay(0)
+    with_their_core(xn, gq, k, xt, took[1], swap[1])
+    for cp in cross[1]: cp.start()
     input_gradient()
-    relay(0)
     gains_swap(input_norm())
     stores = [pltpu.make_async_copy(gh, grad_tokens, loc.at[items])]
     stores[0].start()
@@ -1179,41 +1194,44 @@
         stores[-1].start()
     for cp in stores: cp.wait()
     for a in range(items):
-        swap[a].wait_send()
+        if a: swap[a].wait_send()
         for cp in cross[a] + main[a]: cp.wait_send()
     line.finish(0)
 
 
-def gradient_all(nz, gal, ctx, xn, gq, wq, tokens, grad_hidden, gain, gain_mlp, cid):
+def gradient_all(nz, sums, xn, gq, wq, tokens, grad_hidden, gain, gain_mlp, cid):
     dma, vm = pltpu.SemaphoreType.DMA, pltpu.VMEM
     bf16, f32 = jnp.bfloat16, jnp.float32
-    slots, width = gal.shape
+    slots, width = xn.shape
     m = 3
     part = width // (CHIPS * CORES)
     rows = part // nz
-    widths = (ctx.shape[1], gq.shape[1], 128)
+    widths = (sums.shape[2], gq.shape[1], 128)
     shape = jax.ShapeDtypeStruct
     blocks = [vm((CHIPS, part, w), bf16) for w in widths]
     row = pl.BlockSpec((1, width), lambda: (0, 0))
     return pl.pallas_call(
         functools.partial(gradient_kernel, nz),
         out_shape=(shape((rows, widths[0]), bf16),) + tuple(shape((part, w), bf16) for w in widths[1:]) + (shape((slots, width), f32),),
-        in_specs=[ANY] * 7 + [row, row], out_specs=(ANY,) * (m + 1),
-        scratch_shapes=blocks + blocks + [vm((3 * part + 2 * nz * rows, w), bf16) for w in widths]
-        + [vm(gal.shape, bf16), vm(ctx.shape, bf16), vm(xn.shape, bf16), vm(gq.shape, bf16), vm(wq.shape, bf16), vm(tokens.shape, bf16),
+        in_specs=[ANY] * 6 + [row, row], out_specs=(ANY,) * (m + 1),
+        scratch_shapes=blocks + blocks[1:] + [vm((3 * part + 2 * nz * rows, w), bf16) for w in widths]
+        + [vm(xn.shape, bf16), vm(gq.shape, bf16), vm(wq.shape, bf16), vm(tokens.shape, bf16),
            vm((slots, width), f32), vm((slots, width), f32), vm((CHIPS * part, slots), bf16), vm((8, width), f32)]
-        + [dma((m,)), dma((m,)), dma((m, 2)), dma((m, 2)), dma((m, 4)), dma((m, 4)), dma((m, 2, nz)), dma((m, 2, nz)), dma((7,)), dma((m + 1,))],
+        + [dma((m - 1,)), dma((m - 1,)), dma((m, 2)), dma((m, 2)), dma((m, 4)), dma((m, 4)), dma((1, 2, nz)), dma((1, 2, nz)), dma((6,)), dma((m + 1,))],
         compiler_params=pltpu.CompilerParams(collective_id=cid, has_side_effects=True, vmem_limit_bytes=62 << 20),
         name="gradient_all",
-    )(gal, ctx, xn, gq, wq, tokens, grad_hidden, gain, gain_mlp)
-
-
-def finish_kernel(nz, down, gu, part1, part2, out_q, out_k, out_v, out_gain, out_d, out_g, out_u,
-                  acc1, acc2, in1, in2, ff, wide1, wide2, wide_ff, z_s, z_r, ff_s, ff_r, load, loc):
+    )(sums, xn, gq, wq, tokens, grad_hidden, gain, gain_mlp)
+
+
+def finish_kernel(nz, down, gu, part1, part2, sum_o, parts_hbm, crossed_hbm, hidden_hbm, valid,
+                  out_q, out_k, out_v, out_gain, out_d, out_g, out_u, out_o, output,
+                  acc1, acc2, in1, in2, ff, wide1, wide2, wide_ff, wide_o, parts, crossed, hidden, result,
+                  z_s, z_r, ff_s, ff_r, load, loc):
     f32 = jnp.float32
     c, k, n = place()
     rows, cols = down.shape[1:]
-    loads = [pltpu.make_async_copy(a, b, load.at[i]) for i, (a, b) in enumerate(((part1, acc1), (part2, acc2)))]
+    loads = [pltpu.make_async_copy(a, b, load.at[i]) for i, (a, b) in enumerate(
+        ((part1, acc1), (part2, acc2), (parts_hbm, parts), (crossed_hbm, crossed), (hidden_hbm, hidden)))]
     for cp in loads: cp.start()
     hello([(None, chip_at(c, r), k, n) for r in (1, 2, 3)] + [(n > 0, c, k, n - 1), (n < nz - 1, c, k, n + 1)])
     acc, came = (acc1, acc2), (in1, in2)
@@ -1224,7 +1242,7 @@
              for r in (1, 2, 3)] for m in range(3)]
     for cps in home:
         for cp in cps: cp.start()
-    for cp in loads: cp.wait()
+    for cp in loads[:2]: cp.wait()
     line.step([0, 1], 0)
     stores = []
     def store(src, dst, i):
@@ -1236,7 +1254,19 @@
         at = pl.ds(pl.multiple_of(chip_at(c, r) * cols, 128), cols)
         store(wide_ff.at[m, r], outs[m].at[:, at], 4 + m * CHIPS + r)
     for m in range(3): put(m, 0, term(m, c)[...])
-    for t in range(1, nz): line.step([0, 1], t)
+    wide_o[...] = sum_o[...].astype(f32)
+    store(wide_o, out_o, 4 + 3 * CHIPS)
+    line.step([0, 1], 1)
+    for cp in loads[2:]: cp.wait()
+    def add(i, carry):
+        at = pl.ds(pl.multiple_of(i * 16, 16), 16)
+        total = hidden[at, :] + (parts[0, at, :].astype(f32) + parts[1, at, :].astype(f32) + parts[2, at, :].astype(f32)
+                                 + crossed[at, :].astype(f32))
+        result[at, :] = (valid[at, :] * total).astype(result.dtype)
+        return carry
+    lax.fori_loop(0, result.shape[0] // 16, add, 0)
+    store(result, output, 5 + 3 * CHIPS)
+    for t in range(2, nz): line.step([0, 1], t)
     for m in range(3):
         for r in (1, 2, 3):
             home[m][r - 1].wait_recv()
@@ -1254,7 +1284,7 @@
     for a in range(2): line.finish(a)
 
 
-def finish_all(nz, down, gu, part1, part2, key_width, cid):
+def finish_all(nz, down, gu, part1, part2, sum_o, parts, crossed, hidden, valid, key_width, cid):
     dma, vm = pltpu.SemaphoreType.DMA, pltpu.VMEM
     bf16, f32 = jnp.bfloat16, jnp.float32
     rows, cols = down.shape[1:]
@@ -1262,14 +1292,16 @@
     def out(w): return jax.ShapeDtypeStruct((rows, w), f32)
     return pl.pallas_call(
         functools.partial(finish_kernel, nz),
-        out_shape=(out(w1 - 2 * key_width), out(key_width), out(key_width), out(w2)) + (out(CHIPS * cols),) * 3,
-        in_specs=[VMEM, VMEM, ANY, ANY], out_specs=(ANY,) * 7,
+        out_shape=(out(w1 - 2 * key_width), out(key_width), out(key_width), out(w2)) + (out(CHIPS * cols),) * 3
+        + (out(sum_o.shape[1]), jax.ShapeDtypeStruct(hidden.shape, bf16)),
+        in_specs=[VMEM, VMEM, ANY, ANY, VMEM, ANY, ANY, ANY, VMEM], out_specs=(ANY,) * 9,
         scratch_shapes=[vm(part1.shape, bf16), vm(part2.shape, bf16), vm((2, nz - 1, rows, w1), bf16), vm((2, nz - 1, rows, w2), bf16),
                         vm((3, CHIPS - 1, rows, cols), bf16), vm((rows, w1), f32), vm((rows, w2), f32), vm((3, CHIPS, rows, cols), f32),
-                        dma((2, 2, nz)), dma((2, 2, nz)), dma((3, 3)), dma((3, 3)), dma((2,)), dma((4 + 3 * CHIPS,))],
+                        vm(sum_o.shape, f32), vm(parts.shape, bf16), vm(crossed.shape, bf16), vm(hidden.shape, f32), vm(hidden.shape, bf16),
+                        dma((2, 2, nz)), dma((2, 2, nz)), dma((3, 3)), dma((3, 3)), dma((5,)), dma((6 + 3 * CHIPS,))],
         compiler_params=pltpu.CompilerParams(collective_id=cid, has_side_effects=True, vmem_limit_bytes=40 << 20),
         name="finish_all",
-    )(down, gu, part1, part2)
+    )(down, gu, part1, part2, sum_o, parts, crossed, hidden, valid)
 
 
 def fits(mesh):
@@ -1320,18 +1352,27 @@
     grad_hidden = grad_y + norm_back(grad_xn2 * gain_mlp, normed_mlp, hidden)
     grad_attn_low = grad_hidden.astype(bf16)
     grad_context = jnp.dot(grad_attn_low, w_out, preferred_element_type=f32).astype(bf16)
-    grad_query, grad_key, grad_value, mlp_crossed = attend_back_all(
-        query_rotated, key_rotated, value_reduced, log_totals, grad_context, tables, mlp_cross
-    )
-    output = (valid_rows * (hidden + jnp.sum(mlp_parts.astype(f32), axis=0) + mlp_crossed.astype(f32))).astype(bf16)
+    grad_query, grad_key, grad_value, mlp_crossed, out_sums = attend_back_all(
+        query_rotated, key_rotated, value_reduced, log_totals, grad_context, tables, mlp_cross, grad_attn_low, context
+    )
     grad_qkv = jnp.concatenate([grad_query, grad_key.astype(bf16), grad_value.astype(bf16)], 1)
     ff_sums = lax.psum_scatter(ff_sums, "narrow", scatter_dimension=0, tiled=True)
-    grad_w_output, qkv_part, gain_part, grad_tokens = gradient_all(
-        nz, grad_attn_low, context, scaled_attn, grad_qkv, w_qkv, tokens, grad_hidden, gain_attn[None], grad_gain_mlp[None], 3
-    )
-    grad_w_output = grad_w_output.astype(f32)
-    grad_w_query, grad_w_key, grad_w_value, gain_sums, grad_w_down, grad_w_gate, grad_w_up = finish_all(
-        nz, down_sums, ff_sums.reshape(CHIPS, rows, 2 * cols), qkv_part, gain_part, key_width, 5
+    out_part, qkv_part, gain_part, grad_tokens = gradient_all(
+        nz, out_sums, scaled_attn, grad_qkv, w_qkv, tokens, grad_hidden, gain_attn[None], grad_gain_mlp[None], 3
+    )
+    grad_w_query, grad_w_key, grad_w_value, gain_sums, grad_w_down, grad_w_gate, grad_w_up, grad_w_output, output = finish_all(
+        nz,
+        down_sums,
+        ff_sums.reshape(CHIPS, rows, 2 * cols),
+        qkv_part,
+        gain_part,
+        out_part,
+        mlp_parts,
+        mlp_crossed,
+        hidden,
+        valid_rows,
+        key_width,
+        5,
     )
     grad_norm_attn, grad_norm_mlp = gain_sums[:, 0], gain_sums[:, 1]
     return (

time: 574 us -> 564 us (0.983)
  Pallas kernels: 510 us -> 501 us
  other arithmetic: 26.8 us -> 19.6 us
    pallas_call x1, Pallas kernels: 97 us -> 84.9 us  [gradient_all(): pl.pallas_call(functools.partial(gradient_kernel, nz), out_shape=(shape((...]
    unnamed x51 -> x45, local copies, waits for them, and re-layouts: 11.1 us -> 16.5 us
  transfers between devices with their start and end apart: 1 -> 1, of which waited for: 0 -> 0; matrix products, arithmetic and copies ran while one was open for 3% -> 2% of each run, Pallas kernels for 23% -> 22%
where the time goes in v8:
time: 564 us; the launch traced here: 557 us
  Pallas kernels  501 us (89%)
  other arithmetic  19.6 us (3%)
  local copies, waits for them, and re-layouts  17.6 us (3%)
  between operations  15.4 us (3%)
    pallas_call x1, Pallas kernels, gather_all(): pl.pallas_call(functools.partial(gather_kernel, nz), out_shape=(shape((wi...  146 us
    pallas_call x1, Pallas kernels, mlp_all(): pl.pallas_call(functools.partial(mlp_kernel, nz), out_shape=(blocks(width...  144 us
    pallas_call x1, Pallas kernels, gradient_all(): pl.pallas_call(functools.partial(gradient_kernel, nz), out_shape=(shape((...  84.9 us
    pallas_call x1, Pallas kernels, attend_all(): pl.pallas_call(functools.partial(attend_kernel, nz), grid=(KEY_VALUE_HEAD...  61.3 us
    pallas_call x1, Pallas kernels, attend_back_all(): pl.pallas_call(attend_back_kernel, grid=(KEY_VALUE_HEADS,), out_shape=(sh...  37.1 us
    pallas_call x1, Pallas kernels, finish_all(): pl.pallas_call(functools.partial(finish_kernel, nz), out_shape=(out(w1 -...  28.2 us
    unnamed x45, local copies, waits for them, and re-layouts  16.5 us
  transfers between devices with their start and end apart: 1, of which 0 were waited for; matrix products, arithmetic and copies ran while one was open for 2% of the time, Pallas kernels for 22%

profile of v8, /device:TPU:0, one launch (start us, length us, event | category | flops | bytes accessed | tf_op | source)
XLA Modules:
  0.0 557.2 jit_solution(5907277424743545024)
XLA Ops:
  7.2 0.0 reduce-scatter.2.cloned.1.call-start
  7.2 0.6 compare_reduce_fusion.1
  7.9 0.6 compare_reduce_fusion
  8.5 0.7 convert_element_type.73
  9.2 0.6 multiply_cosine_fusion
  9.9 0.2 maximum_bitcast_fusion
  10.1 1.4 fusion.4
  11.5 0.1 copy.26
  11.6 1.3 fusion.5
  12.9 0.1 copy.27
  13.0 0.1 scatter.9.gains
  13.2 0.6 copy-done.15
  13.8 145.6 %gather_all.1 = (bf16[2048,2560]{1,0:T(8,128)(2,1)}, bf16[2048,2048]{1,0:T(8,128)(2,1)}, bf16[2048,128]{1,0:T(8,128)(2,1)}, bf16[4,8,64,2816]{3,2,1,0:T(8,128)(2,1)}, bf16[4,64,1408]{2,1,0:T(8,128)(2,1)}) custom-call(bf16[64,2048]{1,0:T(8,128)(2,1)} %wq.1, bf16[64,256]{1,0:T(8,128)(2,1)} %wk.1, bf16[64,256]{1,0:T(8,128)(2,1)} %wv.1, bf16[64,2048]{1,0:T(8,128)(2,1)} %wo.1, ...), custom_call_target="tpu_custom_call" | custom-call | tf_op jit(solution)/shard_map/gather_all/pallas_call | solution.py:544
  159.4 2.3 convert_reduce_fusion.1
  162.4 0.1 negate_select_fusion
  162.5 0.2 maximum_bitcast_fusion.1
  162.7 1.3 fusion.gy
  164.0 0.8 pad_maximum_fusion.1.tab_ref
  164.9 61.3 %attend.1 = (bf16[320,2048]{1,0:T(8,128)(2,1)}, bf16[4,320,128]{2,1,0:T(8,128)(2,1)}, bf16[4,320,128]{2,1,0:T(8,128)(2,1)}, f32[4,320,128]{2,1,0:T(8,128)}, bf16...) custom-call(bf16[320,2048]{1,0:T(8,128)(2,1)} %tok_hbm.1, ...), custom_call_target="tpu_custom_call" | custom-call | flops 5368709120 | bytes 41943040 | tf_op jit(solution)/shard_map/attend/pallas_call | solution.py:932
  226.2 143.5 %mlp_all.1 = (bf16[4,320,2048]{2,1,0:T(8,128)(2,1)}, bf16[3,320,2048]{2,1,0:T(8,128)(2,1)}, bf16[320,2048]{1,0:T(8,128)(2,1)}, bf16[4,64,1408]{2,1,0:T(8,128)(2,1)}, bf16[4,4,64,2816]{3,2,1,0:T(8,128)(2,1)}) custom-call(bf16[320,2048]{1,0:T(8,128)(2,1)} %get-tuple-element.77.x, bf16[4,320,2048]{2,1,0:T(8,128)(2,1)} %get-tuple-element.78.gy, ...), custom_call_target="tpu_custom_call" | custom-call | flops 66437775360 | bytes 62914560 | tf_op jit(solution)/shard_map/mlp_all/pallas_call | solution.py:768
  369.7 0.0 reduce-scatter.2.cloned.1.call-update
  369.7 1.7 copy-done.9
  371.4 0.3 multiply_reduce_fusion.2
  371.7 4.0 convert_reduce_fusion
  375.8 1.2 multiply_reduce_fusion
  377.0 2.4 fusion.6
  379.4 0.9 slice-done.1
  380.3 4.0 convolution_convert_fusion.gc_ref
  384.3 37.1 %attend_back.1 = (bf16[320,2048]{1,0:T(8,128)(2,1)S(1)}, f32[320,256]{1,0:T(8,128)S(1)}, f32[320,256]{1,0:T(8,128)S(1)}, bf16[320,2048]{1,0:T(8,128)(2,1)S(1)}, bf16[4,256,2048]{2,1,0:T(8,128)(2,1)}) custom-call(bf16[320,2048]{1,0:T(8,128)(2,1)} %get-tuple-element.83.q_ref, bf16[4,320,128]{2,1,0:T(8,128)(2,1)S(1)} %copy-done.5, ...), custom_call_target="tpu_custom_call" | custom-call | tf_op jit(solution)/shard_map/attend_back/pallas_call | solution.py:1051
  421.4 1.3 pad_maximum_fusion.gq_hbm
  422.7 84.9 %gradient_all.1 = (bf16[64,2048]{1,0:T(8,128)(2,1)}, bf16[256,2560]{1,0:T(8,128)(2,1)}, bf16[256,128]{1,0:T(8,128)(2,1)}, f32[320,2048]{1,0:T(8,128)}) custom-call(bf16[4,256,2048]{2,1,0:T(8,128)(2,1)} %get-tuple-element.91.sums_hbm, bf16[320,2048]{1,0:T(8,128)(2,1)} %get-tuple-element.92.xn_hbm, bf16[320,2560]{1,0:T(8,128)(2,1)} %pad_maximum_fusion.gq_hbm, ...), custom_call_target="tpu_custom_call" | custom-call | tf_op jit(solution)/shard_map/gradient_all/pallas_call | solution.py:1213
  507.6 0.0 reduce-scatter.2.cloned.1.call-done
  507.7 1.4 copy-done.1
  509.0 1.3 copy-done.2
  510.4 0.9 copy-done.7
  511.3 0.8 copy-done.8
  512.2 28.2 %finish_all.1 = (f32[64,2048]{1,0:T(8,128)S(1)}, f32[64,256]{1,0:T(8,128)S(1)}, f32[64,256]{1,0:T(8,128)S(1)}, f32[64,128]{1,0:T(8,128)S(1)}, f32[64,5632]{1,0:T...) custom-call(bf16[4,64,1408]{2,1,0:T(8,128)(2,1)S(1)} %copy-done.3, ...), custom_call_target="tpu_custom_call" | custom-call | tf_op jit(solution)/shard_map/finish_all/pallas_call | solution.py:1293
  540.3 0.7 slice_reduce_fusion
  541.0 1.1 copy.39
  542.1 0.1 copy-done.13
  542.2 1.5 copy.40
  543.7 0.8 copy.41
  544.5 0.6 copy.42
  545.2 0.6 copy.43
  545.8 0.8 copy.44
  546.6 1.1 copy.45
  547.7 1.1 copy.46
  548.8 1.1 copy.47
  (38 shorter events, 0.2 us)
Async XLA Ops:
  7.2 500.5 %reduce-scatter.2.cloned.1.call-start = ((), (), s32[]{:S(2)}) async-start(), calls=%async_computation.1 | async-start | bytes 7208960 | tf_op jit(solution)/shard_map/reduce_scatter | solution.py:1359
  10.1 152.6 %copy-start.10 = (bf16[320,2048]{1,0:T(8,128)(2,1)S(1)}, bf16[320,2048]{1,0:T(8,128)(2,1)}, u32[]{:S(2)}) copy-start(bf16[320,2048]{1,0:T(8,128)(2,1)} %param.18) | copy-start | bytes 3932164
  13.2 0.6 copy-start.15
  369.7 1.7 copy-start.9
  371.7 4.0 copy-start.14
  371.7 5.3 copy-start.11
  375.8 3.6 slice-start
  377.0 3.2 slice-start.1
  379.4 4.8 copy-start.12
  380.3 4.0 copy-start
  380.3 4.0 copy-start.4
  380.3 4.0 copy-start.5
  380.3 4.0 copy-start.6
  422.7 85.0 %copy-start.3 = (bf16[4,64,1408]{2,1,0:T(8,128)(2,1)S(1)}, bf16[4,64,1408]{2,1,0:T(8,128)(2,1)}, u32[]{:S(2)}) copy-start(bf16[4,64,1408]{2,1,0:T(8,128)(2,1)} %get-tuple-element.81.down) | copy-start | bytes 2162692
  507.7 1.4 copy-start.1
  509.0 1.3 copy-start.2
  510.4 0.9 copy-start.7
  511.3 0.8 copy-start.8
  540.3 1.9 copy-start.13
Sparse Core Ops, SparseCore 0:
  369.9 100.8 reduce-scatter.1

commit v9 on v8

--- a/solution.py
+++ b/solution.py
@@ -1334,12 +1334,13 @@
     tables = lane_tables(positions)
     grad_y = cotangent.astype(f32) * valid_rows
     grad_y_low = grad_y.astype(bf16)
-    gains = jnp.zeros((rows, 128), bf16).at[:, 0].set(norm_attn).at[:, 1].set(norm_mlp)
+    lanes = jnp.arange(128)[None]
+    gains = jnp.where(lanes == 0, norm_attn[:, None], jnp.where(lanes == 1, norm_mlp[:, None], jnp.zeros((), bf16)))
     w_qkv, w_out, gain_cols, ff_gate_up, ff_down = gather_all(
         nz, w_query, w_key, w_value, w_output, gains, w_gate, w_up, w_down
     )
-    gain_attn = gain_cols[:, 0].astype(f32)
-    gain_mlp = gain_cols[:, 1].astype(f32)
+    gain_rows = lax.dot_general(jnp.eye(8, 128, dtype=bf16), gain_cols, contract_last, preferred_element_type=f32)
+    gain_attn, gain_mlp = gain_rows[0], gain_rows[1]
 
     query_rotated, key_rotated, value_reduced, log_totals, context, scaled_attn, hidden, scaled_mlp, gy_all, ff_down = attend_all(
         nz, tokens, gain_attn[None], gain_mlp[None], tables, w_qkv, w_out, grad_y_low, ff_down

time: 564 us -> 559 us (level)
    unnamed x45 -> x43, local copies, waits for them, and re-layouts: 16.5 us -> 15.9 us
where the time goes in v9:
time: 559 us; the launch traced here: 554 us
  Pallas kernels  501 us (90%)
  local copies, waits for them, and re-layouts  17.2 us (3%)
  between operations  15.4 us (3%)
  other arithmetic  14.9 us (3%)
    pallas_call x1, Pallas kernels, gather_all(): pl.pallas_call(functools.partial(gather_kernel, nz), out_shape=(shape((wi...  146 us
    pallas_call x1, Pallas kernels, mlp_all(): pl.pallas_call(functools.partial(mlp_kernel, nz), out_shape=(blocks(width...  144 us
    pallas_call x1, Pallas kernels, gradient_all(): pl.pallas_call(functools.partial(gradient_kernel, nz), out_shape=(shape((...  84.9 us
    pallas_call x1, Pallas kernels, attend_all(): pl.pallas_call(functools.partial(attend_kernel, nz), grid=(KEY_VALUE_HEAD...  61.3 us
    pallas_call x1, Pallas kernels, attend_back_all(): pl.pallas_call(attend_back_kernel, grid=(KEY_VALUE_HEADS,), out_shape=(sh...  37 us
    pallas_call x1, Pallas kernels, finish_all(): pl.pallas_call(functools.partial(finish_kernel, nz), out_shape=(out(w1 -...  28.5 us
    unnamed x43, local copies, waits for them, and re-layouts  15.9 us
  transfers between devices with their start and end apart: 1, of which 0 were waited for; matrix products, arithmetic and copies ran while one was open for 2% of the time, Pallas kernels for 22%

profile of v9, /device:TPU:0, one launch (start us, length us, event | category | flops | bytes accessed | tf_op | source)
XLA Modules:
  0.0 553.5 jit_solution(2521233141507903009)
XLA Ops:
  7.2 0.0 reduce-scatter.2.cloned.1.call-start
  7.2 0.0 copy-start.10
  7.3 0.8 convert_element_type.38
  8.1 0.6 multiply_cosine_fusion
  8.7 0.2 maximum_bitcast_fusion
  8.9 1.4 select_select_fusion.gains
  10.3 145.6 %gather_all.1 = (bf16[2048,2560]{1,0:T(8,128)(2,1)}, bf16[2048,2048]{1,0:T(8,128)(2,1)}, bf16[2048,128]{1,0:T(8,128)(2,1)}, bf16[4,8,64,2816]{3,2,1,0:T(8,128)(2,1)}, bf16[4,64,1408]{2,1,0:T(8,128)(2,1)}) custom-call(bf16[64,2048]{1,0:T(8,128)(2,1)} %wq.1, bf16[64,256]{1,0:T(8,128)(2,1)} %wk.1, bf16[64,256]{1,0:T(8,128)(2,1)} %wv.1, bf16[64,2048]{1,0:T(8,128)(2,1)} %wo.1, ...), custom_call_target="tpu_custom_call" | custom-call | tf_op jit(solution)/shard_map/gather_all/pallas_call | solution.py:544
  155.9 1.3 fusion.3
  157.2 0.6 fusion.6
  158.5 0.1 negate_select_fusion
  158.6 0.2 maximum_bitcast_fusion.1
  158.8 0.0 copy-done.10
  158.8 1.3 fusion.gy
  160.1 0.8 pad_maximum_fusion.1.tab_ref
  160.9 61.3 %attend.1 = (bf16[320,2048]{1,0:T(8,128)(2,1)}, bf16[4,320,128]{2,1,0:T(8,128)(2,1)}, bf16[4,320,128]{2,1,0:T(8,128)(2,1)}, f32[4,320,128]{2,1,0:T(8,128)}, bf16...) custom-call(bf16[320,2048]{1,0:T(8,128)(2,1)} %tok_hbm.1, ...), custom_call_target="tpu_custom_call" | custom-call | flops 5368709120 | bytes 41943040 | tf_op jit(solution)/shard_map/attend/pallas_call | solution.py:932
  222.2 143.5 %mlp_all.1 = (bf16[4,320,2048]{2,1,0:T(8,128)(2,1)}, bf16[3,320,2048]{2,1,0:T(8,128)(2,1)}, bf16[320,2048]{1,0:T(8,128)(2,1)}, bf16[4,64,1408]{2,1,0:T(8,128)(2,1)}, bf16[4,4,64,2816]{3,2,1,0:T(8,128)(2,1)}) custom-call(bf16[320,2048]{1,0:T(8,128)(2,1)} %get-tuple-element.53.x, bf16[4,320,2048]{2,1,0:T(8,128)(2,1)} %get-tuple-element.54.gy, ...), custom_call_target="tpu_custom_call" | custom-call | flops 66437775360 | bytes 62914560 | tf_op jit(solution)/shard_map/mlp_all/pallas_call | solution.py:768
  365.8 0.0 reduce-scatter.2.cloned.1.call-update
  365.8 1.7 copy-done.9
  367.5 0.3 multiply_reduce_fusion.2
  367.8 0.0 copy-start.11
  367.8 4.1 convert_reduce_fusion
  372.0 0.0 slice-start
  372.0 1.2 multiply_reduce_fusion
  373.2 2.4 fusion.5
  375.6 0.8 slice-done.1
  376.4 4.0 convolution_convert_fusion.gc_ref
  380.4 0.0 copy-done.12
  380.4 0.0 copy-done.4
  380.4 37.0 %attend_back.1 = (bf16[320,2048]{1,0:T(8,128)(2,1)S(1)}, f32[320,256]{1,0:T(8,128)S(1)}, f32[320,256]{1,0:T(8,128)S(1)}, bf16[320,2048]{1,0:T(8,128)(2,1)S(1)}, bf16[4,256,2048]{2,1,0:T(8,128)(2,1)}) custom-call(bf16[320,2048]{1,0:T(8,128)(2,1)} %get-tuple-element.59.q_ref, bf16[4,320,128]{2,1,0:T(8,128)(2,1)S(1)} %copy-done.5, ...), custom_call_target="tpu_custom_call" | custom-call | tf_op jit(solution)/shard_map/attend_back/pallas_call | solution.py:1051
  417.5 1.3 pad_maximum_fusion.gq_hbm
  418.8 84.9 %gradient_all.1 = (bf16[64,2048]{1,0:T(8,128)(2,1)}, bf16[256,2560]{1,0:T(8,128)(2,1)}, bf16[256,128]{1,0:T(8,128)(2,1)}, f32[320,2048]{1,0:T(8,128)}) custom-call(bf16[4,256,2048]{2,1,0:T(8,128)(2,1)} %get-tuple-element.67.sums_hbm, bf16[320,2048]{1,0:T(8,128)(2,1)} %get-tuple-element.68.xn_hbm, bf16[320,2560]{1,0:T(8,128)(2,1)} %pad_maximum_fusion.gq_hbm, ...), custom_call_target="tpu_custom_call" | custom-call | tf_op jit(solution)/shard_map/gradient_all/pallas_call | solution.py:1213
  503.7 0.0 reduce-scatter.2.cloned.1.call-done
  503.8 1.4 copy-done.1
  505.1 1.3 copy-done.2
  506.4 0.9 copy-done.7
  507.4 0.8 copy-done.8
  508.2 28.5 %finish_all.1 = (f32[64,2048]{1,0:T(8,128)S(1)}, f32[64,256]{1,0:T(8,128)S(1)}, f32[64,256]{1,0:T(8,128)S(1)}, f32[64,128]{1,0:T(8,128)S(1)}, f32[64,5632]{1,0:T...) custom-call(bf16[4,64,1408]{2,1,0:T(8,128)(2,1)S(1)} %copy-done.3, ...), custom_call_target="tpu_custom_call" | custom-call | tf_op jit(solution)/shard_map/finish_all/pallas_call | solution.py:1293
  536.7 0.7 slice_reduce_fusion
  537.4 1.1 copy.34
  538.5 0.1 copy-done.13
  538.6 1.5 copy.35
  540.1 0.8 copy.36
  540.9 0.6 copy.37
  541.5 0.6 copy.38
  542.2 0.8 copy.39
  543.0 1.1 copy.40
  544.1 1.1 copy.41
  545.1 1.1 copy.42
  (31 shorter events, 0.1 us)
Async XLA Ops:
  7.2 496.6 %reduce-scatter.2.cloned.1.call-start = ((), (), s32[]{:S(2)}) async-start(), calls=%async_computation.1 | async-start | bytes 7208960 | tf_op jit(solution)/shard_map/reduce_scatter | solution.py:1360
  7.2 151.5 %copy-start.10 = (bf16[320,2048]{1,0:T(8,128)(2,1)S(1)}, bf16[320,2048]{1,0:T(8,128)(2,1)}, u32[]{:S(2)}) copy-start(bf16[320,2048]{1,0:T(8,128)(2,1)} %param.14) | copy-start | bytes 3932164
  365.8 1.7 copy-start.9
  367.8 4.2 copy-start.14
  367.8 5.4 copy-start.11
  372.0 3.6 slice-start
  373.2 3.2 slice-start.1
  375.6 4.8 copy-start.12
  376.4 4.0 copy-start
  376.4 4.0 copy-start.4
  376.4 4.0 copy-start.5
  376.4 4.0 copy-start.6
  418.8 85.0 %copy-start.3 = (bf16[4,64,1408]{2,1,0:T(8,128)(2,1)S(1)}, bf16[4,64,1408]{2,1,0:T(8,128)(2,1)}, u32[]{:S(2)}) copy-start(bf16[4,64,1408]{2,1,0:T(8,128)(2,1)} %get-tuple-element.57.down) | copy-start | bytes 2162692
  503.8 1.4 copy-start.1
  505.1 1.3 copy-start.2
  506.4 0.9 copy-start.7
  507.4 0.8 copy-start.8
  536.7 1.9 copy-start.13
Sparse Core Ops, SparseCore 0:
  365.9 100.6 reduce-scatter.1

commit v10 on v9

--- a/solution.py
+++ b/solution.py
@@ -658,17 +658,18 @@
             def _():
                 for i in (2 * t, 2 * t + 1):
                     (to_owner(gx, gx_parts, i, rs_s, rs_r) if t else kept(gx, gx_parts.at[0], i, i)).start()
+                if t > 1:
+                    for i in (2 * t - 2, 2 * t - 1): to_owner(mo, mlp_parts, i, mo_s, mo_r).start()
         def down(i, carry):
             at = pl.ds(pl.multiple_of(i * tile, 128), tile)
             put(mo, at, lax.dot_general(both(mix), some_rows(gd, i), contract_last, preferred_element_type=f32))
             return carry
         lax.fori_loop(0, CHIPS * CORES, down, 0)
-        for t in range(CHIPS):
+        for t in (0, 3):
             @pl.when(r == t)
             def _():
                 for i in (2 * t, 2 * t + 1):
-                    (kept(mo, mlp_parts.at[0], i, 2 + i) if t == 0 else kept(mo, mlp_cross, i, i - 2) if t == 3
-                     else to_owner(mo, mlp_parts, i, mo_s, mo_r)).start()
+                    (kept(mo, mlp_parts.at[0], i, 2 + i) if t == 0 else kept(mo, mlp_cross, i, i - 2)).start()
         return carry
     lax.fori_loop(0, CHIPS, block, 0)
 

time: 559 us -> 559 us (level)
  no operation moved by 1% of the time
where the time goes in v10:
time: 559 us; the launch traced here: 553 us
  Pallas kernels  501 us (90%)
  local copies, waits for them, and re-layouts  17.2 us (3%)
  between operations  15.4 us (3%)
  other arithmetic  14.8 us (3%)
    pallas_call x1, Pallas kernels, gather_all(): pl.pallas_call(functools.partial(gather_kernel, nz), out_shape=(shape((wi...  146 us
    pallas_call x1, Pallas kernels, mlp_all(): pl.pallas_call(functools.partial(mlp_kernel, nz), out_shape=(blocks(width...  143 us
    pallas_call x1, Pallas kernels, gradient_all(): pl.pallas_call(functools.partial(gradient_kernel, nz), out_shape=(shape((...  84.9 us
    pallas_call x1, Pallas kernels, attend_all(): pl.pallas_call(functools.partial(attend_kernel, nz), grid=(KEY_VALUE_HEAD...  61.3 us
    pallas_call x1, Pallas kernels, attend_back_all(): pl.pallas_call(attend_back_kernel, grid=(KEY_VALUE_HEADS,), out_shape=(sh...  37 us
    pallas_call x1, Pallas kernels, finish_all(): pl.pallas_call(functools.partial(finish_kernel, nz), out_shape=(out(w1 -...  28.4 us
    unnamed x43, local copies, waits for them, and re-layouts  15.9 us
  transfers between devices with their start and end apart: 1, of which 0 were waited for; matrix products, arithmetic and copies ran while one was open for 2% of the time, Pallas kernels for 22%

profile of v10, /device:TPU:0, one launch (start us, length us, event | category | flops | bytes accessed | tf_op | source)
XLA Modules:
  0.0 553.5 jit_solution(7212143777616896990)
XLA Ops:
  7.2 0.0 reduce-scatter.2.cloned.1.call-start
  7.2 0.0 copy-start.10
  7.3 0.8 convert_element_type.38
  8.1 0.6 multiply_cosine_fusion
  8.7 0.2 maximum_bitcast_fusion
  8.9 1.4 select_select_fusion.gains
  10.3 145.6 %gather_all.1 = (bf16[2048,2560]{1,0:T(8,128)(2,1)}, bf16[2048,2048]{1,0:T(8,128)(2,1)}, bf16[2048,128]{1,0:T(8,128)(2,1)}, bf16[4,8,64,2816]{3,2,1,0:T(8,128)(2,1)}, bf16[4,64,1408]{2,1,0:T(8,128)(2,1)}) custom-call(bf16[64,2048]{1,0:T(8,128)(2,1)} %wq.1, bf16[64,256]{1,0:T(8,128)(2,1)} %wk.1, bf16[64,256]{1,0:T(8,128)(2,1)} %wv.1, bf16[64,2048]{1,0:T(8,128)(2,1)} %wo.1, ...), custom_call_target="tpu_custom_call" | custom-call | tf_op jit(solution)/shard_map/gather_all/pallas_call | solution.py:544
  155.9 1.3 fusion.3
  157.2 0.6 fusion.6
  158.5 0.1 negate_select_fusion
  158.6 0.2 maximum_bitcast_fusion.1
  158.8 0.0 copy-done.10
  158.8 1.3 fusion.gy
  160.1 0.8 pad_maximum_fusion.1.tab_ref
  160.9 61.3 %attend.1 = (bf16[320,2048]{1,0:T(8,128)(2,1)}, bf16[4,320,128]{2,1,0:T(8,128)(2,1)}, bf16[4,320,128]{2,1,0:T(8,128)(2,1)}, f32[4,320,128]{2,1,0:T(8,128)}, bf16...) custom-call(bf16[320,2048]{1,0:T(8,128)(2,1)} %tok_hbm.1, ...), custom_call_target="tpu_custom_call" | custom-call | flops 5368709120 | bytes 41943040 | tf_op jit(solution)/shard_map/attend/pallas_call | solution.py:933
  222.2 143.5 %mlp_all.1 = (bf16[4,320,2048]{2,1,0:T(8,128)(2,1)}, bf16[3,320,2048]{2,1,0:T(8,128)(2,1)}, bf16[320,2048]{1,0:T(8,128)(2,1)}, bf16[4,64,1408]{2,1,0:T(8,128)(2,1)}, bf16[4,4,64,2816]{3,2,1,0:T(8,128)(2,1)}) custom-call(bf16[320,2048]{1,0:T(8,128)(2,1)} %get-tuple-element.53.x, bf16[4,320,2048]{2,1,0:T(8,128)(2,1)} %get-tuple-element.54.gy, ...), custom_call_target="tpu_custom_call" | custom-call | flops 66437775360 | bytes 62914560 | tf_op jit(solution)/shard_map/mlp_all/pallas_call | solution.py:769
  365.7 0.0 reduce-scatter.2.cloned.1.call-update
  365.8 1.7 copy-done.9
  367.5 0.3 multiply_reduce_fusion.2
  367.8 0.0 copy-start.11
  367.8 4.1 convert_reduce_fusion
  371.9 0.0 copy-done.14
  371.9 0.0 slice-start
  371.9 1.2 multiply_reduce_fusion
  373.2 2.4 fusion.5
  375.6 0.8 slice-done.1
  376.4 4.0 convolution_convert_fusion.gc_ref
  380.4 0.0 copy-done.4
  380.4 37.0 %attend_back.1 = (bf16[320,2048]{1,0:T(8,128)(2,1)S(1)}, f32[320,256]{1,0:T(8,128)S(1)}, f32[320,256]{1,0:T(8,128)S(1)}, bf16[320,2048]{1,0:T(8,128)(2,1)S(1)}, bf16[4,256,2048]{2,1,0:T(8,128)(2,1)}) custom-call(bf16[320,2048]{1,0:T(8,128)(2,1)} %get-tuple-element.59.q_ref, bf16[4,320,128]{2,1,0:T(8,128)(2,1)S(1)} %copy-done.5, ...), custom_call_target="tpu_custom_call" | custom-call | tf_op jit(solution)/shard_map/attend_back/pallas_call | solution.py:1052
  417.4 1.3 pad_maximum_fusion.gq_hbm
  418.7 84.9 %gradient_all.1 = (bf16[64,2048]{1,0:T(8,128)(2,1)}, bf16[256,2560]{1,0:T(8,128)(2,1)}, bf16[256,128]{1,0:T(8,128)(2,1)}, f32[320,2048]{1,0:T(8,128)}) custom-call(bf16[4,256,2048]{2,1,0:T(8,128)(2,1)} %get-tuple-element.67.sums_hbm, bf16[320,2048]{1,0:T(8,128)(2,1)} %get-tuple-element.68.xn_hbm, bf16[320,2560]{1,0:T(8,128)(2,1)} %pad_maximum_fusion.gq_hbm, ...), custom_call_target="tpu_custom_call" | custom-call | tf_op jit(solution)/shard_map/gradient_all/pallas_call | solution.py:1214
  503.7 0.0 reduce-scatter.2.cloned.1.call-done
  503.7 1.4 copy-done.1
  505.1 1.3 copy-done.2
  506.4 0.9 copy-done.7
  507.3 0.8 copy-done.8
  508.2 28.4 %finish_all.1 = (f32[64,2048]{1,0:T(8,128)S(1)}, f32[64,256]{1,0:T(8,128)S(1)}, f32[64,256]{1,0:T(8,128)S(1)}, f32[64,128]{1,0:T(8,128)S(1)}, f32[64,5632]{1,0:T...) custom-call(bf16[4,64,1408]{2,1,0:T(8,128)(2,1)S(1)} %copy-done.3, ...), custom_call_target="tpu_custom_call" | custom-call | tf_op jit(solution)/shard_map/finish_all/pallas_call | solution.py:1294
  536.7 0.7 slice_reduce_fusion
  537.4 1.1 copy.34
  538.4 0.1 copy-done.13
  538.6 1.5 copy.35
  540.0 0.8 copy.36
  540.8 0.6 copy.37
  541.5 0.6 copy.38
  542.1 0.8 copy.39
  542.9 1.1 copy.40
  544.0 1.1 copy.41
  545.1 1.1 copy.42
  (31 shorter events, 0.1 us)
Async XLA Ops:
  7.2 496.5 %reduce-scatter.2.cloned.1.call-start = ((), (), s32[]{:S(2)}) async-start(), calls=%async_computation.1 | async-start | bytes 7208960 | tf_op jit(solution)/shard_map/reduce_scatter | solution.py:1361
  7.2 151.5 %copy-start.10 = (bf16[320,2048]{1,0:T(8,128)(2,1)S(1)}, bf16[320,2048]{1,0:T(8,128)(2,1)}, u32[]{:S(2)}) copy-start(bf16[320,2048]{1,0:T(8,128)(2,1)} %param.14) | copy-start | bytes 3932164
  365.7 1.7 copy-start.9
  367.8 4.2 copy-start.14
  367.8 5.4 copy-start.11
  371.9 3.6 slice-start
  373.2 3.2 slice-start.1
  375.6 4.8 copy-start.12
  376.4 4.0 copy-start
  376.4 4.0 copy-start.4
  376.4 4.0 copy-start.5
  376.4 4.0 copy-start.6
  418.7 85.0 %copy-start.3 = (bf16[4,64,1408]{2,1,0:T(8,128)(2,1)S(1)}, bf16[4,64,1408]{2,1,0:T(8,128)(2,1)}, u32[]{:S(2)}) copy-start(bf16[4,64,1408]{2,1,0:T(8,128)(2,1)} %get-tuple-element.57.down) | copy-start | bytes 2162692
  503.7 1.4 copy-start.1
  505.1 1.3 copy-start.2
  506.4 0.9 copy-start.7
  507.3 0.8 copy-start.8
  536.6 1.9 copy-start.13
Sparse Core Ops, SparseCore 0:
  365.9 100.6 reduce-scatter.1
